TPU v7x, 256 devices: a whole 4x4x8 slice. The times are simulated.
256 devices in a mesh: gx: 16 (over z, core), gy: 16 (over x, y).
Axes of the slice: x: 4, y: 4, z: 8, core: 2. Of those that a mesh axis runs over, the one named last changes fastest.
Arguments:
- pressure: float32 [4096, 4096], P('gx', 'gy'), may hold values from -6 to 6
- source: float32 [4096, 4096], P('gx', 'gy'), may hold values from -6 to 6
- conductivity: float32 [4096, 4096], P('gx', 'gy'), may hold values from 0.2 to 5
- storage: float32 [4096, 4096], P('gx', 'gy'), may hold values from 0.2 to 1
Outputs:
- pressure_next: float32 [4096, 4096], P('gx', 'gy')
All inputs are finite; a program needn't handle non-finite values.
Results may differ from a plain program's by a relative error of at most 0.0001.
Values sent between devices are 32-bit elements; how exact they have to be, the bound alone decides.
No kernel may reach another device: no remote copies, remote signals or barrier semaphores. Data moves between devices by JAX's collectives and lax.ppermute only.
A program may use at most 128 MiB of HBM per device.

v0:
```python
import jax
import jax.numpy as jnp
from jax import lax
from jax.sharding import PartitionSpec as P

LEVELS_SPLIT = 4
LEVELS_MERGED = 2
COARSE_SWEEPS = 8


OMEGA = 0.8


def shifted(block, axis, distance):
    devices = range(lax.axis_size(axis))
    route = [(i - distance, i) for i in devices if i - distance in devices]
    return lax.ppermute(block, axis, route)


def with_halo(x, sides, width):
    for axis, dim in sides:
        size, length = (lax.axis_size(axis), x.shape[dim])
        up = [(i, (i + 1) % size) for i in range(size - 1)]
        down = [(j, i) for i, j in up]
        last = lax.slice_in_dim(x, length - width, length, axis=dim)
        first = lax.slice_in_dim(x, 0, width, axis=dim)
        before = lax.ppermute(last, axis, up)
        after = lax.ppermute(first, axis, down)
        x = jnp.concatenate([before, x, after], axis=dim)
    return x


def from_partner(block, axis, bit):
    count = lax.axis_size(axis)
    route = []
    for low in range(count):
        high = low | 1 << bit
        if high != low and high < count:
            route += [(low, high), (high, low)]
    return lax.ppermute(block, axis, route)


def coarsen(grid):
    height, breadth = grid.shape
    return grid.reshape(height // 2, 2, breadth // 2, 2).sum(axis=(1, 3))


def prolong(grid):
    return jnp.repeat(jnp.repeat(grid, 2, axis=0), 2, axis=1)


def rim_shift(edge_piece, offset):
    return shifted(edge_piece, ("gx", "gy"), offset)


def padded_block(field, span_x, span_y):
    size_y = lax.axis_size("gy")
    if span_x == 1 and span_y == 1:
        return with_halo(field, (("gx", 0), ("gy", 1)), 1)
    lower_row = rim_shift(field[-1:, :], span_x * size_y)
    upper_row = rim_shift(field[:1, :], -span_x * size_y)
    column_place = lax.axis_index("gy")
    lower_col = jnp.where(column_place >= span_y, rim_shift(field[:, -1:], span_y), 0.0)
    upper_col = jnp.where(column_place + span_y < size_y, rim_shift(field[:, :1], -span_y), 0.0)
    corner = jnp.zeros((1, 1), field.dtype)
    middle = jnp.concatenate([lower_col, field, upper_col], axis=1)
    top_row = jnp.concatenate([corner, lower_row, corner], axis=1)
    bottom_row = jnp.concatenate([corner, upper_row, corner], axis=1)
    return jnp.concatenate([top_row, middle, bottom_row], axis=0)


def face_terms(conduct, stored, span_x, span_y):
    padded = padded_block(conduct, span_x, span_y)
    west_face = 0.5 * (conduct + padded[:-2, 1:-1])
    east_face = 0.5 * (conduct + padded[2:, 1:-1])
    south_face = 0.5 * (conduct + padded[1:-1, :-2])
    north_face = 0.5 * (conduct + padded[1:-1, 2:])
    diagonal = stored + west_face + east_face + south_face + north_face
    return (diagonal, west_face, east_face, south_face, north_face, span_x, span_y)


def pre_smooth(section, right_side, start_field):
    if start_field is None:
        field = first_sweep(right_side, section)
    else:
        field = jacobi_sweep(start_field, right_side, section)
    field = jacobi_sweep(field, right_side, section)
    residual = right_side - operate(field, section)
    return (field, residual, right_side)


def post_smooth(section, right_side, field):
    field = jacobi_sweep(field, right_side, section)
    return jacobi_sweep(field, right_side, section)


def operate(field, section):
    diagonal, west_face, east_face, south_face, north_face = section[:5]
    span_x, span_y = (section[5], section[6])
    padded = padded_block(field, span_x, span_y)
    return (
        diagonal * field
        - west_face * padded[:-2, 1:-1]
        - east_face * padded[2:, 1:-1]
        - south_face * padded[1:-1, :-2]
        - north_face * padded[1:-1, 2:]
    )


def jacobi_sweep(field, right_side, section):
    return field + OMEGA * (right_side - operate(field, section)) / section[0]


def first_sweep(right_side, section):
    return OMEGA * right_side / section[0]


def join_halves(stacked, own_bit, flip_bit, along):
    partner = from_partner(stacked, ("gx", "gy"), flip_bit)
    lower_half = jnp.where(own_bit == 0, stacked, partner)
    upper_half = jnp.where(own_bit == 0, partner, stacked)
    return jnp.concatenate([lower_half, upper_half], axis=along)


def merge_both(stacked, span_now):
    size_y = lax.axis_size("gy")
    bit_y = lax.axis_index("gy") // span_now % 2
    bit_x = lax.axis_index("gx") // span_now % 2
    stacked = join_halves(stacked, bit_y, span_now.bit_length() - 1, 2)
    stacked = join_halves(stacked, bit_x, (span_now * size_y).bit_length() - 1, 1)
    return stacked


def own_half(correction, span_now):
    half_x = correction.shape[0] // 2
    half_y = correction.shape[1] // 2
    bit_x = lax.axis_index("gx") // span_now % 2
    bit_y = lax.axis_index("gy") // span_now % 2
    part = lax.dynamic_slice_in_dim(correction, bit_x * half_x, half_x, 0)
    return lax.dynamic_slice_in_dim(part, bit_y * half_y, half_y, 1)


def cycle(sections, depth, right_side, start_field):
    section = sections[depth]
    if depth == len(sections) - 1:
        field = first_sweep(right_side, section)
        for _ in range(COARSE_SWEEPS - 1):
            field = jacobi_sweep(field, right_side, section)
        return field
    field, residual, side_wide = pre_smooth(section, right_side, start_field)
    coarse_side = coarsen(residual)
    if depth + 1 >= LEVELS_SPLIT:
        coarse_side = merge_both(coarse_side[None], section[5])[0]
    correction = cycle(sections, depth + 1, coarse_side, None)
    if depth + 1 >= LEVELS_SPLIT:
        correction = own_half(correction, section[5])
    field = field + prolong(correction)
    return post_smooth(section, right_side, field)


def per_device(pressure, source, conductivity, storage):
    conduct, stored = (conductivity, storage)
    sections = []
    for depth in range(LEVELS_SPLIT):
        if depth > 0:
            conduct = 0.5 * coarsen(conduct)
            stored = coarsen(stored)
        sections.append(face_terms(conduct, stored, 1, 1))
    conduct = 0.5 * coarsen(conduct)
    stored = coarsen(stored)
    span_now = 1
    for depth in range(LEVELS_MERGED):
        if depth > 0:
            conduct = 0.5 * coarsen(conduct)
            stored = coarsen(stored)
        merged = merge_both(jnp.stack([conduct, stored]), span_now)
        conduct, stored = (merged[0], merged[1])
        span_now = 2 * span_now
        sections.append(face_terms(conduct, stored, span_now, span_now))
    return cycle(sections, 0, source, pressure)


def solution(mesh):
    placed = (P("gx", "gy"), P("gx", "gy"), P("gx", "gy"), P("gx", "gy"))
    return jax.shard_map(
        per_device, mesh=mesh, in_specs=placed, out_specs=P("gx", "gy"), check_vma=False
    )
```

profile of v0, /device:TPU:130, one launch (start us, length us, event | category | flops | bytes accessed | tf_op | source)
XLA Modules:
  0.0 707.1 jit_solution(9270971714888408560)
XLA Ops:
  15.9 18.9 %reshape.96 = f32[128,2,128,2]{3,2,1,0:T(8,128)} reshape(f32[256,256]{1,0:T(8,128)} %param.6) | data formatting | bytes 524288 | tf_op jit(solution)/shard_map/reshape | solution.py:45
  34.7 8.0 %reduce_sum.137 = f32[128,128]{1,0:T(8,128)S(1)} reduce(f32[128,2,128,2]{3,2,1,0:T(8,128)} %reshape.96, f32[]{:T(128)} %constant.129.clone.1), dimensions={1,3}, to_apply=%region_2.0 | reduce | flops 49152 | bytes 327684 | tf_op jit(solution)/shard_map/reduce_sum | solution.py:45
  45.6 18.1 %reshape.95 = f32[128,2,128,2]{3,2,1,0:T(8,128)} reshape(f32[256,256]{1,0:T(8,128)S(1)} %copy-done.1) | data formatting | bytes 524288 | tf_op jit(solution)/shard_map/reshape | solution.py:45
  63.7 5.5 mul.674
  73.7 8.0 %reduce_sum.136 = f32[128,128]{1,0:T(8,128)S(1)} reduce(f32[128,2,128,2]{3,2,1,0:T(8,128)} %reshape.95, f32[]{:T(128)} %constant.129.clone.1), dimensions={1,3}, to_apply=%region_1.0 | reduce | flops 49152 | bytes 327684 | tf_op jit(solution)/shard_map/reduce_sum | solution.py:45
  81.7 5.6 reshape.98
  94.0 4.9 collective-permute-start.41
  99.0 4.9 collective-permute-start.7
  108.4 5.4 collective-permute-start.3
  125.9 4.9 collective-permute-start.29
  150.1 5.0 collective-permute-done.12
  169.8 18.1 %reshape.94 = f32[128,2,128,2]{3,2,1,0:T(8,128)} reshape(f32[256,256]{1,0:T(8,128)S(1)} %copy.203) | data formatting | bytes 524288 | tf_op jit(solution)/shard_map/reshape | solution.py:45
  187.9 8.0 %reduce_sum.135 = f32[128,128]{1,0:T(8,128)S(1)} reduce(f32[128,2,128,2]{3,2,1,0:T(8,128)} %reshape.94, f32[]{:T(128)} %constant.129.clone.1), dimensions={1,3}, to_apply=%region_0.0 | reduce | flops 49152 | bytes 327684 | tf_op jit(solution)/shard_map/reduce_sum | solution.py:45
  210.5 6.4 collective-permute-done.22
  236.3 5.6 reshape.97
  300.5 5.6 collective-permute-done.46
  386.8 5.4 collective-permute-start.75
  400.3 6.3 collective-permute-start.79
  408.5 5.6 collective-permute-done.76
  423.0 4.8 collective-permute-start.80
  439.5 4.8 collective-permute-start.84
  456.0 4.8 collective-permute-start.88
  472.4 4.8 collective-permute-start.92
  488.9 4.8 collective-permute-start.96
  496.7 5.4 collective-permute-start.102
  505.9 4.8 collective-permute-start.100
  513.9 6.1 collective-permute-start.106
  530.7 6.3 collective-permute-start.110
  556.1 5.9 collective-permute-start.115
  564.0 5.8 collective-permute-done.114
  671.4 5.0 collective-permute-done.136
  691.0 5.0 collective-permute-done.140
  (512 shorter events, 485.5 us)
Async XLA Ops:
  1.5 90.5 %collective-permute-start.5 = (f32[1,256]{0,1:T(8,128)}, f32[1,256]{0,1:T(8,128)S(1)}, u32[]{:S(2)}, u32[]{:S(2)}) collective-permute-start(f32[1,256]{0,1:T(8,128)} %copy.196), channel_id=1, source_target_pairs={{16,0},{32,16},{48,32},{64,48},{80,64},{96,80},{112,96},{128,112},... | collective-permute-start | bytes 3080 | tf_op jit(solution)/shard_map/ppermute | solution.py:28
  4.2 89.8 %collective-permute-start.4 = (f32[1,256]{0,1:T(8,128)}, f32[1,256]{0,1:T(8,128)S(1)}, u32[]{:S(2)}, u32[]{:S(2)}) collective-permute-start(f32[1,256]{0,1:T(8,128)} %copy.194), channel_id=1, source_target_pairs={{0,16},{16,32},{32,48},{48,64},{64,80},{80,96},{96,112},{112,128},... | collective-permute-start | bytes 3080 | tf_op jit(solution)/shard_map/ppermute | solution.py:27
  8.2 90.8 %collective-permute-start = (f32[1,256]{0,1:T(8,128)}, f32[1,256]{0,1:T(8,128)S(1)}, u32[]{:S(2)}, u32[]{:S(2)}) collective-permute-start(f32[1,256]{0,1:T(8,128)} %copy.183), channel_id=1, source_target_pairs={{0,16},{16,32},{32,48},{48,64},{64,80},{80,96},{96,112},{112,128},... | collective-permute-start | bytes 3080 | tf_op jit(solution)/shard_map/ppermute | solution.py:27
  12.0 91.9 %collective-permute-start.1 = (f32[1,256]{0,1:T(8,128)}, f32[1,256]{0,1:T(8,128)S(1)}, u32[]{:S(2)}, u32[]{:S(2)}) collective-permute-start(f32[1,256]{0,1:T(8,128)} %copy.187), channel_id=1, source_target_pairs={{16,0},{32,16},{48,32},{64,48},{80,64},{96,80},{112,96},{128,112},... | collective-permute-start | bytes 3080 | tf_op jit(solution)/shard_map/ppermute | solution.py:28
  42.8 102.9 %collective-permute-start.16 = (f32[1,128]{1,0:T(1,128)S(1)}, f32[1,128]{1,0:T(1,128)S(1)}, u32[]{:S(2)}, u32[]{:S(2)}) collective-permute-start(f32[1,128]{1,0:T(1,128)S(1)} %get-tuple-element.73), channel_id=1, source_target_pairs={{0,16},{16,32},{32,48},{48,64},{64,80},{80,96},{96,112},{112,128},... | collective-permute-start | bytes 1544 | tf_op jit(solution)/shard_map/ppermute | solution.py:27
  92.1 13.8 %collective-permute-start.40 = (f32[1,32]{1,0:T(1,128)S(1)}, f32[1,32]{1,0:T(1,128)S(1)}, u32[]{:S(2)}, u32[]{:S(2)}) collective-permute-start(f32[1,32]{1,0:T(1,128)S(1)} %get-tuple-element.181), channel_id=1, source_target_pairs={{0,16},{16,32},{32,48},{48,64},{64,80},{80,96},{96,112},{112,128},... | collective-permute-start | bytes 392 | tf_op jit(solution)/shard_map/ppermute | solution.py:27
  94.0 14.4 %collective-permute-start.41 = (f32[1,32]{1,0:T(1,128)S(1)}, f32[1,32]{1,0:T(1,128)S(1)}, u32[]{:S(2)}, u32[]{:S(2)}) collective-permute-start(f32[1,32]{1,0:T(1,128)S(1)} %get-tuple-element.180), channel_id=1, source_target_pairs={{16,0},{32,16},{48,32},{64,48},{80,64},{96,80},{112,96},{128,112},... | collective-permute-start | bytes 392 | tf_op jit(solution)/shard_map/ppermute | solution.py:28
  99.0 14.9 %collective-permute-start.7 = (f32[258,1]{0,1:T(1,128)S(1)}, f32[258,1]{0,1:T(1,128)S(1)}, u32[]{:S(2)}, u32[]{:S(2)}) collective-permute-start(f32[258,1]{0,1:T(1,128)S(1)} %get-tuple-element.41), channel_id=1, source_target_pairs={{1,0},{2,1},{3,2},{4,3},{5,4},{6,5},{7,6},{8,7},{9,8},{10,9},{11,1... | collective-permute-start | bytes 3104 | tf_op jit(solution)/shard_map/ppermute | solution.py:28
  113.9 33.7 %collective-permute-start.17 = (f32[1,128]{1,0:T(1,128)S(1)}, f32[1,128]{1,0:T(1,128)S(1)}, u32[]{:S(2)}, u32[]{:S(2)}) collective-permute-start(f32[1,128]{1,0:T(1,128)S(1)} %get-tuple-element.72), channel_id=1, source_target_pairs={{16,0},{32,16},{48,32},{64,48},{80,64},{96,80},{112,96},{128,112},... | collective-permute-start | bytes 1544 | tf_op jit(solution)/shard_map/ppermute | solution.py:28
  115.8 15.2 %collective-permute-start.28 = (f32[1,64]{1,0:T(1,128)S(1)}, f32[1,64]{1,0:T(1,128)S(1)}, u32[]{:S(2)}, u32[]{:S(2)}) collective-permute-start(f32[1,64]{1,0:T(1,128)S(1)} %get-tuple-element.105), channel_id=1, source_target_pairs={{0,16},{16,32},{32,48},{48,64},{64,80},{80,96},{96,112},{112,128},... | collective-permute-start | bytes 776 | tf_op jit(solution)/shard_map/ppermute | solution.py:27
  130.8 77.8 %collective-permute-start.54 = (f32[2,16,16]{2,1,0:T(8,128)S(1)}, f32[2,16,16]{2,1,0:T(8,128)S(1)}, u32[]{:S(2)}, u32[]{:S(2)}) collective-permute-start(f32[2,16,16]{2,1,0:T(8,128)S(1)} %pad_maximum_fusion.313), channel_id=1, source_target_pairs={{0,1},{1,0},{2,3},{3,2},{4,5},{5,4},{6,7},{7,6},{8,9},{9,8},{10,11... | collective-permute-start | bytes 6152 | tf_op jit(solution)/shard_map/ppermute | solution.py:40
  136.9 147.4 %collective-permute-start.42 = (f32[34,1]{1,0:T(8,128)}, f32[34,1]{1,0:T(8,128)}, u32[]{:S(2)}, u32[]{:S(2)}) collective-permute-start(f32[34,1]{1,0:T(8,128)} %get-tuple-element.115), channel_id=1, source_target_pairs={{0,1},{1,2},{2,3},{3,4},{4,5},{5,6},{6,7},{7,8},{8,9},{9,10},{10,1... | collective-permute-start | bytes 416 | tf_op jit(solution)/shard_map/ppermute | solution.py:27
  142.5 141.8 %collective-permute-start.43 = (f32[34,1]{1,0:T(8,128)}, f32[34,1]{1,0:T(8,128)}, u32[]{:S(2)}, u32[]{:S(2)}) collective-permute-start(f32[34,1]{1,0:T(8,128)} %get-tuple-element.114), channel_id=1, source_target_pairs={{1,0},{2,1},{3,2},{4,3},{5,4},{6,5},{7,6},{8,7},{9,8},{10,9},{11,1... | collective-permute-start | bytes 416 | tf_op jit(solution)/shard_map/ppermute | solution.py:28
  161.2 34.8 %collective-permute-start.18 = (f32[130,1]{1,0:T(8,128)S(1)}, f32[130,1]{1,0:T(8,128)S(1)}, u32[]{:S(2)}, u32[]{:S(2)}) collective-permute-start(f32[130,1]{1,0:T(8,128)S(1)} %get-tuple-element.63), channel_id=1, source_target_pairs={{0,1},{1,2},{2,3},{3,4},{4,5},{5,6},{6,7},{7,8},{8,9},{9,10},{10,1... | collective-permute-start | bytes 1568 | tf_op jit(solution)/shard_map/ppermute | solution.py:27
  166.7 29.2 %collective-permute-start.19 = (f32[130,1]{1,0:T(8,128)S(1)}, f32[130,1]{1,0:T(8,128)S(1)}, u32[]{:S(2)}, u32[]{:S(2)}) collective-permute-start(f32[130,1]{1,0:T(8,128)S(1)} %get-tuple-element.62), channel_id=1, source_target_pairs={{1,0},{2,1},{3,2},{4,3},{5,4},{6,5},{7,6},{8,7},{9,8},{10,9},{11,1... | collective-permute-start | bytes 1568 | tf_op jit(solution)/shard_map/ppermute | solution.py:28
  200.5 44.2 %collective-permute-start.30 = (f32[66,1]{1,0:T(8,128)S(1)}, f32[66,1]{1,0:T(8,128)S(1)}, u32[]{:S(2)}, u32[]{:S(2)}) collective-permute-start(f32[66,1]{1,0:T(8,128)S(1)} %get-tuple-element.83), channel_id=1, source_target_pairs={{0,1},{1,2},{2,3},{3,4},{4,5},{5,6},{6,7},{7,8},{8,9},{9,10},{10,1... | collective-permute-start | bytes 800 | tf_op jit(solution)/shard_map/ppermute | solution.py:27
  232.1 12.6 %collective-permute-start.31 = (f32[66,1]{1,0:T(8,128)S(1)}, f32[66,1]{1,0:T(8,128)S(1)}, u32[]{:S(2)}, u32[]{:S(2)}) collective-permute-start(f32[66,1]{1,0:T(8,128)S(1)} %get-tuple-element.82), channel_id=1, source_target_pairs={{1,0},{2,1},{3,2},{4,3},{5,4},{6,5},{7,6},{8,7},{9,8},{10,9},{11,1... | collective-permute-start | bytes 800 | tf_op jit(solution)/shard_map/ppermute | solution.py:28
  267.4 58.5 %collective-permute-start.58 = (f32[32,1]{1,0:T(8,128)}, f32[32,1]{1,0:T(8,128)}, u32[]{:S(2)}, u32[]{:S(2)}) collective-permute-start(f32[32,1]{1,0:T(8,128)} %get-tuple-element.171), channel_id=1, source_target_pairs={{2,0},{3,1},{4,2},{5,3},{6,4},{7,5},{8,6},{9,7},{10,8},{11,9},{12,... | collective-permute-start | bytes 392 | tf_op jit(solution)/shard_map/ppermute | solution.py:17
  277.5 52.2 %collective-permute-start.57 = (f32[32,1]{1,0:T(8,128)}, f32[32,1]{1,0:T(8,128)}, u32[]{:S(2)}, u32[]{:S(2)}) collective-permute-start(f32[32,1]{1,0:T(8,128)} %get-tuple-element.170), channel_id=1, source_target_pairs={{0,2},{1,3},{2,4},{3,5},{4,6},{5,7},{6,8},{7,9},{8,10},{9,11},{10,... | collective-permute-start | bytes 392 | tf_op jit(solution)/shard_map/ppermute | solution.py:17
  311.1 19.8 %collective-permute-start.56 = (f32[1,32]{1,0:T(1,128)S(1)}, f32[1,32]{1,0:T(1,128)S(1)}, u32[]{:S(2)}, u32[]{:S(2)}) collective-permute-start(f32[1,32]{1,0:T(1,128)S(1)} %slice_bitcast_fusion.3), channel_id=1, source_target_pairs={{0,32},{1,33},{2,34},{3,35},{4,36},{5,37},{6,38},{7,39},{8,40},{9,... | collective-permute-start | bytes 392 | tf_op jit(solution)/shard_map/ppermute | solution.py:17
  331.8 13.5 %collective-permute-start.62 = (f32[32,1]{1,0:T(8,128)S(1)}, f32[32,1]{1,0:T(8,128)S(1)}, u32[]{:S(2)}, u32[]{:S(2)}) collective-permute-start(f32[32,1]{1,0:T(8,128)S(1)} %get-tuple-element.169), channel_id=1, source_target_pairs={{2,0},{3,1},{4,2},{5,3},{6,4},{7,5},{8,6},{9,7},{10,8},{11,9},{12,... | collective-permute-start | bytes 392 | tf_op jit(solution)/shard_map/ppermute | solution.py:17
  349.4 13.2 %collective-permute-start.66 = (f32[32,1]{1,0:T(8,128)S(1)}, f32[32,1]{1,0:T(8,128)S(1)}, u32[]{:S(2)}, u32[]{:S(2)}) collective-permute-start(f32[32,1]{1,0:T(8,128)S(1)} %get-tuple-element.165), channel_id=1, source_target_pairs={{2,0},{3,1},{4,2},{5,3},{6,4},{7,5},{8,6},{9,7},{10,8},{11,9},{12,... | collective-permute-start | bytes 392 | tf_op jit(solution)/shard_map/ppermute | solution.py:17
  378.4 13.8 %collective-permute-start.74 = (f32[32,1]{1,0:T(8,128)S(1)}, f32[32,1]{1,0:T(8,128)S(1)}, u32[]{:S(2)}, u32[]{:S(2)}) collective-permute-start(f32[32,1]{1,0:T(8,128)S(1)} %get-tuple-element.157), channel_id=1, source_target_pairs={{4,0},{5,1},{6,2},{7,3},{8,4},{9,5},{10,6},{11,7},{12,8},{13,9},{1... | collective-permute-start | bytes 392 | tf_op jit(solution)/shard_map/ppermute | solution.py:17
  393.7 14.8 %collective-permute-start.78 = (f32[32,1]{1,0:T(8,128)S(1)}, f32[32,1]{1,0:T(8,128)S(1)}, u32[]{:S(2)}, u32[]{:S(2)}) collective-permute-start(f32[32,1]{1,0:T(8,128)S(1)} %get-tuple-element.155), channel_id=1, source_target_pairs={{4,0},{5,1},{6,2},{7,3},{8,4},{9,5},{10,6},{11,7},{12,8},{13,9},{1... | collective-permute-start | bytes 392 | tf_op jit(solution)/shard_map/ppermute | solution.py:17
  414.3 13.5 %collective-permute-start.82 = (f32[32,1]{1,0:T(8,128)S(1)}, f32[32,1]{1,0:T(8,128)S(1)}, u32[]{:S(2)}, u32[]{:S(2)}) collective-permute-start(f32[32,1]{1,0:T(8,128)S(1)} %get-tuple-element.151), channel_id=1, source_target_pairs={{4,0},{5,1},{6,2},{7,3},{8,4},{9,5},{10,6},{11,7},{12,8},{13,9},{1... | collective-permute-start | bytes 392 | tf_op jit(solution)/shard_map/ppermute | solution.py:17
  430.8 13.5 %collective-permute-start.86 = (f32[32,1]{1,0:T(8,128)S(1)}, f32[32,1]{1,0:T(8,128)S(1)}, u32[]{:S(2)}, u32[]{:S(2)}) collective-permute-start(f32[32,1]{1,0:T(8,128)S(1)} %get-tuple-element.147), channel_id=1, source_target_pairs={{4,0},{5,1},{6,2},{7,3},{8,4},{9,5},{10,6},{11,7},{12,8},{13,9},{1... | collective-permute-start | bytes 392 | tf_op jit(solution)/shard_map/ppermute | solution.py:17
  447.3 13.5 %collective-permute-start.90 = (f32[32,1]{1,0:T(8,128)S(1)}, f32[32,1]{1,0:T(8,128)S(1)}, u32[]{:S(2)}, u32[]{:S(2)}) collective-permute-start(f32[32,1]{1,0:T(8,128)S(1)} %get-tuple-element.143), channel_id=1, source_target_pairs={{4,0},{5,1},{6,2},{7,3},{8,4},{9,5},{10,6},{11,7},{12,8},{13,9},{1... | collective-permute-start | bytes 392 | tf_op jit(solution)/shard_map/ppermute | solution.py:17
  463.7 13.5 %collective-permute-start.94 = (f32[32,1]{1,0:T(8,128)S(1)}, f32[32,1]{1,0:T(8,128)S(1)}, u32[]{:S(2)}, u32[]{:S(2)}) collective-permute-start(f32[32,1]{1,0:T(8,128)S(1)} %get-tuple-element.139), channel_id=1, source_target_pairs={{4,0},{5,1},{6,2},{7,3},{8,4},{9,5},{10,6},{11,7},{12,8},{13,9},{1... | collective-permute-start | bytes 392 | tf_op jit(solution)/shard_map/ppermute | solution.py:17
  480.2 13.5 %collective-permute-start.98 = (f32[32,1]{1,0:T(8,128)S(1)}, f32[32,1]{1,0:T(8,128)S(1)}, u32[]{:S(2)}, u32[]{:S(2)}) collective-permute-start(f32[32,1]{1,0:T(8,128)S(1)} %get-tuple-element.135), channel_id=1, source_target_pairs={{4,0},{5,1},{6,2},{7,3},{8,4},{9,5},{10,6},{11,7},{12,8},{13,9},{1... | collective-permute-start | bytes 392 | tf_op jit(solution)/shard_map/ppermute | solution.py:17
  496.7 14.1 %collective-permute-start.102 = (f32[32,1]{1,0:T(8,128)S(1)}, f32[32,1]{1,0:T(8,128)S(1)}, u32[]{:S(2)}, u32[]{:S(2)}) collective-permute-start(f32[32,1]{1,0:T(8,128)S(1)} %get-tuple-element.131), channel_id=1, source_target_pairs={{4,0},{5,1},{6,2},{7,3},{8,4},{9,5},{10,6},{11,7},{12,8},{13,9},{1... | collective-permute-start | bytes 392 | tf_op jit(solution)/shard_map/ppermute | solution.py:17
  513.9 13.9 %collective-permute-start.106 = (f32[32,1]{1,0:T(8,128)S(1)}, f32[32,1]{1,0:T(8,128)S(1)}, u32[]{:S(2)}, u32[]{:S(2)}) collective-permute-start(f32[32,1]{1,0:T(8,128)S(1)} %get-tuple-element.127), channel_id=1, source_target_pairs={{2,0},{3,1},{4,2},{5,3},{6,4},{7,5},{8,6},{9,7},{10,8},{11,9},{12,... | collective-permute-start | bytes 392 | tf_op jit(solution)/shard_map/ppermute | solution.py:17
  530.7 14.1 %collective-permute-start.110 = (f32[32,1]{1,0:T(8,128)S(1)}, f32[32,1]{1,0:T(8,128)S(1)}, u32[]{:S(2)}, u32[]{:S(2)}) collective-permute-start(f32[32,1]{1,0:T(8,128)S(1)} %get-tuple-element.123), channel_id=1, source_target_pairs={{2,0},{3,1},{4,2},{5,3},{6,4},{7,5},{8,6},{9,7},{10,8},{11,9},{12,... | collective-permute-start | bytes 392 | tf_op jit(solution)/shard_map/ppermute | solution.py:17
  (123 other events, 1575.3 us)
where the time goes:
time: 715 us; the launch traced here: 707 us
  starting transfers between devices  414 us (58%)
  waiting for transfers between devices  150 us (21%)
  local copies, waits for them, and re-layouts  88.5 us (12%)
  other arithmetic  51.6 us (7%)
    ppermute x52, starting transfers between devices, shifted(): return lax.ppermute(block, axis, route)  176 us
    ppermute x42, starting transfers between devices, with_halo(): before = lax.ppermute(last, axis, up)  116 us
    ppermute x42, starting transfers between devices, with_halo(): after = lax.ppermute(first, axis, down)  116 us
    ppermute x42, waiting for transfers between devices, with_halo(): before = lax.ppermute(last, axis, up)  105 us
    reshape x10, local copies, waits for them, and re-layouts, coarsen(): return grid.reshape(height // 2, 2, breadth // 2, 2).sum(axis=(1, 3))  69.6 us
    ppermute x52, waiting for transfers between devices, shifted(): return lax.ppermute(block, axis, route)  35.1 us
    reduce_sum x15, other arithmetic, coarsen(): return grid.reshape(height // 2, 2, breadth // 2, 2).sum(axis=(1, 3))  33.8 us
  transfers between devices with their start and end apart: 144, of which 54 were waited for; matrix products, arithmetic and copies ran while one was open for 18% of the time, Pallas kernels for 0%

commit v1 on v0

v1 whole, which is shorter than its diff:
```python
import jax
import jax.numpy as jnp
from jax import lax
from jax.experimental import pallas as pl
from jax.experimental.pallas import tpu as pltpu
from jax.sharding import PartitionSpec as P

OMEGA = 0.8
COARSE_SWEEPS = 8
SIZE = 256
HALO = 96
FRAME = 512
PAD = 8
LANES = 128
MIB = 1 << 20


def iota(axis):
    return lax.broadcasted_iota(jnp.int32, (8, LANES), axis)


def roll(x, amount, axis):
    return pltpu.roll(x, amount % x.shape[axis], axis)


def row_shift(tiles):
    row = iota(0)
    down = [roll(x, 1, 0) for x in tiles[:-1]]
    up = [roll(x, -1, 0) for x in tiles[1:]]
    before = [jnp.where(row == 0, down[j], down[j + 1]) for j in range(len(down) - 1)]
    after = [jnp.where(row == 7, up[j + 1], up[j]) for j in range(len(up) - 1)]
    return before, after


def lane_shift(tiles, step):
    lane = iota(1)
    right = [roll(x, step, 1) for x in tiles]
    left = [roll(x, -step, 1) for x in tiles]
    count = len(tiles)
    before = [jnp.where(lane < step, right[t - 1], right[t]) for t in range(count)]
    after = [jnp.where(lane >= LANES - step, left[(t + 1) % count], left[t]) for t in range(count)]
    return before, after


def around(ref, row, depth, step):
    count = ref.shape[0]
    rows = [[ref[t, pl.ds(row + 8 * j - 8, 8), :] for j in range(depth + 2)] for t in range(count)]
    west, east = zip(*[row_shift(tiles) for tiles in rows])
    cells = {}
    for j in range(depth):
        here = [rows[t][j + 1] for t in range(count)]
        south, north = lane_shift(here, step)
        for t in range(count):
            cells[t, j] = (here[t], west[t][j], east[t][j], south[t], north[t])
    return cells


def over_rows(first, last, depth, body):
    trips = (last - first) // (8 * depth)

    def trip(i, carry):
        body(pl.multiple_of(first + i * 8 * depth, 8))
        return carry

    lax.fori_loop(0, trips, trip, 0)


def rows_at(row, j):
    return pl.ds(row + 8 * j, 8)


def face_pass(level, first, last, depth, guess=None):
    def body(row):
        cells = None if guess is None else around(guess, row, depth, level["step"])
        for (t, j), (k, kw, ke, ks, kn) in around(level["k"], row, depth, level["step"]).items():
            at = rows_at(row, j)
            west, east, south, north = (0.5 * (k + other) for other in (kw, ke, ks, kn))
            stored = level["s"][t, at, :]
            diagonal = (((stored + west) + east) + south) + north
            scale = jnp.where(stored > 0.0, OMEGA / diagonal, 0.0)
            level["d"][t, at, :] = diagonal
            side = scale * level["b"][t, at, :]
            level["b"][t, at, :] = side
            weights = [scale * face for face in (west, east, south, north)]
            for name, weight in zip("weon", weights):
                level[name][t, at, :] = weight
            if cells:
                v, *others = cells[t, j]
                side = side + (1.0 - OMEGA) * v
                for weight, other in zip(weights, others):
                    side = side + weight * other
            level["u"][t, at, :] = side

    over_rows(first, last, depth, body)


def weighted(level, t, at, cell):
    _, vw, ve, vs, vn = cell
    total = level["b"][t, at, :] + level["w"][t, at, :] * vw
    total = total + level["e"][t, at, :] * ve
    total = total + level["o"][t, at, :] * vs
    return total + level["n"][t, at, :] * vn


def sweep_pass(level, source, target, first, last, depth):
    def body(row):
        for (t, j), cell in around(source, row, depth, level["step"]).items():
            at = rows_at(row, j)
            target[t, at, :] = (1.0 - OMEGA) * cell[0] + weighted(level, t, at, cell)

    over_rows(first, last, depth, body)


def residual_pass(level, source, target, first, last, depth):
    def body(row):
        for (t, j), cell in around(source, row, depth, level["step"]).items():
            at = rows_at(row, j)
            gap = (1.0 / OMEGA) * weighted(level, t, at, cell) - cell[0]
            target[t, at, :] = level["d"][t, at, :] * gap

    over_rows(first, last, depth, body)


def pair_sum(source, t, row, step):
    x = source[t, pl.ds(row, 8, stride=2), :] + source[t, pl.ds(row + 1, 8, stride=2), :]
    upper = (iota(1) & step) != 0
    return x + jnp.where(upper, roll(x, step, 1), roll(x, -step, 1))


def coarsen_pass(triples, step, first, last):
    height = 2 if (last - first) % 16 == 0 else 1

    def body(row):
        for j in range(height):
            for source, target, factor in triples:
                for t in range(source.shape[0]):
                    x = pair_sum(source, t, 2 * row + 16 * j + PAD, step)
                    target[t, rows_at(row + PAD, j), :] = x if factor == 1.0 else factor * x

    over_rows(first, last, height, body)


def correct_pass(source, base, target, first, last, shift):
    def body(row):
        for t in range(source.shape[0]):
            x = source[t, pl.ds(row, 8), :]
            for half in range(2):
                at = pl.ds(2 * row - shift + half, 8, stride=2)
                target[t, at, :] = base[t, at, :] + x

    over_rows(first, last, 1, body)


def clear_rows(refs, at):
    for ref in refs:
        for row in at:
            for t in range(ref.shape[0]):
                ref[t, pl.ds(row, 8), :] = jnp.zeros((8, LANES), jnp.float32)


def pack_kernel(k, s, b, v, own, low, high, sems):
    copies = []
    for i, a in enumerate((k, s, b, v)):
        for t in range(2):
            copies.append(pltpu.make_async_copy(a.at[:, pl.ds(LANES * t, LANES)], own.at[i, t], sems.at[2 * i + t]))
    for copy in copies:
        copy.start()
    for copy in copies:
        copy.wait()

    def body(row):
        lane = iota(1)
        for j in range(2):
            at = rows_at(row, j)
            x = [own[i, 0, at, :] for i in range(4)]
            low[0, at, :] = jnp.where(lane < 96, x[0], roll(x[1], 96, 1))
            low[1, at, :] = jnp.where(lane < 64, roll(x[1], 96, 1), roll(x[2], 64, 1))
            low[2, at, :] = jnp.where(lane < 32, roll(x[2], 64, 1), roll(x[3], 32, 1))
            y = [own[i, 1, at, :] for i in range(4)]
            high[0, at, :] = jnp.where(lane < 96, roll(y[0], 96, 1), roll(y[1], 64, 1))
            high[1, at, :] = jnp.where(lane < 64, roll(y[1], 64, 1), roll(y[2], 32, 1))
            high[2, at, :] = jnp.where(lane < 32, roll(y[2], 32, 1), y[3])

    over_rows(0, SIZE, 2, body)


def unpack_kernel(own, before, after, middle, top, bottom):
    def widened(row):
        lane = iota(1)
        at = pl.ds(row, 8)
        m = [before[i, at, :] for i in range(3)]
        left = (
            roll(m[0], 32, 1),
            jnp.where(lane < 64, roll(m[0], 64, 1), roll(m[1], 64, 1)),
            jnp.where(lane < 96, roll(m[1], 96, 1), roll(m[2], 96, 1)),
            m[2],
        )
        m = [after[i, at, :] for i in range(3)]
        right = (
            m[0],
            jnp.where(lane < 32, roll(m[0], 32, 1), roll(m[1], 32, 1)),
            jnp.where(lane < 64, roll(m[1], 64, 1), roll(m[2], 64, 1)),
            roll(m[2], 96, 1),
        )
        for i in range(4):
            yield i, 0, jnp.where(lane < 32, 0.0, left[i])
            yield i, 1, own[i, 0, at, :]
            yield i, 2, own[i, 1, at, :]
            yield i, 3, jnp.where(lane < 96, right[i], 0.0)

    def part(target, shift):
        def body(row):
            for i, t, x in widened(row):
                middle[i, t, pl.ds(row, 8), :] = x
                if target is not None:
                    target[i, t, pl.ds(row - shift, 8), :] = x

        return body

    over_rows(0, HALO, 1, part(top, 0))
    over_rows(HALO, SIZE - HALO, 1, part(None, 0))
    over_rows(SIZE - HALO, SIZE, 1, part(bottom, SIZE - HALO))


KEPT = "vbweon"
DOWN = ((32, 480, 4), (16, 240, 4), (8, 120, 2), (0, 64, 4))


def frame_rows(depth):
    return (FRAME >> depth) + 2 * PAD


def down_kernel(middle, above, below, *refs):
    kept, message, refs = refs[0:24], refs[24], refs[25:]
    levels = [dict(zip(KEPT, kept))]
    levels[0].update(zip("ksud", refs[:4]))
    frame = [levels[0][n] for n in "ksbv"]
    for depth in range(1, 4):
        level = dict(zip(KEPT, kept[6 * depth : 6 * depth + 6]))
        level.update(zip("ksud", refs[4 * depth : 4 * depth + 4]))
        levels.append(level)
    last4 = refs[16]

    for depth, (level, (first, last, _)) in enumerate(zip(levels, DOWN)):
        level["step"] = 1 << depth
        clear_rows([level[n] for n in "ksbvuweon"], (PAD + first - 8, PAD + last))

    def fill(row):
        for i in range(4):
            for t in range(4):
                frame[i][t, pl.ds(PAD + 32 + row, 8), :] = above[i, t, pl.ds(row, 8), :]
                frame[i][t, pl.ds(PAD + 384 + row, 8), :] = below[i, t, pl.ds(row, 8), :]

    over_rows(0, HALO, 1, fill)

    def fill_middle(row):
        for i in range(4):
            for t in range(4):
                at = pl.ds(PAD + 128 + row, 8)
                frame[i][t, at, :] = middle[i, t, pl.ds(row, 8), :]

    over_rows(0, SIZE, 1, fill_middle)

    for depth, (level, (first, last, height)) in enumerate(zip(levels, DOWN)):
        v, u = level["v"], level["u"]
        face_pass(level, PAD + first, PAD + last, height, None if depth else v)
        sweep_pass(level, u, v, PAD + first, PAD + last, height)
        residual_pass(level, v, u, PAD + first, PAD + last, height)
        if depth < 3:
            coarse = levels[depth + 1]
            goals = (coarse["k"], coarse["s"], coarse["b"])
            start, stop, _ = DOWN[depth + 1]
        else:
            goals = (last4.at[0], last4.at[1], last4.at[2])
            start, stop = 0, 32
        triples = tuple(zip((level["k"], level["s"], u), goals, (0.5, 1.0, 1.0)))
        coarsen_pass(triples, level["step"], start, stop)

    shape = (LANES, LANES)
    source = lax.broadcasted_iota(jnp.int32, shape, 0)
    goal = lax.broadcasted_iota(jnp.int32, shape, 1)
    for i in range(3):
        total = jnp.zeros((32, LANES), jnp.float32)
        for t in range(4):
            pick = (source + LANES * t == 16 * goal).astype(jnp.float32)
            total = total + jnp.dot(
                last4[i, t, pl.ds(PAD, 32), :],
                pick,
                precision=lax.Precision.HIGHEST,
                preferred_element_type=jnp.float32,
            )
        message[i, :, :] = total


def up_kernel(merged, *refs):
    kept, out, refs = refs[0:24], refs[24], refs[25:]
    four = dict(zip("ksbvudweon", refs[0:10]), step=1)
    five = dict(zip("ksbvudweon", refs[10:20]), step=2)
    levels = [dict(zip(KEPT, kept[6 * depth : 6 * depth + 6])) for depth in range(4)]
    for depth, level in enumerate(levels):
        rows = pl.ds(PAD + (128 >> depth) - 16, (SIZE >> depth) + 32)
        for name in KEPT:
            level[name] = level[name].at[:, rows, :]
        level.update(zip("uc", refs[20 + 2 * depth : 22 + 2 * depth]), step=1 << depth)
    wide = refs[28]

    for i, name in enumerate("ksb"):
        four[name][0, pl.ds(PAD, 64), :] = merged[i]
    clear_rows([four[n] for n in "kvu"], (0, PAD + 64))
    clear_rows([five[n] for n in "kvu"], (0, PAD + 32))
    face_pass(four, PAD, PAD + 64, 4)
    sweep_pass(four, four["u"], four["v"], PAD, PAD + 64, 4)
    residual_pass(four, four["v"], four["u"], PAD, PAD + 64, 4)
    goals = (five["k"], five["s"], five["b"])
    coarsen_pass(tuple(zip((four["k"], four["s"], four["u"]), goals, (0.5, 1.0, 1.0))), 1, 0, 32)
    face_pass(five, PAD, PAD + 32, 4)
    v, u = five["v"], five["u"]
    for _ in range(COARSE_SWEEPS - 1):
        sweep_pass(five, u, v, PAD, PAD + 32, 4)
        v, u = u, v
    correct_pass(u, four["v"], four["v"], PAD, PAD + 32, PAD)
    sweep_pass(four, four["v"], four["u"], PAD, PAD + 64, 4)
    sweep_pass(four, four["u"], four["v"], PAD, PAD + 64, 4)

    shape = (LANES, LANES)
    source = lax.broadcasted_iota(jnp.int32, shape, 0)
    goal = lax.broadcasted_iota(jnp.int32, shape, 1)
    fine = four["v"][0, pl.ds(PAD + 16, 32), :]
    for t in range(4):
        pick = (source == (goal + LANES * t) // 16 + 16).astype(jnp.float32)
        wide[t, pl.ds(0, 32), :] = jnp.dot(
            fine, pick, precision=lax.Precision.HIGHEST, preferred_element_type=jnp.float32
        )

    coarse, first, last, shift = wide, 0, 32, 0
    for depth in (3, 2, 1, 0):
        level = levels[depth]
        size = SIZE >> depth
        u, c = level["u"], level["c"]
        correct_pass(coarse, level["v"], c, first, last, shift)
        sweep_pass(level, c, u, 8, size + 24, 2)
        if depth > 0:
            clear_rows([u], (0, size + 24))
            sweep_pass(level, u, c, 8, size + 24, 2)
            coarse, first, last, shift = c, 8, size + 24, 16

    level = levels[0]

    def body(row):
        for (t, j), cell in around(level["u"], row, 2, 1).items():
            if t in (1, 2):
                at = rows_at(row, j)
                value = (1.0 - OMEGA) * cell[0] + weighted(level, t, at, cell)
                out[pl.ds(row + 8 * j - 16, 8), LANES * (t - 1) : LANES * t] = value

    over_rows(16, SIZE + 16, 2, body)


def shape_of(*shape):
    return jax.ShapeDtypeStruct(shape, jnp.float32)


def vmem(*shape):
    return pltpu.VMEM(shape, jnp.float32)


HERE = pl.BlockSpec(memory_space=pltpu.VMEM)
AWAY = pl.BlockSpec(memory_space=pltpu.HBM)


def cost(flops, count):
    return pl.CostEstimate(flops=flops, bytes_accessed=count, transcendentals=0)


def exchange(up_block, down_block, axis):
    count = lax.axis_size(axis)
    up = [(i, i + 1) for i in range(count - 1)]
    down = [(i + 1, i) for i in range(count - 1)]
    return lax.ppermute(up_block, axis, up), lax.ppermute(down_block, axis, down)


def per_device(pressure, source, conductivity, storage):
    blocks = (conductivity, storage, source, pressure)
    own, low, high = pl.pallas_call(
        pack_kernel,
        out_shape=(shape_of(4, 2, SIZE, LANES), shape_of(3, SIZE, LANES), shape_of(3, SIZE, LANES)),
        in_specs=[AWAY] * 4,
        out_specs=(HERE,) * 3,
        scratch_shapes=[pltpu.SemaphoreType.DMA((8,))],
        cost_estimate=cost(2 * MIB, 2 * MIB),
        compiler_params=pltpu.CompilerParams(vmem_limit_bytes=8 * MIB),
    )(*blocks)
    before, after = exchange(high, low, "gy")

    middle, top, bottom = pl.pallas_call(
        unpack_kernel,
        out_shape=(shape_of(4, 4, SIZE, LANES), shape_of(4, 4, HALO, LANES), shape_of(4, 4, HALO, LANES)),
        in_specs=[HERE] * 3,
        out_specs=(HERE,) * 3,
        cost_estimate=cost(4 * MIB, 4 * MIB),
        compiler_params=pltpu.CompilerParams(vmem_limit_bytes=16 * MIB),
    )(own, before, after)
    above, below = exchange(bottom, top, "gx")

    levels = [(4, frame_rows(depth), LANES) for depth in range(4)]
    kept = [shape for shape in levels for _ in range(6)]
    *kept, message = pl.pallas_call(
        down_kernel,
        out_shape=(
            *[shape_of(*shape) for shape in kept],
            shape_of(3, 32, LANES),
        ),
        in_specs=[HERE] * 3,
        out_specs=(HERE,) * 25,
        scratch_shapes=[
            *[vmem(*shape) for shape in levels for _ in range(4)],
            vmem(3, 4, 32 + 2 * PAD, LANES),
        ],
        cost_estimate=cost(40 * MIB, 12 * MIB),
        compiler_params=pltpu.CompilerParams(vmem_limit_bytes=40 * MIB),
    )(middle, above, below)

    left, right = exchange(message, message, "gy")
    wide = jnp.concatenate(
        [left[:, :, 0:20], message[:, :, 4:28], right[:, :, 12:32], jnp.zeros((3, 32, 64), jnp.float32)], axis=2
    )
    upper, lower = exchange(wide, wide, "gx")
    merged = jnp.concatenate([upper[:, 0:20], wide[:, 4:28], lower[:, 12:32]], axis=1)

    return pl.pallas_call(
        up_kernel,
        out_shape=shape_of(SIZE, SIZE),
        in_specs=[HERE] * 25,
        out_specs=HERE,
        scratch_shapes=[
            *[vmem(1, 64 + 2 * PAD, LANES)] * 10,
            *[vmem(1, 32 + 2 * PAD, LANES)] * 10,
            *[vmem(4, (SIZE >> depth) + 32, LANES) for depth in range(4) for _ in range(2)],
            vmem(4, 32, LANES),
        ],
        cost_estimate=cost(40 * MIB, 12 * MIB),
        compiler_params=pltpu.CompilerParams(vmem_limit_bytes=40 * MIB),
    )(merged, *kept)


def solution(mesh):
    placed = (P("gx", "gy"),) * 4
    return jax.shard_map(per_device, mesh=mesh, in_specs=placed, out_specs=P("gx", "gy"), check_vma=False)
```

time: 715 us -> 94.6 us (0.13)
  the two profiles are of different devices: /device:TPU:130 before, /device:TPU:99 now
where the time goes in v1:
time: 94.6 us; the launch traced here: 94.2 us
  Pallas kernels  30.1 us (32%)
  waiting for transfers between devices  29.5 us (31%)
  starting transfers between devices  29 us (31%)
  local copies, waits for them, and re-layouts  5.37 us (6%)
    ppermute x4, waiting for transfers between devices, exchange(): lax.ppermute(up_block, axis, up)  18.4 us
    pallas_call x1, Pallas kernels, per_device(): pl.pallas_call(down_kernel, out_shape=(*[shape_of(*shape) for shape in ke...  16.9 us
    ppermute x4, starting transfers between devices, exchange(): lax.ppermute(up_block, axis, up)  14.7 us
    ppermute x4, starting transfers between devices, exchange(): lax.ppermute(down_block, axis, down)  14.2 us
    ppermute x4, waiting for transfers between devices, exchange(): lax.ppermute(down_block, axis, down)  11.2 us
    pallas_call x1, Pallas kernels, per_device(): pl.pallas_call(up_kernel, out_shape=shape_of(SIZE, SIZE), in_specs=[HERE]...  9.1 us
    unnamed x10, local copies, waits for them, and re-layouts  5.13 us
    pallas_call x1, Pallas kernels, per_device(): pl.pallas_call(unpack_kernel, out_shape=(shape_of(4, 4, SIZE, LANES), sha...  2.66 us
  transfers between devices with their start and end apart: 8, of which 6 were waited for; matrix products, arithmetic and copies ran while one was open for 0% of the time, Pallas kernels for 0%

profile of v1, /device:TPU:99, one launch (start us, length us, event | category | flops | bytes accessed | tf_op | source)
XLA Modules:
  0.0 94.2 jit_solution(10001808769138783782)
XLA Ops:
  0.0 0.0 copy-start.1
  0.0 0.9 %copy-done.1 = f32[256,256]{1,0:T(8,128)S(1)} copy-done((f32[256,256]{1,0:T(8,128)S(1)}, f32[256,256]{1,0:T(8,128)}, u32[]{:S(2)}) %copy-start.1) | copy-done | bytes 262168
  1.0 0.0 copy-start.2
  1.0 0.9 %copy-done.2 = f32[256,256]{1,0:T(8,128)S(1)} copy-done((f32[256,256]{1,0:T(8,128)S(1)}, f32[256,256]{1,0:T(8,128)}, u32[]{:S(2)}) %copy-start.2) | copy-done | bytes 262168
  1.9 0.9 %copy-done.3 = f32[256,256]{1,0:T(8,128)S(1)} copy-done((f32[256,256]{1,0:T(8,128)S(1)}, f32[256,256]{1,0:T(8,128)}, u32[]{:S(2)}) %copy-start.3) | copy-done | bytes 262168
  2.9 0.9 %copy-done.4 = f32[256,256]{1,0:T(8,128)S(1)} copy-done((f32[256,256]{1,0:T(8,128)S(1)}, f32[256,256]{1,0:T(8,128)}, u32[]{:S(2)}) %copy-start.4) | copy-done | bytes 262168
  3.8 1.5 %shard_map.46 = (f32[4,2,256,128]{3,2,1,0:T(8,128)S(1)}, f32[3,256,128]{2,1,0:T(8,128)S(1)}, f32[3,256,128]{2,1,0:T(8,128)S(1)}) custom-call(f32[256,256]{1,0:T(8,128)S(1)} %copy-done.1, f32[256,256]{1,0:T(8,128)S(1)} %copy-done.2, f32[256,256]{1,0:T(8,128)S(1)} %copy-done.3, f32[256,256]{1,0:T(8,128)S(1)} %copy-done.4), custom_call_target="tpu_custom_call" | custom-call | flops 2097152 | bytes 2097152 | tf_op jit(solution)/shard_map/pallas_call | solution.py:384
  5.3 3.2 %collective-permute-start = (f32[3,256,128]{2,1,0:T(8,128)S(1)}, f32[3,256,128]{2,1,0:T(8,128)S(1)}, u32[]{:S(2)}, u32[]{:S(2)}) collective-permute-start(f32[3,256,128]{2,1,0:T(8,128)S(1)} %get-tuple-element.37), channel_id=1, source_target_pairs={{0,1},{1,2},{2,3},{3,4},{4,5},{5,6},{6,7},{7,8},{8,9},{9,10},{10,1... | collective-permute-start | bytes 1179656 | tf_op jit(solution)/shard_map/ppermute | solution.py:379
  8.5 4.2 %collective-permute-start.1 = (f32[3,256,128]{2,1,0:T(8,128)S(1)}, f32[3,256,128]{2,1,0:T(8,128)S(1)}, u32[]{:S(2)}, u32[]{:S(2)}) collective-permute-start(f32[3,256,128]{2,1,0:T(8,128)S(1)} %get-tuple-element.38), channel_id=1, source_target_pairs={{1,0},{2,1},{3,2},{4,3},{5,4},{6,5},{7,6},{8,7},{9,8},{10,9},{11,1... | collective-permute-start | bytes 1179656 | tf_op jit(solution)/shard_map/ppermute | solution.py:379
  12.7 6.6 %collective-permute-done.before = f32[3,256,128]{2,1,0:T(8,128)S(1)} collective-permute-done((f32[3,256,128]{2,1,0:T(8,128)S(1)}, f32[3,256,128]{2,1,0:T(8,128)S(1)}, u32[]{:S(2)}, u32[]{:S(2)}) %collective-permute-start) | collective-permute-done | bytes 393248 | tf_op jit(solution)/shard_map/ppermute | solution.py:379
  19.3 0.9 collective-permute-done.1.after
  20.2 2.7 %shard_map.47 = (f32[4,4,256,128]{3,2,1,0:T(8,128)S(1)}, f32[4,4,96,128]{3,2,1,0:T(8,128)S(1)}, f32[4,4,96,128]{3,2,1,0:T(8,128)S(1)}) custom-call(f32[4,2,256,128]{3,2,1,0:T(8,128)S(1)} %get-tuple-element.36.own, f32[3,256,128]{2,1,0:T(8,128)S(1)} %collective-permute-done.before, f32[3,256,128]{2,1,0:T(8,128)S(1)} %collective-permute-done.1.after), custom_call_target="tpu_custom_call" | custom-call | flops 4194304 | bytes 4194304 | tf_op jit(solution)/shard_map/pallas_call | solution.py:395
  22.8 0.0 copy-start
  22.9 1.3 %copy-done = f32[4,4,256,128]{3,2,1,0:T(8,128)} copy-done((f32[4,4,256,128]{3,2,1,0:T(8,128)}, f32[4,4,256,128]{3,2,1,0:T(8,128)S(1)}, u32[]{:S(2)}) %copy-start) | copy-done | bytes 2097176
  24.2 6.4 %collective-permute-start.2 = (f32[4,4,96,128]{3,2,1,0:T(8,128)S(1)}, f32[4,4,96,128]{3,2,1,0:T(8,128)S(1)}, u32[]{:S(2)}, u32[]{:S(2)}) collective-permute-start(f32[4,4,96,128]{3,2,1,0:T(8,128)S(1)} %get-tuple-element.40), channel_id=1, source_target_pairs={{0,16},{16,32},{32,48},{48,64},{64,80},{80,96},{96,112},{112,128},... | collective-permute-start | bytes 2359304 | tf_op jit(solution)/shard_map/ppermute | solution.py:379
  30.6 1.9 %collective-permute-start.3 = (f32[4,4,96,128]{3,2,1,0:T(8,128)S(1)}, f32[4,4,96,128]{3,2,1,0:T(8,128)S(1)}, u32[]{:S(2)}, u32[]{:S(2)}) collective-permute-start(f32[4,4,96,128]{3,2,1,0:T(8,128)S(1)} %get-tuple-element.41), channel_id=1, source_target_pairs={{16,0},{32,16},{48,32},{64,48},{80,64},{96,80},{112,96},{128,112},... | collective-permute-start | bytes 2359304 | tf_op jit(solution)/shard_map/ppermute | solution.py:379
  32.6 7.0 %collective-permute-done.2.above = f32[4,4,96,128]{3,2,1,0:T(8,128)S(1)} collective-permute-done((f32[4,4,96,128]{3,2,1,0:T(8,128)S(1)}, f32[4,4,96,128]{3,2,1,0:T(8,128)S(1)}, u32[]{:S(2)}, u32[]{:S(2)}) %collective-permute-start.2) | collective-permute-done | bytes 786464 | tf_op jit(solution)/shard_map/ppermute | solution.py:379
  39.5 5.6 %collective-permute-done.3.below = f32[4,4,96,128]{3,2,1,0:T(8,128)S(1)} collective-permute-done((f32[4,4,96,128]{3,2,1,0:T(8,128)S(1)}, f32[4,4,96,128]{3,2,1,0:T(8,128)S(1)}, u32[]{:S(2)}, u32[]{:S(2)}) %collective-permute-start.3) | collective-permute-done | bytes 786464 | tf_op jit(solution)/shard_map/ppermute | solution.py:379
  45.1 16.9 %shard_map.48 = (f32[4,528,128]{2,1,0:T(8,128)S(1)}, f32[4,528,128]{2,1,0:T(8,128)S(1)}, f32[4,528,128]{2,1,0:T(8,128)S(1)}, f32[4,528,128]{2,1,0:T(8,128)S(1)},...) custom-call(f32[4,4,256,128]{3,2,1,0:T(8,128)} %copy-done, ...), custom_call_target="tpu_custom_call" | custom-call | flops 41943040 | bytes 12582912 | tf_op jit(solution)/shard_map/pallas_call | solution.py:407
  62.0 6.2 %collective-permute-start.5 = (f32[3,32,128]{2,1,0:T(8,128)S(1)}, f32[3,32,128]{2,1,0:T(8,128)S(1)}, u32[]{:S(2)}, u32[]{:S(2)}) collective-permute-start(f32[3,32,128]{2,1,0:T(8,128)S(1)} %get-tuple-element.42), channel_id=1, source_target_pairs={{1,0},{2,1},{3,2},{4,3},{5,4},{6,5},{7,6},{8,7},{9,8},{10,9},{11,1... | collective-permute-start | bytes 147464 | tf_op jit(solution)/shard_map/ppermute | solution.py:379
  68.2 1.9 %collective-permute-start.4 = (f32[3,32,128]{2,1,0:T(8,128)S(1)}, f32[3,32,128]{2,1,0:T(8,128)S(1)}, u32[]{:S(2)}, u32[]{:S(2)}) collective-permute-start(f32[3,32,128]{2,1,0:T(8,128)S(1)} %get-tuple-element.42), channel_id=1, source_target_pairs={{0,1},{1,2},{2,3},{3,4},{4,5},{5,6},{6,7},{7,8},{8,9},{9,10},{10,1... | collective-permute-start | bytes 147464 | tf_op jit(solution)/shard_map/ppermute | solution.py:379
  70.2 0.1 pad.6.clone
  70.2 0.1 slice.19
  70.3 0.0 collective-permute-done.5
  70.3 0.1 slice.25
  70.4 4.8 %collective-permute-done.4 = f32[3,32,128]{2,1,0:T(8,128)S(1)} collective-permute-done((f32[3,32,128]{2,1,0:T(8,128)S(1)}, f32[3,32,128]{2,1,0:T(8,128)S(1)}, u32[]{:S(2)}, u32[]{:S(2)}) %collective-permute-start.4) | collective-permute-done | bytes 49184 | tf_op jit(solution)/shard_map/ppermute | solution.py:379
  75.2 0.1 maximum_maximum_fusion
  75.3 3.2 %collective-permute-start.6 = (f32[3,32,128]{2,1,0:T(8,128)S(1)}, f32[3,32,128]{2,1,0:T(8,128)S(1)}, u32[]{:S(2)}, u32[]{:S(2)}) collective-permute-start(f32[3,32,128]{2,1,0:T(8,128)S(1)} %maximum_maximum_fusion), channel_id=1, source_target_pairs={{0,16},{16,32},{32,48},{48,64},{64,80},{80,96},{96,112},{112,128},... | collective-permute-start | bytes 147464 | tf_op jit(solution)/shard_map/ppermute | solution.py:379
  78.5 1.9 %collective-permute-start.7 = (f32[3,32,128]{2,1,0:T(8,128)S(1)}, f32[3,32,128]{2,1,0:T(8,128)S(1)}, u32[]{:S(2)}, u32[]{:S(2)}) collective-permute-start(f32[3,32,128]{2,1,0:T(8,128)S(1)} %maximum_maximum_fusion), channel_id=1, source_target_pairs={{16,0},{32,16},{48,32},{64,48},{80,64},{96,80},{112,96},{128,112},... | collective-permute-start | bytes 147464 | tf_op jit(solution)/shard_map/ppermute | solution.py:379
  80.4 0.0 collective-permute-done.6
  80.4 4.7 %collective-permute-done.7 = f32[3,32,128]{2,1,0:T(8,128)S(1)} collective-permute-done((f32[3,32,128]{2,1,0:T(8,128)S(1)}, f32[3,32,128]{2,1,0:T(8,128)S(1)}, u32[]{:S(2)}, u32[]{:S(2)}) %collective-permute-start.7) | collective-permute-done | bytes 49184 | tf_op jit(solution)/shard_map/ppermute | solution.py:379
  85.1 9.1 %shard_map.49 = f32[256,256]{1,0:T(8,128)} custom-call(f32[3,64,128]{2,1,0:T(8,128)S(1)} %pad_maximum_fusion.merged, f32[4,528,128]{2,1,0:T(8,128)S(1)} %get-tuple-element.43.refs_0_, f32[4,528,128]{2,1,0:T(8,128)S(1)} %get-tuple-element.44.refs_1_, f32[4,528,128]{2,1,0:T(8,128)S(1)} %get-tuple-element.45.refs_2_, ...), custom_call_target="tpu_custom_call" | custom-call | flops 41943040 | bytes 12582912 | tf_op jit(solution)/shard_map/pallas_call | solution.py:430
  (7 shorter events, 0.0 us)
Async XLA Ops:
  0.0 0.9 %copy-start.1 = (f32[256,256]{1,0:T(8,128)S(1)}, f32[256,256]{1,0:T(8,128)}, u32[]{:S(2)}) copy-start(f32[256,256]{1,0:T(8,128)} %k.1) | copy-start | bytes 786436
  1.0 0.9 %copy-start.2 = (f32[256,256]{1,0:T(8,128)S(1)}, f32[256,256]{1,0:T(8,128)}, u32[]{:S(2)}) copy-start(f32[256,256]{1,0:T(8,128)} %s.1) | copy-start | bytes 786436
  1.9 0.9 %copy-start.3 = (f32[256,256]{1,0:T(8,128)S(1)}, f32[256,256]{1,0:T(8,128)}, u32[]{:S(2)}) copy-start(f32[256,256]{1,0:T(8,128)} %b.1) | copy-start | bytes 786436
  2.9 0.9 %copy-start.4 = (f32[256,256]{1,0:T(8,128)S(1)}, f32[256,256]{1,0:T(8,128)}, u32[]{:S(2)}) copy-start(f32[256,256]{1,0:T(8,128)} %v.1) | copy-start | bytes 786436
  5.3 14.0 %collective-permute-start = (f32[3,256,128]{2,1,0:T(8,128)S(1)}, f32[3,256,128]{2,1,0:T(8,128)S(1)}, u32[]{:S(2)}, u32[]{:S(2)}) collective-permute-start(f32[3,256,128]{2,1,0:T(8,128)S(1)} %get-tuple-element.37), channel_id=1, source_target_pairs={{0,1},{1,2},{2,3},{3,4},{4,5},{5,6},{6,7},{7,8},{8,9},{9,10},{10,1... | collective-permute-start | bytes 1179656 | tf_op jit(solution)/shard_map/ppermute | solution.py:379
  8.5 11.7 %collective-permute-start.1 = (f32[3,256,128]{2,1,0:T(8,128)S(1)}, f32[3,256,128]{2,1,0:T(8,128)S(1)}, u32[]{:S(2)}, u32[]{:S(2)}) collective-permute-start(f32[3,256,128]{2,1,0:T(8,128)S(1)} %get-tuple-element.38), channel_id=1, source_target_pairs={{1,0},{2,1},{3,2},{4,3},{5,4},{6,5},{7,6},{8,7},{9,8},{10,9},{11,1... | collective-permute-start | bytes 1179656 | tf_op jit(solution)/shard_map/ppermute | solution.py:379
  22.8 1.3 %copy-start = (f32[4,4,256,128]{3,2,1,0:T(8,128)}, f32[4,4,256,128]{3,2,1,0:T(8,128)S(1)}, u32[]{:S(2)}) copy-start(f32[4,4,256,128]{3,2,1,0:T(8,128)S(1)} %get-tuple-element.39.middle) | copy-start | bytes 6291460
  24.2 15.4 %collective-permute-start.2 = (f32[4,4,96,128]{3,2,1,0:T(8,128)S(1)}, f32[4,4,96,128]{3,2,1,0:T(8,128)S(1)}, u32[]{:S(2)}, u32[]{:S(2)}) collective-permute-start(f32[4,4,96,128]{3,2,1,0:T(8,128)S(1)} %get-tuple-element.40), channel_id=1, source_target_pairs={{0,16},{16,32},{32,48},{48,64},{64,80},{80,96},{96,112},{112,128},... | collective-permute-start | bytes 2359304 | tf_op jit(solution)/shard_map/ppermute | solution.py:379
  30.6 14.5 %collective-permute-start.3 = (f32[4,4,96,128]{3,2,1,0:T(8,128)S(1)}, f32[4,4,96,128]{3,2,1,0:T(8,128)S(1)}, u32[]{:S(2)}, u32[]{:S(2)}) collective-permute-start(f32[4,4,96,128]{3,2,1,0:T(8,128)S(1)} %get-tuple-element.41), channel_id=1, source_target_pairs={{16,0},{32,16},{48,32},{64,48},{80,64},{96,80},{112,96},{128,112},... | collective-permute-start | bytes 2359304 | tf_op jit(solution)/shard_map/ppermute | solution.py:379
  62.0 8.3 %collective-permute-start.5 = (f32[3,32,128]{2,1,0:T(8,128)S(1)}, f32[3,32,128]{2,1,0:T(8,128)S(1)}, u32[]{:S(2)}, u32[]{:S(2)}) collective-permute-start(f32[3,32,128]{2,1,0:T(8,128)S(1)} %get-tuple-element.42), channel_id=1, source_target_pairs={{1,0},{2,1},{3,2},{4,3},{5,4},{6,5},{7,6},{8,7},{9,8},{10,9},{11,1... | collective-permute-start | bytes 147464 | tf_op jit(solution)/shard_map/ppermute | solution.py:379
  68.2 6.9 %collective-permute-start.4 = (f32[3,32,128]{2,1,0:T(8,128)S(1)}, f32[3,32,128]{2,1,0:T(8,128)S(1)}, u32[]{:S(2)}, u32[]{:S(2)}) collective-permute-start(f32[3,32,128]{2,1,0:T(8,128)S(1)} %get-tuple-element.42), channel_id=1, source_target_pairs={{0,1},{1,2},{2,3},{3,4},{4,5},{5,6},{6,7},{7,8},{8,9},{9,10},{10,1... | collective-permute-start | bytes 147464 | tf_op jit(solution)/shard_map/ppermute | solution.py:379
  75.3 5.1 %collective-permute-start.6 = (f32[3,32,128]{2,1,0:T(8,128)S(1)}, f32[3,32,128]{2,1,0:T(8,128)S(1)}, u32[]{:S(2)}, u32[]{:S(2)}) collective-permute-start(f32[3,32,128]{2,1,0:T(8,128)S(1)} %maximum_maximum_fusion), channel_id=1, source_target_pairs={{0,16},{16,32},{32,48},{48,64},{64,80},{80,96},{96,112},{112,128},... | collective-permute-start | bytes 147464 | tf_op jit(solution)/shard_map/ppermute | solution.py:379
  78.5 6.6 %collective-permute-start.7 = (f32[3,32,128]{2,1,0:T(8,128)S(1)}, f32[3,32,128]{2,1,0:T(8,128)S(1)}, u32[]{:S(2)}, u32[]{:S(2)}) collective-permute-start(f32[3,32,128]{2,1,0:T(8,128)S(1)} %maximum_maximum_fusion), channel_id=1, source_target_pairs={{16,0},{32,16},{48,32},{64,48},{80,64},{96,80},{112,96},{128,112},... | collective-permute-start | bytes 147464 | tf_op jit(solution)/shard_map/ppermute | solution.py:379

commit v2 on v1

--- a/solution.py
+++ b/solution.py
@@ -184,7 +184,7 @@
     over_rows(0, SIZE, 2, body)
 
 
-def unpack_kernel(own, before, after, middle, top, bottom):
+def unpack_kernel(edges, own, before, after, middle, top, bottom):
     def widened(row):
         lane = iota(1)
         at = pl.ds(row, 8)
@@ -203,10 +203,10 @@
             roll(m[2], 96, 1),
         )
         for i in range(4):
-            yield i, 0, jnp.where(lane < 32, 0.0, left[i])
+            yield i, 0, jnp.where(lane < edges[0], 0.0, left[i])
             yield i, 1, own[i, 0, at, :]
             yield i, 2, own[i, 1, at, :]
-            yield i, 3, jnp.where(lane < 96, right[i], 0.0)
+            yield i, 3, jnp.where(lane < edges[1], right[i], 0.0)
 
     def part(target, shift):
         def body(row):
@@ -230,7 +230,7 @@
     return (FRAME >> depth) + 2 * PAD
 
 
-def down_kernel(middle, above, below, *refs):
+def down_kernel(edges, middle, above, below, *refs):
     kept, message, refs = refs[0:24], refs[24], refs[25:]
     levels = [dict(zip(KEPT, kept))]
     levels[0].update(zip("ksud", refs[:4]))
@@ -246,10 +246,12 @@
         clear_rows([level[n] for n in "ksbvuweon"], (PAD + first - 8, PAD + last))
 
     def fill(row):
+        lane = iota(1)
         for i in range(4):
             for t in range(4):
-                frame[i][t, pl.ds(PAD + 32 + row, 8), :] = above[i, t, pl.ds(row, 8), :]
-                frame[i][t, pl.ds(PAD + 384 + row, 8), :] = below[i, t, pl.ds(row, 8), :]
+                at = pl.ds(row, 8)
+                frame[i][t, pl.ds(PAD + 32 + row, 8), :] = jnp.where(lane < edges[2], above[i, t, at, :], 0.0)
+                frame[i][t, pl.ds(PAD + 384 + row, 8), :] = jnp.where(lane < edges[3], below[i, t, at, :], 0.0)
 
     over_rows(0, HALO, 1, fill)
 
@@ -365,6 +367,7 @@
 
 
 HERE = pl.BlockSpec(memory_space=pltpu.VMEM)
+SCALARS = pl.BlockSpec(memory_space=pltpu.SMEM)
 AWAY = pl.BlockSpec(memory_space=pltpu.HBM)
 
 
@@ -374,13 +377,16 @@
 
 def exchange(up_block, down_block, axis):
     count = lax.axis_size(axis)
-    up = [(i, i + 1) for i in range(count - 1)]
-    down = [(i + 1, i) for i in range(count - 1)]
+    up = [(i, (i + 1) % count) for i in range(count)]
+    down = [(j, i) for i, j in up]
     return lax.ppermute(up_block, axis, up), lax.ppermute(down_block, axis, down)
 
 
 def per_device(pressure, source, conductivity, storage):
     blocks = (conductivity, storage, source, pressure)
+    x, y = lax.axis_index("gx"), lax.axis_index("gy")
+    inside = (y > 0, y < lax.axis_size("gy") - 1, x > 0, x < lax.axis_size("gx") - 1)
+    edges = jnp.stack([jnp.where(here, some, none) for here, some, none in zip(inside, (32, 96, 128, 128), (128, 0, 0, 0))])
     own, low, high = pl.pallas_call(
         pack_kernel,
         out_shape=(shape_of(4, 2, SIZE, LANES), shape_of(3, SIZE, LANES), shape_of(3, SIZE, LANES)),
@@ -388,18 +394,18 @@
         out_specs=(HERE,) * 3,
         scratch_shapes=[pltpu.SemaphoreType.DMA((8,))],
         cost_estimate=cost(2 * MIB, 2 * MIB),
-        compiler_params=pltpu.CompilerParams(vmem_limit_bytes=8 * MIB),
-    )(*blocks)
+        compiler_params=pltpu.CompilerParams(vmem_limit_bytes=2 * MIB),
+    )(*[pltpu.with_memory_space_constraint(block, pltpu.HBM) for block in blocks])
     before, after = exchange(high, low, "gy")
 
     middle, top, bottom = pl.pallas_call(
         unpack_kernel,
         out_shape=(shape_of(4, 4, SIZE, LANES), shape_of(4, 4, HALO, LANES), shape_of(4, 4, HALO, LANES)),
-        in_specs=[HERE] * 3,
+        in_specs=[SCALARS] + [HERE] * 3,
         out_specs=(HERE,) * 3,
         cost_estimate=cost(4 * MIB, 4 * MIB),
-        compiler_params=pltpu.CompilerParams(vmem_limit_bytes=16 * MIB),
-    )(own, before, after)
+        compiler_params=pltpu.CompilerParams(vmem_limit_bytes=2 * MIB),
+    )(edges, own, before, after)
     above, below = exchange(bottom, top, "gx")
 
     levels = [(4, frame_rows(depth), LANES) for depth in range(4)]
@@ -410,21 +416,23 @@
             *[shape_of(*shape) for shape in kept],
             shape_of(3, 32, LANES),
         ),
-        in_specs=[HERE] * 3,
+        in_specs=[SCALARS] + [HERE] * 3,
         out_specs=(HERE,) * 25,
         scratch_shapes=[
             *[vmem(*shape) for shape in levels for _ in range(4)],
             vmem(3, 4, 32 + 2 * PAD, LANES),
         ],
         cost_estimate=cost(40 * MIB, 12 * MIB),
-        compiler_params=pltpu.CompilerParams(vmem_limit_bytes=40 * MIB),
-    )(middle, above, below)
+        compiler_params=pltpu.CompilerParams(vmem_limit_bytes=11 * MIB),
+    )(edges, middle, above, below)
 
     left, right = exchange(message, message, "gy")
+    left, right = jnp.where(inside[0], left, 0.0), jnp.where(inside[1], right, 0.0)
     wide = jnp.concatenate(
         [left[:, :, 0:20], message[:, :, 4:28], right[:, :, 12:32], jnp.zeros((3, 32, 64), jnp.float32)], axis=2
     )
     upper, lower = exchange(wide, wide, "gx")
+    upper, lower = jnp.where(inside[2], upper, 0.0), jnp.where(inside[3], lower, 0.0)
     merged = jnp.concatenate([upper[:, 0:20], wide[:, 4:28], lower[:, 12:32]], axis=1)
 
     return pl.pallas_call(
@@ -439,7 +447,7 @@
             vmem(4, 32, LANES),
         ],
         cost_estimate=cost(40 * MIB, 12 * MIB),
-        compiler_params=pltpu.CompilerParams(vmem_limit_bytes=40 * MIB),
+        compiler_params=pltpu.CompilerParams(vmem_limit_bytes=5 * MIB),
     )(merged, *kept)
 
 

time: 94.6 us -> 74.1 us (0.78)
  the two profiles are of different devices: /device:TPU:99 before, /device:TPU:97 now
where the time goes in v2:
time: 74.1 us; the launch traced here: 73.8 us
  Pallas kernels  30.9 us (42%)
  waiting for transfers between devices  27.2 us (37%)
  starting transfers between devices  15.2 us (21%)
    ppermute x4, waiting for transfers between devices, exchange(): lax.ppermute(up_block, axis, up)  19.9 us
    pallas_call x1, Pallas kernels, per_device(): pl.pallas_call(down_kernel, out_shape=(*[shape_of(*shape) for shape in ke...  16 us
    pallas_call x1, Pallas kernels, per_device(): pl.pallas_call(up_kernel, out_shape=shape_of(SIZE, SIZE), in_specs=[HERE]...  9.1 us
    ppermute x4, starting transfers between devices, exchange(): lax.ppermute(down_block, axis, down)  8.61 us
    ppermute x4, waiting for transfers between devices, exchange(): lax.ppermute(down_block, axis, down)  7.24 us
    ppermute x4, starting transfers between devices, exchange(): lax.ppermute(up_block, axis, up)  6.59 us
    pallas_call x1, Pallas kernels, per_device(): pl.pallas_call(unpack_kernel, out_shape=(shape_of(4, 4, SIZE, LANES), sha...  3.15 us
    pallas_call x1, Pallas kernels, per_device(): pl.pallas_call(pack_kernel, out_shape=(shape_of(4, 2, SIZE, LANES), shape...  2.65 us
  transfers between devices with their start and end apart: 8, of which 6 were waited for; matrix products, arithmetic and copies ran while one was open for 0% of the time, Pallas kernels for 0%

profile of v2, /device:TPU:97, one launch (start us, length us, event | category | flops | bytes accessed | tf_op | source)
XLA Modules:
  0.0 73.8 jit_solution(11237940342167069213)
XLA Ops:
  0.0 2.6 %shard_map.46 = (f32[4,2,256,128]{3,2,1,0:T(8,128)S(1)}, f32[3,256,128]{2,1,0:T(8,128)S(1)}, f32[3,256,128]{2,1,0:T(8,128)S(1)}) custom-call(f32[256,256]{1,0:T(8,128)} %k.1, f32[256,256]{1,0:T(8,128)} %s.1, f32[256,256]{1,0:T(8,128)} %b.1, f32[256,256]{1,0:T(8,128)} %v.1), custom_call_target="tpu_custom_call" | custom-call | flops 2097152 | bytes 2097152 | tf_op jit(solution)/shard_map/pallas_call | solution.py:390
  2.7 1.4 %collective-permute-start = (f32[3,256,128]{2,1,0:T(8,128)S(1)}, f32[3,256,128]{2,1,0:T(8,128)S(1)}, u32[]{:S(2)}, u32[]{:S(2)}) collective-permute-start(f32[3,256,128]{2,1,0:T(8,128)S(1)} %get-tuple-element.37), channel_id=1, source_target_pairs={{0,1},{1,2},{2,3},{3,4},{4,5},{5,6},{6,7},{7,8},{8,9},{9,10},{10,1... | collective-permute-start | bytes 1179656 | tf_op jit(solution)/shard_map/ppermute | solution.py:382
  4.0 3.7 %collective-permute-start.1 = (f32[3,256,128]{2,1,0:T(8,128)S(1)}, f32[3,256,128]{2,1,0:T(8,128)S(1)}, u32[]{:S(2)}, u32[]{:S(2)}) collective-permute-start(f32[3,256,128]{2,1,0:T(8,128)S(1)} %get-tuple-element.38), channel_id=1, source_target_pairs={{1,0},{2,1},{3,2},{4,3},{5,4},{6,5},{7,6},{8,7},{9,8},{10,9},{11,1... | collective-permute-start | bytes 1179656 | tf_op jit(solution)/shard_map/ppermute | solution.py:382
  7.7 0.1 pad_add_fusion.edges
  7.8 8.5 %collective-permute-done.before = f32[3,256,128]{2,1,0:T(8,128)S(1)} collective-permute-done((f32[3,256,128]{2,1,0:T(8,128)S(1)}, f32[3,256,128]{2,1,0:T(8,128)S(1)}, u32[]{:S(2)}, u32[]{:S(2)}) %collective-permute-start) | collective-permute-done | bytes 393248 | tf_op jit(solution)/shard_map/ppermute | solution.py:382
  16.3 0.0 collective-permute-done.1.after
  16.4 3.2 %shard_map.47 = (f32[4,4,256,128]{3,2,1,0:T(8,128)S(1)}, f32[4,4,96,128]{3,2,1,0:T(8,128)S(1)}, f32[4,4,96,128]{3,2,1,0:T(8,128)S(1)}) custom-call(s32[4]{0:T(128)S(1)} %pad_add_fusion.edges, f32[4,2,256,128]{3,2,1,0:T(8,128)S(1)} %get-tuple-element.36.own, f32[3,256,128]{2,1,0:T(8,128)S(1)} %collective-permute-done.before, ...), custom_call_target="tpu_custom_call" | custom-call | flops 4194304 | bytes 4194304 | tf_op jit(solution)/shard_map/pallas_call | solution.py:401
  19.5 4.1 %collective-permute-start.2 = (f32[4,4,96,128]{3,2,1,0:T(8,128)S(1)}, f32[4,4,96,128]{3,2,1,0:T(8,128)S(1)}, u32[]{:S(2)}, u32[]{:S(2)}) collective-permute-start(f32[4,4,96,128]{3,2,1,0:T(8,128)S(1)} %get-tuple-element.40), channel_id=1, source_target_pairs={{0,16},{16,32},{32,48},{48,64},{64,80},{80,96},{96,112},{112,128},... | collective-permute-start | bytes 2359304 | tf_op jit(solution)/shard_map/ppermute | solution.py:382
  23.6 0.0 collective-permute-start.3
  23.6 8.9 %collective-permute-done.2.above = f32[4,4,96,128]{3,2,1,0:T(8,128)S(1)} collective-permute-done((f32[4,4,96,128]{3,2,1,0:T(8,128)S(1)}, f32[4,4,96,128]{3,2,1,0:T(8,128)S(1)}, u32[]{:S(2)}, u32[]{:S(2)}) %collective-permute-start.2) | collective-permute-done | bytes 786464 | tf_op jit(solution)/shard_map/ppermute | solution.py:382
  32.6 3.7 %collective-permute-done.3.below = f32[4,4,96,128]{3,2,1,0:T(8,128)S(1)} collective-permute-done((f32[4,4,96,128]{3,2,1,0:T(8,128)S(1)}, f32[4,4,96,128]{3,2,1,0:T(8,128)S(1)}, u32[]{:S(2)}, u32[]{:S(2)}) %collective-permute-start.3) | collective-permute-done | bytes 786464 | tf_op jit(solution)/shard_map/ppermute | solution.py:382
  36.3 16.0 %shard_map.48 = (f32[4,528,128]{2,1,0:T(8,128)S(1)}, f32[4,528,128]{2,1,0:T(8,128)S(1)}, f32[4,528,128]{2,1,0:T(8,128)S(1)}, f32[4,528,128]{2,1,0:T(8,128)S(1)},...) custom-call(s32[4]{0:T(128)S(1)} %pad_add_fusion.edges, ...), custom_call_target="tpu_custom_call" | custom-call | flops 41943040 | bytes 12582912 | tf_op jit(solution)/shard_map/pallas_call | solution.py:413
  52.3 0.0 collective-permute-start.4
  52.3 0.1 pad.6.clone
  52.4 4.9 %collective-permute-start.5 = (f32[3,32,128]{2,1,0:T(8,128)S(1)}, f32[3,32,128]{2,1,0:T(8,128)S(1)}, u32[]{:S(2)}, u32[]{:S(2)}) collective-permute-start(f32[3,32,128]{2,1,0:T(8,128)S(1)} %get-tuple-element.42), channel_id=1, source_target_pairs={{1,0},{2,1},{3,2},{4,3},{5,4},{6,5},{7,6},{8,7},{9,8},{10,9},{11,1... | collective-permute-start | bytes 147464 | tf_op jit(solution)/shard_map/ppermute | solution.py:382
  57.3 0.1 slice.19
  57.3 1.3 %collective-permute-done.4 = f32[3,32,128]{2,1,0:T(8,128)S(1)} collective-permute-done((f32[3,32,128]{2,1,0:T(8,128)S(1)}, f32[3,32,128]{2,1,0:T(8,128)S(1)}, u32[]{:S(2)}, u32[]{:S(2)}) %collective-permute-start.4) | collective-permute-done | bytes 49184 | tf_op jit(solution)/shard_map/ppermute | solution.py:382
  58.7 0.0 collective-permute-done.5
  58.7 0.1 slice_select_fusion
  58.7 0.1 maximum_maximum_fusion
  58.8 1.1 %collective-permute-start.6 = (f32[3,32,128]{2,1,0:T(8,128)S(1)}, f32[3,32,128]{2,1,0:T(8,128)S(1)}, u32[]{:S(2)}, u32[]{:S(2)}) collective-permute-start(f32[3,32,128]{2,1,0:T(8,128)S(1)} %maximum_maximum_fusion), channel_id=1, source_target_pairs={{0,16},{16,32},{32,48},{48,64},{64,80},{80,96},{96,112},{112,128},... | collective-permute-start | bytes 147464 | tf_op jit(solution)/shard_map/ppermute | solution.py:382
  59.9 0.0 collective-permute-start.7
  59.9 1.2 %collective-permute-done.6 = f32[3,32,128]{2,1,0:T(8,128)S(1)} collective-permute-done((f32[3,32,128]{2,1,0:T(8,128)S(1)}, f32[3,32,128]{2,1,0:T(8,128)S(1)}, u32[]{:S(2)}, u32[]{:S(2)}) %collective-permute-start.6) | collective-permute-done | bytes 49184 | tf_op jit(solution)/shard_map/ppermute | solution.py:382
  61.1 3.5 %collective-permute-done.7 = f32[3,32,128]{2,1,0:T(8,128)S(1)} collective-permute-done((f32[3,32,128]{2,1,0:T(8,128)S(1)}, f32[3,32,128]{2,1,0:T(8,128)S(1)}, u32[]{:S(2)}, u32[]{:S(2)}) %collective-permute-start.7) | collective-permute-done | bytes 49184 | tf_op jit(solution)/shard_map/ppermute | solution.py:382
  64.7 9.1 %shard_map.49 = f32[256,256]{1,0:T(8,128)} custom-call(f32[3,64,128]{2,1,0:T(8,128)S(1)} %pad_maximum_fusion.merged, f32[4,528,128]{2,1,0:T(8,128)S(1)} %get-tuple-element.43.refs_0_, f32[4,528,128]{2,1,0:T(8,128)S(1)} %get-tuple-element.44.refs_1_, f32[4,528,128]{2,1,0:T(8,128)S(1)} %get-tuple-element.45.refs_2_, ...), custom_call_target="tpu_custom_call" | custom-call | flops 41943040 | bytes 12582912 | tf_op jit(solution)/shard_map/pallas_call | solution.py:438
  (6 shorter events, 0.0 us)
Async XLA Ops:
  2.7 13.7 %collective-permute-start = (f32[3,256,128]{2,1,0:T(8,128)S(1)}, f32[3,256,128]{2,1,0:T(8,128)S(1)}, u32[]{:S(2)}, u32[]{:S(2)}) collective-permute-start(f32[3,256,128]{2,1,0:T(8,128)S(1)} %get-tuple-element.37), channel_id=1, source_target_pairs={{0,1},{1,2},{2,3},{3,4},{4,5},{5,6},{6,7},{7,8},{8,9},{9,10},{10,1... | collective-permute-start | bytes 1179656 | tf_op jit(solution)/shard_map/ppermute | solution.py:382
  4.0 12.3 %collective-permute-start.1 = (f32[3,256,128]{2,1,0:T(8,128)S(1)}, f32[3,256,128]{2,1,0:T(8,128)S(1)}, u32[]{:S(2)}, u32[]{:S(2)}) collective-permute-start(f32[3,256,128]{2,1,0:T(8,128)S(1)} %get-tuple-element.38), channel_id=1, source_target_pairs={{1,0},{2,1},{3,2},{4,3},{5,4},{6,5},{7,6},{8,7},{9,8},{10,9},{11,1... | collective-permute-start | bytes 1179656 | tf_op jit(solution)/shard_map/ppermute | solution.py:382
  19.5 13.1 %collective-permute-start.2 = (f32[4,4,96,128]{3,2,1,0:T(8,128)S(1)}, f32[4,4,96,128]{3,2,1,0:T(8,128)S(1)}, u32[]{:S(2)}, u32[]{:S(2)}) collective-permute-start(f32[4,4,96,128]{3,2,1,0:T(8,128)S(1)} %get-tuple-element.40), channel_id=1, source_target_pairs={{0,16},{16,32},{32,48},{48,64},{64,80},{80,96},{96,112},{112,128},... | collective-permute-start | bytes 2359304 | tf_op jit(solution)/shard_map/ppermute | solution.py:382
  23.6 12.6 %collective-permute-start.3 = (f32[4,4,96,128]{3,2,1,0:T(8,128)S(1)}, f32[4,4,96,128]{3,2,1,0:T(8,128)S(1)}, u32[]{:S(2)}, u32[]{:S(2)}) collective-permute-start(f32[4,4,96,128]{3,2,1,0:T(8,128)S(1)} %get-tuple-element.41), channel_id=1, source_target_pairs={{16,0},{32,16},{48,32},{64,48},{80,64},{96,80},{112,96},{128,112},... | collective-permute-start | bytes 2359304 | tf_op jit(solution)/shard_map/ppermute | solution.py:382
  52.3 6.3 %collective-permute-start.4 = (f32[3,32,128]{2,1,0:T(8,128)S(1)}, f32[3,32,128]{2,1,0:T(8,128)S(1)}, u32[]{:S(2)}, u32[]{:S(2)}) collective-permute-start(f32[3,32,128]{2,1,0:T(8,128)S(1)} %get-tuple-element.42), channel_id=1, source_target_pairs={{0,1},{1,2},{2,3},{3,4},{4,5},{5,6},{6,7},{7,8},{8,9},{9,10},{10,1... | collective-permute-start | bytes 147464 | tf_op jit(solution)/shard_map/ppermute | solution.py:382
  52.4 6.3 %collective-permute-start.5 = (f32[3,32,128]{2,1,0:T(8,128)S(1)}, f32[3,32,128]{2,1,0:T(8,128)S(1)}, u32[]{:S(2)}, u32[]{:S(2)}) collective-permute-start(f32[3,32,128]{2,1,0:T(8,128)S(1)} %get-tuple-element.42), channel_id=1, source_target_pairs={{1,0},{2,1},{3,2},{4,3},{5,4},{6,5},{7,6},{8,7},{9,8},{10,9},{11,1... | collective-permute-start | bytes 147464 | tf_op jit(solution)/shard_map/ppermute | solution.py:382
  58.8 2.3 %collective-permute-start.6 = (f32[3,32,128]{2,1,0:T(8,128)S(1)}, f32[3,32,128]{2,1,0:T(8,128)S(1)}, u32[]{:S(2)}, u32[]{:S(2)}) collective-permute-start(f32[3,32,128]{2,1,0:T(8,128)S(1)} %maximum_maximum_fusion), channel_id=1, source_target_pairs={{0,16},{16,32},{32,48},{48,64},{64,80},{80,96},{96,112},{112,128},... | collective-permute-start | bytes 147464 | tf_op jit(solution)/shard_map/ppermute | solution.py:382
  59.9 4.7 %collective-permute-start.7 = (f32[3,32,128]{2,1,0:T(8,128)S(1)}, f32[3,32,128]{2,1,0:T(8,128)S(1)}, u32[]{:S(2)}, u32[]{:S(2)}) collective-permute-start(f32[3,32,128]{2,1,0:T(8,128)S(1)} %maximum_maximum_fusion), channel_id=1, source_target_pairs={{16,0},{32,16},{48,32},{64,48},{80,64},{96,80},{112,96},{128,112},... | collective-permute-start | bytes 147464 | tf_op jit(solution)/shard_map/ppermute | solution.py:382

commit v3 on v2

v3 whole, which is shorter than its diff:
```python
import jax
import jax.numpy as jnp
from jax import lax
from jax.experimental import pallas as pl
from jax.experimental.pallas import tpu as pltpu
from jax.sharding import PartitionSpec as P

OMEGA = 0.8
COARSE_SWEEPS = 8
SIZE = 256
HALO = 16
RIM = 24
PAD = 8
LANES = 128
MIB = 1 << 20


def iota(axis):
    return lax.broadcasted_iota(jnp.int32, (8, LANES), axis)


def roll(x, amount, axis):
    return pltpu.roll(x, amount % x.shape[axis], axis)


def row_shift(tiles):
    row = iota(0)
    down = [roll(x, 1, 0) for x in tiles[:-1]]
    up = [roll(x, -1, 0) for x in tiles[1:]]
    before = [jnp.where(row == 0, down[j], down[j + 1]) for j in range(len(down) - 1)]
    after = [jnp.where(row == 7, up[j + 1], up[j]) for j in range(len(up) - 1)]
    return before, after


def lane_shift(tiles, step):
    lane = iota(1)
    right = [roll(x, step, 1) for x in tiles]
    left = [roll(x, -step, 1) for x in tiles]
    count = len(tiles)
    before = [jnp.where(lane < step, right[t - 1], right[t]) for t in range(count)]
    after = [jnp.where(lane >= LANES - step, left[(t + 1) % count], left[t]) for t in range(count)]
    return before, after


def around(ref, row, depth, step):
    count = ref.shape[0]
    rows = [[ref[t, pl.ds(row + 8 * j - 8, 8), :] for j in range(depth + 2)] for t in range(count)]
    west, east = zip(*[row_shift(tiles) for tiles in rows])
    cells = {}
    for j in range(depth):
        here = [rows[t][j + 1] for t in range(count)]
        south, north = lane_shift(here, step)
        for t in range(count):
            cells[t, j] = (here[t], west[t][j], east[t][j], south[t], north[t])
    return cells


def over_rows(first, last, depth, body):
    trips = (last - first) // (8 * depth)

    def trip(i, carry):
        body(pl.multiple_of(first + i * 8 * depth, 8))
        return carry

    lax.fori_loop(0, trips, trip, 0)


def rows_at(row, j):
    return pl.ds(row + 8 * j, 8)


def face_pass(level, first, last, depth, guess=None):
    def body(row):
        cells = None if guess is None else around(guess, row, depth, level["step"])
        for (t, j), (k, kw, ke, ks, kn) in around(level["k"], row, depth, level["step"]).items():
            at = rows_at(row, j)
            west, east, south, north = (0.5 * (k + other) for other in (kw, ke, ks, kn))
            stored = level["s"][t, at, :]
            diagonal = (((stored + west) + east) + south) + north
            scale = jnp.where(stored > 0.0, OMEGA / diagonal, 0.0)
            level["d"][t, at, :] = diagonal
            side = scale * level["b"][t, at, :]
            level["b"][t, at, :] = side
            weights = [scale * face for face in (west, east, south, north)]
            for name, weight in zip("weon", weights):
                level[name][t, at, :] = weight
            if cells:
                v, *others = cells[t, j]
                side = side + (1.0 - OMEGA) * v
                for weight, other in zip(weights, others):
                    side = side + weight * other
            level["u"][t, at, :] = side

    over_rows(first, last, depth, body)


def weighted(level, t, at, cell):
    _, vw, ve, vs, vn = cell
    total = level["b"][t, at, :] + level["w"][t, at, :] * vw
    total = total + level["e"][t, at, :] * ve
    total = total + level["o"][t, at, :] * vs
    return total + level["n"][t, at, :] * vn


def sweep_pass(level, source, target, first, last, depth):
    def body(row):
        for (t, j), cell in around(source, row, depth, level["step"]).items():
            at = rows_at(row, j)
            target[t, at, :] = (1.0 - OMEGA) * cell[0] + weighted(level, t, at, cell)

    over_rows(first, last, depth, body)


def residual_pass(level, source, target, first, last, depth):
    def body(row):
        for (t, j), cell in around(source, row, depth, level["step"]).items():
            at = rows_at(row, j)
            gap = (1.0 / OMEGA) * weighted(level, t, at, cell) - cell[0]
            target[t, at, :] = level["d"][t, at, :] * gap

    over_rows(first, last, depth, body)


def pair_sum(source, t, row, step):
    x = source[t, pl.ds(row, 8, stride=2), :] + source[t, pl.ds(row + 1, 8, stride=2), :]
    upper = (iota(1) & step) != 0
    return x + jnp.where(upper, roll(x, step, 1), roll(x, -step, 1))


def coarsen_pass(triples, step, first, last):
    height = 2 if (last - first) % 16 == 0 else 1

    def body(row):
        for j in range(height):
            for source, target, factor in triples:
                for t in range(source.shape[0]):
                    x = pair_sum(source, t, 2 * row + 16 * j + PAD, step)
                    target[t, rows_at(row + PAD, j), :] = x if factor == 1.0 else factor * x

    over_rows(first, last, height, body)


def correct_pass(source, base, target, first, last, shift):
    def body(row):
        for t in range(source.shape[0]):
            x = source[t, pl.ds(row, 8), :]
            for half in range(2):
                at = pl.ds(2 * row - shift + half, 8, stride=2)
                target[t, at, :] = base[t, at, :] + x

    over_rows(first, last, 1, body)


def clear_rows(refs, at):
    for ref in refs:
        for row in at:
            for t in range(ref.shape[0]):
                ref[t, pl.ds(row, 8), :] = jnp.zeros((8, LANES), jnp.float32)


TILES = (3, 3, 1, 1)
ROWS = (320, 160, 112, 56)
PLACE = (32, 16, RIM, RIM // 2)
STEP = (1, 2, 1, 2)
KEPT = "vbweon"


def array_of(depth):
    return (TILES[depth], ROWS[depth] + 2 * PAD, LANES)


def pack_kernel(k, s, b, v, own, low, high, sems):
    copies = []
    for i, a in enumerate((k, s, b, v)):
        for t in range(2):
            copies.append(pltpu.make_async_copy(a.at[:, pl.ds(LANES * t, LANES)], own.at[i, t], sems.at[2 * i + t]))
    for copy in copies:
        copy.start()
    for copy in copies:
        copy.wait()

    def body(row):
        lane = iota(1)
        for target, t, shift in ((low, 0, 0), (high, 1, HALO)):
            parts = []
            for half in range(2):
                for i in range(4):
                    x = own[i, t, pl.ds(row + 128 * half, 8), :]
                    amount = shift + 64 * half + HALO * i
                    parts.append(roll(x, amount, 1) if amount else x)
            total = parts[7]
            for n in range(6, -1, -1):
                total = jnp.where(lane < HALO * (n + 1), parts[n], total)
            target[pl.ds(row, 8), :] = total

    over_rows(0, 128, 1, body)


def widened(edges, own, before, after, row, half):
    lane = iota(1)
    left = before[pl.ds(row - 128 * half, 8), :]
    right = after[pl.ds(row - 128 * half, 8), :]
    for i in range(4):
        x, y = (roll(own[i, t, pl.ds(row, 8), :], 64, 1) for t in range(2))
        start = 64 * half + HALO * i
        low, high = roll(left, 48 - start, 1), roll(right, 64 - start, 1)
        low = jnp.where(lane < 64 - HALO * edges[0], 0.0, low)
        high = jnp.where(lane < 64 + HALO * edges[1], high, 0.0)
        yield i, 0, jnp.where(lane < 64, low, x)
        yield i, 1, jnp.where(lane < 64, x, y)
        yield i, 2, jnp.where(lane < 64, y, high)


def edge_kernel(edges, own, before, after, top, bottom):
    for j in range(HALO // 8):
        for target, row, half in ((top, 8 * j, 0), (bottom, SIZE - HALO + 8 * j, 1)):
            for i, t, x in widened(edges, own, before, after, row, half):
                target[i, t, pl.ds(8 * j, 8), :] = x


def pick(rule):
    shape = (LANES, LANES)
    rows = lax.broadcasted_iota(jnp.int32, shape, 0)
    columns = lax.broadcasted_iota(jnp.int32, shape, 1)
    return rule(rows, columns).astype(jnp.float32)


def choose(x, chooser):
    return jnp.dot(x, chooser, precision=lax.Precision.HIGHEST, preferred_element_type=jnp.float32)


def smooth_down(level, first, last, height, guess=None):
    face_pass(level, PAD + first, PAD + last, height, guess)
    sweep_pass(level, level["u"], level["v"], PAD + first, PAD + last, height)
    residual_pass(level, level["v"], level["u"], PAD + first, PAD + last, height)


def coarsen_into(level, goals, first, last):
    triples = tuple(zip((level["k"], level["s"], level["u"]), goals, (0.5, 1.0, 1.0)))
    coarsen_pass(triples, level["step"], first, last)


def named_levels(depths, kept, scratch):
    levels = []
    for n, depth in enumerate(depths):
        level = dict(zip(KEPT, kept[6 * n : 6 * n + 6]), step=STEP[depth])
        level.update(zip("ksud", scratch[4 * n : 4 * n + 4]))
        levels.append(level)
    return levels


def fine_kernel(edges, own, before, after, above, below, *refs):
    kept, own2, low2, high2, refs = refs[0:12], refs[12], refs[13], refs[14], refs[15:]
    zero, one = named_levels((0, 1), kept, refs)
    two = refs[8]
    clear_rows([zero[n] for n in "ksbvuweon"], (PAD + 8, PAD + 304))
    clear_rows([one[n] for n in "ksbvuweon"], (PAD, PAD + 152))
    frame = [zero[n] for n in "ksbv"]

    for half in range(2):

        def fill(row):
            for i, t, x in widened(edges, own, before, after, row, half):
                frame[i][t, pl.ds(PAD + 32 + row, 8), :] = x

        over_rows(128 * half, 128 * half + 128, 1, fill)
    lane = iota(1)
    for i in range(4):
        for t in range(3):
            for j in range(HALO // 8):
                at = pl.ds(8 * j, 8)
                up = jnp.where(lane < LANES * edges[2], above[i, t, at, :], 0.0)
                down = jnp.where(lane < LANES * edges[3], below[i, t, at, :], 0.0)
                frame[i][t, pl.ds(PAD + 32 - HALO + 8 * j, 8), :] = up
                frame[i][t, pl.ds(PAD + 32 + SIZE + 8 * j, 8), :] = down

    smooth_down(zero, 16, 304, 4, zero["v"])
    coarsen_into(zero, (one["k"], one["s"], one["b"]), 8, 152)
    smooth_down(one, 8, 152, 6)
    coarsen_into(one, (two.at[0], two.at[1], two.at[2]), 8, 72)

    for i in range(3):
        total = jnp.zeros((64, LANES), jnp.float32)
        for t in range(3):
            chooser = pick(lambda r, c: (r + LANES * t == 64 + 4 * (c - RIM)) & (c >= RIM) & (c < RIM + 64))
            total = total + choose(two[i, t, pl.ds(PAD + 8, 64), :], chooser)
        own2[i, :, :] = total

    def send(row):
        lane = iota(1)
        at = pl.ds(row, 8)
        x = [own2[i, at, :] for i in range(3)]
        for target, start in ((low2, RIM), (high2, 64)):
            y = [roll(x[i], RIM * i - start, 1) for i in range(3)]
            target[at, :] = jnp.where(lane < RIM, y[0], jnp.where(lane < 2 * RIM, y[1], y[2]))

    over_rows(0, 64, 1, send)


def join_kernel(edges, own2, left, right, wide, top, bottom):
    lane = iota(1)
    stop = RIM + 64
    for j in range(8):
        at = pl.ds(8 * j, 8)
        for i in range(3):
            low = roll(left[at, :], -RIM * i, 1)
            high = roll(right[at, :], stop - RIM * i, 1)
            x = jnp.where(lane < RIM * edges[0], low, own2[i, at, :])
            x = jnp.where((lane >= stop) & (lane < stop + RIM * edges[1]), high, x)
            wide[i, at, :] = x
            if 8 * j < RIM:
                top[i, at, :] = x
            if 8 * j >= 64 - RIM:
                bottom[i, pl.ds(8 * j - 64 + RIM, 8), :] = x


def middle_kernel(edges, wide, above, below, *refs):
    kept, message, refs = refs[0:12], refs[12], refs[13:]
    two, three = named_levels((2, 3), kept, refs)
    four = refs[8]
    clear_rows([two[n] for n in "ksbvuweon"], (0, PAD + 112))
    clear_rows([three[n] for n in "ksbvuweon"], (0, PAD + 56))
    lane = iota(1)
    for i, name in enumerate("ksb"):
        for j in range(RIM // 8):
            at = pl.ds(8 * j, 8)
            up = jnp.where(lane < LANES * edges[2], above[i, at, :], 0.0)
            down = jnp.where(lane < LANES * edges[3], below[i, at, :], 0.0)
            two[name][0, pl.ds(PAD + 8 * j, 8), :] = up
            two[name][0, pl.ds(PAD + RIM + 64 + 8 * j, 8), :] = down
        two[name][0, pl.ds(PAD + RIM, 64), :] = wide[i]
    smooth_down(two, 0, 112, 7)
    coarsen_into(two, (three["k"], three["s"], three["b"]), 0, 56)
    smooth_down(three, 0, 56, 7)
    coarsen_into(three, (four.at[0], four.at[1], four.at[2]), 0, 32)
    chooser = pick(lambda r, c: (r == 4 * c) & (c < 28))
    for i in range(3):
        message[i, :, :] = choose(four[i, 0, pl.ds(PAD, 32), :], chooser)


def coarse_join_kernel(edges, message, left, right, wide):
    lane = iota(1)
    for i in range(3):
        for j in range(4):
            at = pl.ds(8 * j, 8)
            low, x, high = roll(left[i, at, :], 2, 1), roll(message[i, at, :], 18, 1), roll(right[i, at, :], 34, 1)
            low = jnp.where((lane >= 2) & (lane < 20 * edges[0]), low, 0.0)
            high = jnp.where(lane < 44 + 18 * edges[1], high, 0.0)
            wide[i, at, :] = jnp.where(lane < 20, low, jnp.where(lane < 44, x, high))


def up_kernel(edges, wide, upper, lower, *refs):
    kept, out, refs = refs[0:24], refs[24], refs[25:]
    four = dict(zip("ksbvudweon", refs[0:10]), step=1)
    five = dict(zip("ksbvudweon", refs[10:20]), step=2)
    levels = [dict(zip(KEPT, kept[6 * depth : 6 * depth + 6])) for depth in range(4)]
    for depth, level in enumerate(levels):
        level.update(zip("uc", refs[20 + 2 * depth : 22 + 2 * depth]), step=STEP[depth])
    from4, coarse_fine = refs[28:30]

    column = lax.broadcasted_iota(jnp.int32, (32, LANES), 1)
    clear_rows([four[n] for n in "ksb"], (PAD, PAD + 56))
    for i, name in enumerate("ksb"):
        four[name][0, pl.ds(PAD + 2, 18), :] = jnp.where(column < LANES * edges[2], upper[i], 0.0)[0:18]
        four[name][0, pl.ds(PAD + 20, 24), :] = wide[i, 2:26, :]
        four[name][0, pl.ds(PAD + 44, 18), :] = jnp.where(column < LANES * edges[3], lower[i], 0.0)[10:28]
    clear_rows([four[n] for n in "kvu"], (0, PAD + 64))
    clear_rows([five[n] for n in "kvu"], (0, PAD + 32))
    smooth_down(four, 0, 64, 4)
    coarsen_into(four, (five["k"], five["s"], five["b"]), 0, 32)
    face_pass(five, PAD, PAD + 32, 4)
    v, u = five["v"], five["u"]
    for _ in range(COARSE_SWEEPS - 1):
        sweep_pass(five, u, v, PAD, PAD + 32, 4)
        v, u = u, v
    correct_pass(u, four["v"], four["v"], PAD, PAD + 32, PAD)
    sweep_pass(four, four["v"], four["u"], PAD, PAD + 64, 4)
    sweep_pass(four, four["u"], four["v"], PAD, PAD + 64, 4)
    from4[0, :, :] = choose(four["v"][0, pl.ds(PAD + 16, 32), :], pick(lambda r, c: r == c // 4 + 18))

    def rise(depth, coarse, first, last, shift, start, stop, height, twice=True):
        level = levels[depth]
        u, c = level["u"], level["c"]
        correct_pass(coarse, level["v"], c, first, last, shift)
        sweep_pass(level, c, u, start, stop, height)
        if twice:
            clear_rows([u], (start - 8, stop))
            sweep_pass(level, u, c, start, stop, height)
        return c

    c = rise(3, from4, 0, 32, -4, 8, 64, 7)
    c = rise(2, c, 8, 64, 8, 24, 104, 5)
    fine = c[0, pl.ds(24, 80), :]
    for t in range(3):
        coarse_fine[t, :, :] = choose(fine, pick(lambda r, c: r == (c + LANES * t) // 4 + 8))
    c = rise(1, coarse_fine, 0, 80, -8, 16, 160, 6)
    rise(0, c, 16, 160, 8, 32, 304, 2, False)

    level = levels[0]

    def body(row):
        lane = iota(1)
        cells = around(level["u"], row, 2, 1)
        for j in range(2):
            values = []
            for t in range(3):
                value = (1.0 - OMEGA) * cells[t, j][0] + weighted(level, t, rows_at(row, j), cells[t, j])
                values.append(roll(value, 64, 1))
            for t in range(2):
                at = pl.ds(row + 8 * j - PAD - 32, 8)
                out[at, LANES * t : LANES * (t + 1)] = jnp.where(lane < 64, values[t], values[t + 1])

    over_rows(PAD + 32, PAD + 32 + SIZE, 2, body)


def shape_of(*shape):
    return jax.ShapeDtypeStruct(shape, jnp.float32)


def vmem(*shape):
    return pltpu.VMEM(shape, jnp.float32)


HERE = pl.BlockSpec(memory_space=pltpu.VMEM)
SCALARS = pl.BlockSpec(memory_space=pltpu.SMEM)
AWAY = pl.BlockSpec(memory_space=pltpu.HBM)


def cost(flops, count):
    return pl.CostEstimate(flops=flops, bytes_accessed=count, transcendentals=0)


def exchange(up_block, down_block, axis):
    count = lax.axis_size(axis)
    up = [(i, (i + 1) % count) for i in range(count)]
    down = [(j, i) for i, j in up]
    return lax.ppermute(up_block, axis, up), lax.ppermute(down_block, axis, down)


def call(kernel, outs, ins, scratch=(), grant=4):
    return pl.pallas_call(
        kernel,
        out_shape=tuple(shape_of(*shape) for shape in outs),
        in_specs=[SCALARS] + [HERE] * (len(ins) - 1),
        out_specs=(HERE,) * len(outs),
        scratch_shapes=scratch,
        cost_estimate=cost(8 * MIB, 4 * MIB),
        compiler_params=pltpu.CompilerParams(vmem_limit_bytes=grant * MIB),
    )(*ins)


def per_device(pressure, source, conductivity, storage):
    blocks = (conductivity, storage, source, pressure)
    x, y = lax.axis_index("gx"), lax.axis_index("gy")
    inside = (y > 0, y < lax.axis_size("gy") - 1, x > 0, x < lax.axis_size("gx") - 1)
    edges = jnp.stack(inside).astype(jnp.int32)
    own, low, high = pl.pallas_call(
        pack_kernel,
        out_shape=(shape_of(4, 2, SIZE, LANES), shape_of(128, LANES), shape_of(128, LANES)),
        in_specs=[AWAY] * 4,
        out_specs=(HERE,) * 3,
        scratch_shapes=[pltpu.SemaphoreType.DMA((8,))],
        cost_estimate=cost(2 * MIB, 2 * MIB),
        compiler_params=pltpu.CompilerParams(vmem_limit_bytes=2 * MIB),
    )(*[pltpu.with_memory_space_constraint(block, pltpu.HBM) for block in blocks])
    before, after = exchange(high, low, "gy")
    top, bottom = call(edge_kernel, [(4, 3, HALO, LANES)] * 2, (edges, own, before, after))
    above, below = exchange(bottom, top, "gx")

    *kept, own2, low2, high2 = call(
        fine_kernel,
        [array_of(0)] * 6 + [array_of(1)] * 6 + [(3, 64, LANES), (64, LANES), (64, LANES)],
        (edges, own, before, after, above, below),
        [vmem(*array_of(0))] * 4 + [vmem(*array_of(1))] * 4 + [vmem(3, 3, 80 + 2 * PAD, LANES)],
        grant=6,
    )
    left, right = exchange(high2, low2, "gy")
    wide2, top2, bottom2 = call(
        join_kernel, [(3, 64, LANES), (3, RIM, LANES), (3, RIM, LANES)], (edges, own2, left, right)
    )
    above2, below2 = exchange(bottom2, top2, "gx")
    *more, message = call(
        middle_kernel,
        [array_of(2)] * 6 + [array_of(3)] * 6 + [(3, 32, LANES)],
        (edges, wide2, above2, below2),
        [vmem(*array_of(2))] * 4 + [vmem(*array_of(3))] * 4 + [vmem(3, 1, 32 + 2 * PAD, LANES)],
    )

    left, right = exchange(message, message, "gy")
    (wide,) = call(coarse_join_kernel, [(3, 32, LANES)], (edges, message, left, right))
    upper, lower = exchange(wide, wide, "gx")
    return pl.pallas_call(
        up_kernel,
        out_shape=shape_of(SIZE, SIZE),
        in_specs=[SCALARS] + [HERE] * 27,
        out_specs=HERE,
        scratch_shapes=[
            *[vmem(1, 64 + 2 * PAD, LANES)] * 10,
            *[vmem(1, 32 + 2 * PAD, LANES)] * 10,
            *[vmem(*array_of(depth)) for depth in range(4) for _ in range(2)],
            vmem(1, 32, LANES),
            vmem(3, 80, LANES),
        ],
        cost_estimate=cost(40 * MIB, 12 * MIB),
        compiler_params=pltpu.CompilerParams(vmem_limit_bytes=5 * MIB),
    )(edges, wide, upper, lower, *kept, *more)


def solution(mesh):
    placed = (P("gx", "gy"),) * 4
    return jax.shard_map(per_device, mesh=mesh, in_specs=placed, out_specs=P("gx", "gy"), check_vma=False)
```

time: 74.1 us -> 70.4 us (0.950)
  starting transfers between devices: 15.2 us -> 23.7 us
  waiting for transfers between devices: 27.2 us -> 20.6 us
  Pallas kernels: 30.9 us -> 25.9 us
    ppermute x4 -> x6, waiting for transfers between devices: 19.9 us -> 10.5 us  [exchange(): lax.ppermute(up_block, axis, up)]
    ppermute x4 -> x6, starting transfers between devices: 8.61 us -> 14 us  [exchange(): lax.ppermute(down_block, axis, down)]
    pallas_call x3 -> x6, Pallas kernels: 28.3 us -> 23.2 us  [the longest x5 14.4 us: call(): pl.pallas_call(kernel, out_shape=tuple((shape_of(*shape) for shape in out...]
    ppermute x4 -> x6, starting transfers between devices: 6.59 us -> 9.67 us  [exchange(): lax.ppermute(up_block, axis, up)]
    ppermute x4 -> x6, waiting for transfers between devices: 7.24 us -> 10.1 us  [exchange(): lax.ppermute(down_block, axis, down)]
  transfers between devices with their start and end apart: 8 -> 12, of which waited for: 6 -> 9; matrix products, arithmetic and copies ran while one was open for 0% -> 0% of each run, Pallas kernels for 0% -> 0%
where the time goes in v3:
time: 70.4 us; the launch traced here: 70.3 us
  Pallas kernels  25.9 us (37%)
  starting transfers between devices  23.7 us (34%)
  waiting for transfers between devices  20.6 us (29%)
    pallas_call x5, Pallas kernels, call(): pl.pallas_call(kernel, out_shape=tuple((shape_of(*shape) for shape in out...  14.4 us
    ppermute x6, starting transfers between devices, exchange(): lax.ppermute(down_block, axis, down)  14 us
    ppermute x6, waiting for transfers between devices, exchange(): lax.ppermute(up_block, axis, up)  10.5 us
    ppermute x6, waiting for transfers between devices, exchange(): lax.ppermute(down_block, axis, down)  10.1 us
    ppermute x6, starting transfers between devices, exchange(): lax.ppermute(up_block, axis, up)  9.67 us
    pallas_call x1, Pallas kernels, per_device(): pl.pallas_call(up_kernel, out_shape=shape_of(SIZE, SIZE), in_specs=[SCALA...  8.86 us
    pallas_call x1, Pallas kernels, per_device(): pl.pallas_call(pack_kernel, out_shape=(shape_of(4, 2, SIZE, LANES), shape...  2.69 us
  transfers between devices with their start and end apart: 12, of which 9 were waited for; matrix products, arithmetic and copies ran while one was open for 0% of the time, Pallas kernels for 0%

profile of v3, /device:TPU:97, one launch (start us, length us, event | category | flops | bytes accessed | tf_op | source)
XLA Modules:
  0.0 70.3 jit_solution(6396782271221981238)
XLA Ops:
  0.0 2.7 %shard_map.46 = (f32[4,2,256,128]{3,2,1,0:T(8,128)S(1)}, f32[128,128]{1,0:T(8,128)S(1)}, f32[128,128]{1,0:T(8,128)S(1)}) custom-call(f32[256,256]{1,0:T(8,128)} %k.1, f32[256,256]{1,0:T(8,128)} %s.1, f32[256,256]{1,0:T(8,128)} %b.1, f32[256,256]{1,0:T(8,128)} %v.1), custom_call_target="tpu_custom_call" | custom-call | flops 2097152 | bytes 2097152 | tf_op jit(solution)/shard_map/pallas_call | solution.py:457
  2.7 1.4 %collective-permute-start = (f32[128,128]{1,0:T(8,128)S(1)}, f32[128,128]{1,0:T(8,128)S(1)}, u32[]{:S(2)}, u32[]{:S(2)}) collective-permute-start(f32[128,128]{1,0:T(8,128)S(1)} %get-tuple-element.42), channel_id=1, source_target_pairs={{0,1},{1,2},{2,3},{3,4},{4,5},{5,6},{6,7},{7,8},{8,9},{9,10},{10,1... | collective-permute-start | bytes 196616 | tf_op jit(solution)/shard_map/ppermute | solution.py:437
  4.1 3.7 %collective-permute-start.1 = (f32[128,128]{1,0:T(8,128)S(1)}, f32[128,128]{1,0:T(8,128)S(1)}, u32[]{:S(2)}, u32[]{:S(2)}) collective-permute-start(f32[128,128]{1,0:T(8,128)S(1)} %get-tuple-element.43), channel_id=1, source_target_pairs={{1,0},{2,1},{3,2},{4,3},{5,4},{6,5},{7,6},{8,7},{9,8},{10,9},{11,1... | collective-permute-start | bytes 196616 | tf_op jit(solution)/shard_map/ppermute | solution.py:437
  7.8 0.1 add_convert_fusion.edges
  7.9 1.5 %collective-permute-done.before = f32[128,128]{1,0:T(8,128)S(1)} collective-permute-done((f32[128,128]{1,0:T(8,128)S(1)}, f32[128,128]{1,0:T(8,128)S(1)}, u32[]{:S(2)}, u32[]{:S(2)}) %collective-permute-start) | collective-permute-done | bytes 65568 | tf_op jit(solution)/shard_map/ppermute | solution.py:437
  9.4 0.0 collective-permute-done.1.after
  9.4 0.7 shard_map.47
  10.0 4.4 %collective-permute-start.2 = (f32[4,3,16,128]{3,2,1,0:T(8,128)S(1)}, f32[4,3,16,128]{3,2,1,0:T(8,128)S(1)}, u32[]{:S(2)}, u32[]{:S(2)}) collective-permute-start(f32[4,3,16,128]{3,2,1,0:T(8,128)S(1)} %get-tuple-element.44), channel_id=1, source_target_pairs={{0,16},{16,32},{32,48},{48,64},{64,80},{80,96},{96,112},{112,128},... | collective-permute-start | bytes 294920 | tf_op jit(solution)/shard_map/ppermute | solution.py:437
  14.5 0.0 collective-permute-start.3
  14.5 1.6 %collective-permute-done.2.above = f32[4,3,16,128]{3,2,1,0:T(8,128)S(1)} collective-permute-done((f32[4,3,16,128]{3,2,1,0:T(8,128)S(1)}, f32[4,3,16,128]{3,2,1,0:T(8,128)S(1)}, u32[]{:S(2)}, u32[]{:S(2)}) %collective-permute-start.2) | collective-permute-done | bytes 98336 | tf_op jit(solution)/shard_map/ppermute | solution.py:437
  16.1 3.6 %collective-permute-done.3.below = f32[4,3,16,128]{3,2,1,0:T(8,128)S(1)} collective-permute-done((f32[4,3,16,128]{3,2,1,0:T(8,128)S(1)}, f32[4,3,16,128]{3,2,1,0:T(8,128)S(1)}, u32[]{:S(2)}, u32[]{:S(2)}) %collective-permute-start.3) | collective-permute-done | bytes 98336 | tf_op jit(solution)/shard_map/ppermute | solution.py:437
  19.7 10.1 %shard_map.48 = (f32[3,336,128]{2,1,0:T(8,128)S(1)}, f32[3,336,128]{2,1,0:T(8,128)S(1)}, f32[3,336,128]{2,1,0:T(8,128)S(1)}, f32[3,336,128]{2,1,0:T(8,128)S(1)},...) custom-call(s32[4]{0:T(128)S(1)} %add_convert_fusion.edges, ...), custom_call_target="tpu_custom_call" | custom-call | flops 8388608 | bytes 4194304 | tf_op jit(solution)/shard_map/pallas_call | solution.py:441
  29.8 0.0 collective-permute-start.4
  29.8 5.1 %collective-permute-start.5 = (f32[64,128]{1,0:T(8,128)S(1)}, f32[64,128]{1,0:T(8,128)S(1)}, u32[]{:S(2)}, u32[]{:S(2)}) collective-permute-start(f32[64,128]{1,0:T(8,128)S(1)} %get-tuple-element.48), channel_id=1, source_target_pairs={{1,0},{2,1},{3,2},{4,3},{5,4},{6,5},{7,6},{8,7},{9,8},{10,9},{11,1... | collective-permute-start | bytes 98312 | tf_op jit(solution)/shard_map/ppermute | solution.py:437
  35.0 1.2 %collective-permute-done.4.left = f32[64,128]{1,0:T(8,128)S(1)} collective-permute-done((f32[64,128]{1,0:T(8,128)S(1)}, f32[64,128]{1,0:T(8,128)S(1)}, u32[]{:S(2)}, u32[]{:S(2)}) %collective-permute-start.4) | collective-permute-done | bytes 32800 | tf_op jit(solution)/shard_map/ppermute | solution.py:437
  36.2 0.0 collective-permute-done.5.right
  36.2 0.6 shard_map.49
  36.9 0.9 %collective-permute-start.6 = (f32[3,24,128]{2,1,0:T(8,128)S(1)}, f32[3,24,128]{2,1,0:T(8,128)S(1)}, u32[]{:S(2)}, u32[]{:S(2)}) collective-permute-start(f32[3,24,128]{2,1,0:T(8,128)S(1)} %get-tuple-element.50), channel_id=1, source_target_pairs={{0,16},{16,32},{32,48},{48,64},{64,80},{80,96},{96,112},{112,128},... | collective-permute-start | bytes 110600 | tf_op jit(solution)/shard_map/ppermute | solution.py:437
  37.7 0.0 collective-permute-start.7
  37.7 1.1 %collective-permute-done.6.above = f32[3,24,128]{2,1,0:T(8,128)S(1)} collective-permute-done((f32[3,24,128]{2,1,0:T(8,128)S(1)}, f32[3,24,128]{2,1,0:T(8,128)S(1)}, u32[]{:S(2)}, u32[]{:S(2)}) %collective-permute-start.6) | collective-permute-done | bytes 36896 | tf_op jit(solution)/shard_map/ppermute | solution.py:437
  38.8 3.5 %collective-permute-done.7.below = f32[3,24,128]{2,1,0:T(8,128)S(1)} collective-permute-done((f32[3,24,128]{2,1,0:T(8,128)S(1)}, f32[3,24,128]{2,1,0:T(8,128)S(1)}, u32[]{:S(2)}, u32[]{:S(2)}) %collective-permute-start.7) | collective-permute-done | bytes 36896 | tf_op jit(solution)/shard_map/ppermute | solution.py:437
  42.3 2.3 %shard_map.50 = (f32[1,128,128]{2,1,0:T(8,128)S(1)}, f32[1,128,128]{2,1,0:T(8,128)S(1)}, f32[1,128,128]{2,1,0:T(8,128)S(1)}, f32[1,128,128]{2,1,0:T(8,128)S(1)},...) custom-call(s32[4]{0:T(128)S(1)} %add_convert_fusion.edges, ...), custom_call_target="tpu_custom_call" | custom-call | flops 8388608 | bytes 4194304 | tf_op jit(solution)/shard_map/pallas_call | solution.py:441
  44.7 5.2 %collective-permute-start.9 = (f32[3,32,128]{2,1,0:T(8,128)S(1)}, f32[3,32,128]{2,1,0:T(8,128)S(1)}, u32[]{:S(2)}, u32[]{:S(2)}) collective-permute-start(f32[3,32,128]{2,1,0:T(8,128)S(1)} %get-tuple-element.52.message), channel_id=1, source_target_pairs={{1,0},{2,1},{3,2},{4,3},{5,4},{6,5},{7,6},{8,7},{9,8},{10,9},{11,1... | collective-permute-start | bytes 147464 | tf_op jit(solution)/shard_map/ppermute | solution.py:437
  49.8 0.0 collective-permute-start.8
  49.8 1.2 %collective-permute-done.9.right = f32[3,32,128]{2,1,0:T(8,128)S(1)} collective-permute-done((f32[3,32,128]{2,1,0:T(8,128)S(1)}, f32[3,32,128]{2,1,0:T(8,128)S(1)}, u32[]{:S(2)}, u32[]{:S(2)}) %collective-permute-start.9) | collective-permute-done | bytes 49184 | tf_op jit(solution)/shard_map/ppermute | solution.py:437
  51.0 5.1 %collective-permute-done.8.left = f32[3,32,128]{2,1,0:T(8,128)S(1)} collective-permute-done((f32[3,32,128]{2,1,0:T(8,128)S(1)}, f32[3,32,128]{2,1,0:T(8,128)S(1)}, u32[]{:S(2)}, u32[]{:S(2)}) %collective-permute-start.8) | collective-permute-done | bytes 49184 | tf_op jit(solution)/shard_map/ppermute | solution.py:437
  56.1 0.6 shard_map.51.wide
  56.7 0.0 collective-permute-start.11
  56.8 2.9 %collective-permute-start.10 = (f32[3,32,128]{2,1,0:T(8,128)S(1)}, f32[3,32,128]{2,1,0:T(8,128)S(1)}, u32[]{:S(2)}, u32[]{:S(2)}) collective-permute-start(f32[3,32,128]{2,1,0:T(8,128)S(1)} %shard_map.51.wide), channel_id=1, source_target_pairs={{0,16},{16,32},{32,48},{48,64},{64,80},{80,96},{96,112},{112,128},... | collective-permute-start | bytes 147464 | tf_op jit(solution)/shard_map/ppermute | solution.py:437
  59.7 1.8 %collective-permute-done.11.lower = f32[3,32,128]{2,1,0:T(8,128)S(1)} collective-permute-done((f32[3,32,128]{2,1,0:T(8,128)S(1)}, f32[3,32,128]{2,1,0:T(8,128)S(1)}, u32[]{:S(2)}, u32[]{:S(2)}) %collective-permute-start.11) | collective-permute-done | bytes 49184 | tf_op jit(solution)/shard_map/ppermute | solution.py:437
  61.5 0.0 collective-permute-done.10.upper
  61.5 8.9 %shard_map.52 = f32[256,256]{1,0:T(8,128)} custom-call(s32[4]{0:T(128)S(1)} %add_convert_fusion.edges, f32[3,32,128]{2,1,0:T(8,128)S(1)} %shard_map.51.wide, f32[3,32,128]{2,1,0:T(8,128)S(1)} %collective-permute-done.10.upper, f32[3,32,128]{2,1,0:T(8,128)S(1)} %collective-permute-done.11.lower, f32[3,336,128]{2,1,0:T(8,128)S(1)} %get-tuple-element.53.refs_0_, ...), custom_call_target="tpu_custom_call" | custom-call | flops 41943040 | bytes 12582912 | tf_op jit(solution)/shard_map/pallas_call | solution.py:492
Async XLA Ops:
  2.7 6.7 %collective-permute-start = (f32[128,128]{1,0:T(8,128)S(1)}, f32[128,128]{1,0:T(8,128)S(1)}, u32[]{:S(2)}, u32[]{:S(2)}) collective-permute-start(f32[128,128]{1,0:T(8,128)S(1)} %get-tuple-element.42), channel_id=1, source_target_pairs={{0,1},{1,2},{2,3},{3,4},{4,5},{5,6},{6,7},{7,8},{8,9},{9,10},{10,1... | collective-permute-start | bytes 196616 | tf_op jit(solution)/shard_map/ppermute | solution.py:437
  4.1 5.3 %collective-permute-start.1 = (f32[128,128]{1,0:T(8,128)S(1)}, f32[128,128]{1,0:T(8,128)S(1)}, u32[]{:S(2)}, u32[]{:S(2)}) collective-permute-start(f32[128,128]{1,0:T(8,128)S(1)} %get-tuple-element.43), channel_id=1, source_target_pairs={{1,0},{2,1},{3,2},{4,3},{5,4},{6,5},{7,6},{8,7},{9,8},{10,9},{11,1... | collective-permute-start | bytes 196616 | tf_op jit(solution)/shard_map/ppermute | solution.py:437
  10.0 6.1 %collective-permute-start.2 = (f32[4,3,16,128]{3,2,1,0:T(8,128)S(1)}, f32[4,3,16,128]{3,2,1,0:T(8,128)S(1)}, u32[]{:S(2)}, u32[]{:S(2)}) collective-permute-start(f32[4,3,16,128]{3,2,1,0:T(8,128)S(1)} %get-tuple-element.44), channel_id=1, source_target_pairs={{0,16},{16,32},{32,48},{48,64},{64,80},{80,96},{96,112},{112,128},... | collective-permute-start | bytes 294920 | tf_op jit(solution)/shard_map/ppermute | solution.py:437
  14.5 5.3 %collective-permute-start.3 = (f32[4,3,16,128]{3,2,1,0:T(8,128)S(1)}, f32[4,3,16,128]{3,2,1,0:T(8,128)S(1)}, u32[]{:S(2)}, u32[]{:S(2)}) collective-permute-start(f32[4,3,16,128]{3,2,1,0:T(8,128)S(1)} %get-tuple-element.45), channel_id=1, source_target_pairs={{16,0},{32,16},{48,32},{64,48},{80,64},{96,80},{112,96},{128,112},... | collective-permute-start | bytes 294920 | tf_op jit(solution)/shard_map/ppermute | solution.py:437
  29.8 6.4 %collective-permute-start.4 = (f32[64,128]{1,0:T(8,128)S(1)}, f32[64,128]{1,0:T(8,128)S(1)}, u32[]{:S(2)}, u32[]{:S(2)}) collective-permute-start(f32[64,128]{1,0:T(8,128)S(1)} %get-tuple-element.47), channel_id=1, source_target_pairs={{0,1},{1,2},{2,3},{3,4},{4,5},{5,6},{6,7},{7,8},{8,9},{9,10},{10,1... | collective-permute-start | bytes 98312 | tf_op jit(solution)/shard_map/ppermute | solution.py:437
  29.8 6.4 %collective-permute-start.5 = (f32[64,128]{1,0:T(8,128)S(1)}, f32[64,128]{1,0:T(8,128)S(1)}, u32[]{:S(2)}, u32[]{:S(2)}) collective-permute-start(f32[64,128]{1,0:T(8,128)S(1)} %get-tuple-element.48), channel_id=1, source_target_pairs={{1,0},{2,1},{3,2},{4,3},{5,4},{6,5},{7,6},{8,7},{9,8},{10,9},{11,1... | collective-permute-start | bytes 98312 | tf_op jit(solution)/shard_map/ppermute | solution.py:437
  36.9 1.9 %collective-permute-start.6 = (f32[3,24,128]{2,1,0:T(8,128)S(1)}, f32[3,24,128]{2,1,0:T(8,128)S(1)}, u32[]{:S(2)}, u32[]{:S(2)}) collective-permute-start(f32[3,24,128]{2,1,0:T(8,128)S(1)} %get-tuple-element.50), channel_id=1, source_target_pairs={{0,16},{16,32},{32,48},{48,64},{64,80},{80,96},{96,112},{112,128},... | collective-permute-start | bytes 110600 | tf_op jit(solution)/shard_map/ppermute | solution.py:437
  37.7 4.6 %collective-permute-start.7 = (f32[3,24,128]{2,1,0:T(8,128)S(1)}, f32[3,24,128]{2,1,0:T(8,128)S(1)}, u32[]{:S(2)}, u32[]{:S(2)}) collective-permute-start(f32[3,24,128]{2,1,0:T(8,128)S(1)} %get-tuple-element.51), channel_id=1, source_target_pairs={{16,0},{32,16},{48,32},{64,48},{80,64},{96,80},{112,96},{128,112},... | collective-permute-start | bytes 110600 | tf_op jit(solution)/shard_map/ppermute | solution.py:437
  44.7 6.3 %collective-permute-start.9 = (f32[3,32,128]{2,1,0:T(8,128)S(1)}, f32[3,32,128]{2,1,0:T(8,128)S(1)}, u32[]{:S(2)}, u32[]{:S(2)}) collective-permute-start(f32[3,32,128]{2,1,0:T(8,128)S(1)} %get-tuple-element.52.message), channel_id=1, source_target_pairs={{1,0},{2,1},{3,2},{4,3},{5,4},{6,5},{7,6},{8,7},{9,8},{10,9},{11,1... | collective-permute-start | bytes 147464 | tf_op jit(solution)/shard_map/ppermute | solution.py:437
  49.8 6.3 %collective-permute-start.8 = (f32[3,32,128]{2,1,0:T(8,128)S(1)}, f32[3,32,128]{2,1,0:T(8,128)S(1)}, u32[]{:S(2)}, u32[]{:S(2)}) collective-permute-start(f32[3,32,128]{2,1,0:T(8,128)S(1)} %get-tuple-element.52.message), channel_id=1, source_target_pairs={{0,1},{1,2},{2,3},{3,4},{4,5},{5,6},{6,7},{7,8},{8,9},{9,10},{10,1... | collective-permute-start | bytes 147464 | tf_op jit(solution)/shard_map/ppermute | solution.py:437
  56.7 4.7 %collective-permute-start.11 = (f32[3,32,128]{2,1,0:T(8,128)S(1)}, f32[3,32,128]{2,1,0:T(8,128)S(1)}, u32[]{:S(2)}, u32[]{:S(2)}) collective-permute-start(f32[3,32,128]{2,1,0:T(8,128)S(1)} %shard_map.51.wide), channel_id=1, source_target_pairs={{16,0},{32,16},{48,32},{64,48},{80,64},{96,80},{112,96},{128,112},... | collective-permute-start | bytes 147464 | tf_op jit(solution)/shard_map/ppermute | solution.py:437
  56.8 4.7 %collective-permute-start.10 = (f32[3,32,128]{2,1,0:T(8,128)S(1)}, f32[3,32,128]{2,1,0:T(8,128)S(1)}, u32[]{:S(2)}, u32[]{:S(2)}) collective-permute-start(f32[3,32,128]{2,1,0:T(8,128)S(1)} %shard_map.51.wide), channel_id=1, source_target_pairs={{0,16},{16,32},{32,48},{48,64},{64,80},{80,96},{96,112},{112,128},... | collective-permute-start | bytes 147464 | tf_op jit(solution)/shard_map/ppermute | solution.py:437

commit v4 on v3

--- a/solution.py
+++ b/solution.py
@@ -201,14 +201,12 @@
     left = before[pl.ds(row - 128 * half, 8), :]
     right = after[pl.ds(row - 128 * half, 8), :]
     for i in range(4):
-        x, y = (roll(own[i, t, pl.ds(row, 8), :], 64, 1) for t in range(2))
         start = 64 * half + HALO * i
-        low, high = roll(left, 48 - start, 1), roll(right, 64 - start, 1)
-        low = jnp.where(lane < 64 - HALO * edges[0], 0.0, low)
-        high = jnp.where(lane < 64 + HALO * edges[1], high, 0.0)
-        yield i, 0, jnp.where(lane < 64, low, x)
-        yield i, 1, jnp.where(lane < 64, x, y)
-        yield i, 2, jnp.where(lane < 64, y, high)
+        low, high = roll(left, -HALO - start, 1), roll(right, -start, 1)
+        low = jnp.where(lane >= LANES - HALO * edges[0], low, 0.0)
+        yield i, 0, own[i, 0, pl.ds(row, 8), :]
+        yield i, 1, own[i, 1, pl.ds(row, 8), :]
+        yield i, 2, jnp.where(lane < HALO * edges[1], high, low)
 
 
 def edge_kernel(edges, own, before, after, top, bottom):
@@ -222,11 +220,17 @@
     shape = (LANES, LANES)
     rows = lax.broadcasted_iota(jnp.int32, shape, 0)
     columns = lax.broadcasted_iota(jnp.int32, shape, 1)
-    return rule(rows, columns).astype(jnp.float32)
+    return rule(rows, columns).astype(jnp.float32).astype(jnp.bfloat16)
 
 
 def choose(x, chooser):
-    return jnp.dot(x, chooser, precision=lax.Precision.HIGHEST, preferred_element_type=jnp.float32)
+    total = None
+    for _ in range(3):
+        term = x.astype(jnp.bfloat16)
+        part = jnp.dot(term, chooser, preferred_element_type=jnp.float32)
+        total = part if total is None else total + part
+        x = x - term.astype(jnp.float32)
+    return total
 
 
 def smooth_down(level, first, last, height, guess=None):
@@ -249,21 +253,30 @@
     return levels
 
 
-def fine_kernel(edges, own, before, after, above, below, *refs):
-    kept, own2, low2, high2, refs = refs[0:12], refs[12], refs[13], refs[14], refs[15:]
-    zero, one = named_levels((0, 1), kept, refs)
-    two = refs[8]
+ALL = KEPT + "ksud"
+
+
+def start_kernel(edges, own, before, after, *refs):
+    zero = dict(zip(ALL, refs), step=STEP[0])
+    frame = [zero[n] for n in "ksbv"]
+    for half in range(2):
+
+        def fill(row):
+            for i, t, x in widened(edges, own, before, after, row, half):
+                frame[i][t, pl.ds(PAD + 32 + row, 8), :] = x
+
+        over_rows(128 * half, 128 * half + 128, 1, fill)
+    face_pass(zero, PAD + 40, PAD + 280, 5, zero["v"])
+
+
+def fine_kernel(edges, above, below, *refs):
+    started, rest, kept1, own2, low2, high2, refs = refs[10:20], refs[0:10], refs[20:26], *refs[26:29], refs[29:]
+    zero = dict(zip(ALL, started), step=STEP[0])
+    one = dict(zip(ALL, (*kept1, *refs[:4])), step=STEP[1])
+    two = refs[4]
     clear_rows([zero[n] for n in "ksbvuweon"], (PAD + 8, PAD + 304))
     clear_rows([one[n] for n in "ksbvuweon"], (PAD, PAD + 152))
     frame = [zero[n] for n in "ksbv"]
-
-    for half in range(2):
-
-        def fill(row):
-            for i, t, x in widened(edges, own, before, after, row, half):
-                frame[i][t, pl.ds(PAD + 32 + row, 8), :] = x
-
-        over_rows(128 * half, 128 * half + 128, 1, fill)
     lane = iota(1)
     for i in range(4):
         for t in range(3):
@@ -274,17 +287,23 @@
                 frame[i][t, pl.ds(PAD + 32 - HALO + 8 * j, 8), :] = up
                 frame[i][t, pl.ds(PAD + 32 + SIZE + 8 * j, 8), :] = down
 
-    smooth_down(zero, 16, 304, 4, zero["v"])
+    face_pass(zero, PAD + 16, PAD + 40, 3, zero["v"])
+    face_pass(zero, PAD + 280, PAD + 304, 3, zero["v"])
+    sweep_pass(zero, zero["u"], zero["v"], PAD + 16, PAD + 304, 4)
+    residual_pass(zero, zero["v"], zero["u"], PAD + 16, PAD + 304, 4)
     coarsen_into(zero, (one["k"], one["s"], one["b"]), 8, 152)
     smooth_down(one, 8, 152, 6)
     coarsen_into(one, (two.at[0], two.at[1], two.at[2]), 8, 72)
 
+    total = None
+    for t in range(2):
+        inside = lambda c: (c >= RIM) & (c < RIM + 64)
+        chooser = pick(lambda r, c: (r + LANES * t == 4 * (c - RIM)) & inside(c))
+        rows = jnp.concatenate([two[i, t, pl.ds(PAD + 8, 64), :] for i in range(3)], axis=0)
+        part = choose(rows, chooser)
+        total = part if total is None else total + part
     for i in range(3):
-        total = jnp.zeros((64, LANES), jnp.float32)
-        for t in range(3):
-            chooser = pick(lambda r, c: (r + LANES * t == 64 + 4 * (c - RIM)) & (c >= RIM) & (c < RIM + 64))
-            total = total + choose(two[i, t, pl.ds(PAD + 8, 64), :], chooser)
-        own2[i, :, :] = total
+        own2[i, :, :] = total[64 * i : 64 * i + 64]
 
     def send(row):
         lane = iota(1)
@@ -334,8 +353,9 @@
     smooth_down(three, 0, 56, 7)
     coarsen_into(three, (four.at[0], four.at[1], four.at[2]), 0, 32)
     chooser = pick(lambda r, c: (r == 4 * c) & (c < 28))
+    total = choose(jnp.concatenate([four[i, 0, pl.ds(PAD, 32), :] for i in range(3)], axis=0), chooser)
     for i in range(3):
-        message[i, :, :] = choose(four[i, 0, pl.ds(PAD, 32), :], chooser)
+        message[i, :, :] = total[32 * i : 32 * i + 32]
 
 
 def coarse_join_kernel(edges, message, left, right, wide):
@@ -392,23 +412,19 @@
     c = rise(2, c, 8, 64, 8, 24, 104, 5)
     fine = c[0, pl.ds(24, 80), :]
     for t in range(3):
-        coarse_fine[t, :, :] = choose(fine, pick(lambda r, c: r == (c + LANES * t) // 4 + 8))
+        turn = lambda c: jnp.where(c < 64, 0, 96) if t == 2 else 0
+        coarse_fine[t, :, :] = choose(fine, pick(lambda r, c: r == (c + LANES * t) // 4 + RIM - turn(c)))
     c = rise(1, coarse_fine, 0, 80, -8, 16, 160, 6)
     rise(0, c, 16, 160, 8, 32, 304, 2, False)
 
     level = levels[0]
 
     def body(row):
-        lane = iota(1)
         cells = around(level["u"], row, 2, 1)
         for j in range(2):
-            values = []
-            for t in range(3):
+            for t in range(2):
                 value = (1.0 - OMEGA) * cells[t, j][0] + weighted(level, t, rows_at(row, j), cells[t, j])
-                values.append(roll(value, 64, 1))
-            for t in range(2):
-                at = pl.ds(row + 8 * j - PAD - 32, 8)
-                out[at, LANES * t : LANES * (t + 1)] = jnp.where(lane < 64, values[t], values[t + 1])
+                out[pl.ds(row + 8 * j - PAD - 32, 8), LANES * t : LANES * (t + 1)] = value
 
     over_rows(PAD + 32, PAD + 32 + SIZE, 2, body)
 
@@ -437,13 +453,14 @@
     return lax.ppermute(up_block, axis, up), lax.ppermute(down_block, axis, down)
 
 
-def call(kernel, outs, ins, scratch=(), grant=4):
+def call(kernel, outs, ins, scratch=(), grant=4, aliases={}):
     return pl.pallas_call(
         kernel,
         out_shape=tuple(shape_of(*shape) for shape in outs),
         in_specs=[SCALARS] + [HERE] * (len(ins) - 1),
         out_specs=(HERE,) * len(outs),
         scratch_shapes=scratch,
+        input_output_aliases=aliases,
         cost_estimate=cost(8 * MIB, 4 * MIB),
         compiler_params=pltpu.CompilerParams(vmem_limit_bytes=grant * MIB),
     )(*ins)
@@ -467,13 +484,15 @@
     top, bottom = call(edge_kernel, [(4, 3, HALO, LANES)] * 2, (edges, own, before, after))
     above, below = exchange(bottom, top, "gx")
 
+    started = call(start_kernel, [array_of(0)] * 10, (edges, own, before, after))
     *kept, own2, low2, high2 = call(
         fine_kernel,
-        [array_of(0)] * 6 + [array_of(1)] * 6 + [(3, 64, LANES), (64, LANES), (64, LANES)],
-        (edges, own, before, after, above, below),
-        [vmem(*array_of(0))] * 4 + [vmem(*array_of(1))] * 4 + [vmem(3, 3, 80 + 2 * PAD, LANES)],
-        grant=6,
+        [array_of(0)] * 10 + [array_of(1)] * 6 + [(3, 64, LANES), (64, LANES), (64, LANES)],
+        (edges, above, below, *started),
+        [vmem(*array_of(1))] * 4 + [vmem(3, 3, 80 + 2 * PAD, LANES)],
+        aliases={3 + n: n for n in range(10)},
     )
+    kept = kept[:6] + kept[10:]
     left, right = exchange(high2, low2, "gy")
     wide2, top2, bottom2 = call(
         join_kernel, [(3, 64, LANES), (3, RIM, LANES), (3, RIM, LANES)], (edges, own2, left, right)

time: 70.4 us -> 66.8 us (0.949)
  waiting for transfers between devices: 20.6 us -> 16.6 us
  starting transfers between devices: 23.7 us -> 25.5 us
  Pallas kernels: 25.9 us -> 24.4 us
    ppermute x6, waiting for transfers between devices: 10.1 us -> 7.71 us  [exchange(): lax.ppermute(down_block, axis, down)]
    ppermute x6, starting transfers between devices: 9.67 us -> 11.4 us  [exchange(): lax.ppermute(up_block, axis, up)]
    ppermute x6, waiting for transfers between devices: 10.5 us -> 8.85 us  [exchange(): lax.ppermute(up_block, axis, up)]
    pallas_call x1, Pallas kernels: 8.86 us -> 7.75 us  [per_device(): pl.pallas_call(up_kernel, out_shape=shape_of(SIZE, SIZE), in_specs=[SCALA...]
    pallas_call x5 -> x6, Pallas kernels: 14.4 us -> 14 us  [call(): pl.pallas_call(kernel, out_shape=tuple((shape_of(*shape) for shape in out...]
  transfers between devices with their start and end apart: 12 -> 12, of which waited for: 9 -> 8; matrix products, arithmetic and copies ran while one was open for 0% -> 0% of each run, Pallas kernels for 0% -> 6%
where the time goes in v4:
time: 66.8 us; the launch traced here: 66.7 us
  starting transfers between devices  25.5 us (38%)
  Pallas kernels  24.4 us (37%)
  waiting for transfers between devices  16.6 us (25%)
    ppermute x6, starting transfers between devices, exchange(): lax.ppermute(down_block, axis, down)  14.1 us
    pallas_call x6, Pallas kernels, call(): pl.pallas_call(kernel, out_shape=tuple((shape_of(*shape) for shape in out...  14 us
    ppermute x6, starting transfers between devices, exchange(): lax.ppermute(up_block, axis, up)  11.4 us
    ppermute x6, waiting for transfers between devices, exchange(): lax.ppermute(up_block, axis, up)  8.85 us
    pallas_call x1, Pallas kernels, per_device(): pl.pallas_call(up_kernel, out_shape=shape_of(SIZE, SIZE), in_specs=[SCALA...  7.75 us
    ppermute x6, waiting for transfers between devices, exchange(): lax.ppermute(down_block, axis, down)  7.71 us
    pallas_call x1, Pallas kernels, per_device(): pl.pallas_call(pack_kernel, out_shape=(shape_of(4, 2, SIZE, LANES), shape...  2.69 us
  transfers between devices with their start and end apart: 12, of which 8 were waited for; matrix products, arithmetic and copies ran while one was open for 0% of the time, Pallas kernels for 6%

profile of v4, /device:TPU:97, one launch (start us, length us, event | category | flops | bytes accessed | tf_op | source)
XLA Modules:
  0.0 66.7 jit_solution(8677906784587306295)
XLA Ops:
  0.0 2.7 %shard_map.46 = (f32[4,2,256,128]{3,2,1,0:T(8,128)S(1)}, f32[128,128]{1,0:T(8,128)S(1)}, f32[128,128]{1,0:T(8,128)S(1)}) custom-call(f32[256,256]{1,0:T(8,128)} %k.1, f32[256,256]{1,0:T(8,128)} %s.1, f32[256,256]{1,0:T(8,128)} %b.1, f32[256,256]{1,0:T(8,128)} %v.1), custom_call_target="tpu_custom_call" | custom-call | flops 2097152 | bytes 2097152 | tf_op jit(solution)/shard_map/pallas_call | solution.py:474
  2.7 1.4 %collective-permute-start = (f32[128,128]{1,0:T(8,128)S(1)}, f32[128,128]{1,0:T(8,128)S(1)}, u32[]{:S(2)}, u32[]{:S(2)}) collective-permute-start(f32[128,128]{1,0:T(8,128)S(1)} %get-tuple-element.52), channel_id=1, source_target_pairs={{0,1},{1,2},{2,3},{3,4},{4,5},{5,6},{6,7},{7,8},{8,9},{9,10},{10,1... | collective-permute-start | bytes 196616 | tf_op jit(solution)/shard_map/ppermute | solution.py:453
  4.1 3.7 %collective-permute-start.1 = (f32[128,128]{1,0:T(8,128)S(1)}, f32[128,128]{1,0:T(8,128)S(1)}, u32[]{:S(2)}, u32[]{:S(2)}) collective-permute-start(f32[128,128]{1,0:T(8,128)S(1)} %get-tuple-element.53), channel_id=1, source_target_pairs={{1,0},{2,1},{3,2},{4,3},{5,4},{6,5},{7,6},{8,7},{9,8},{10,9},{11,1... | collective-permute-start | bytes 196616 | tf_op jit(solution)/shard_map/ppermute | solution.py:453
  7.8 0.1 add_convert_fusion.edges
  7.9 1.5 %collective-permute-done.before = f32[128,128]{1,0:T(8,128)S(1)} collective-permute-done((f32[128,128]{1,0:T(8,128)S(1)}, f32[128,128]{1,0:T(8,128)S(1)}, u32[]{:S(2)}, u32[]{:S(2)}) %collective-permute-start) | collective-permute-done | bytes 65568 | tf_op jit(solution)/shard_map/ppermute | solution.py:453
  9.4 0.0 collective-permute-done.1.after
  9.4 0.6 shard_map.47
  10.0 4.4 %collective-permute-start.2 = (f32[4,3,16,128]{3,2,1,0:T(8,128)S(1)}, f32[4,3,16,128]{3,2,1,0:T(8,128)S(1)}, u32[]{:S(2)}, u32[]{:S(2)}) collective-permute-start(f32[4,3,16,128]{3,2,1,0:T(8,128)S(1)} %get-tuple-element.54), channel_id=1, source_target_pairs={{0,16},{16,32},{32,48},{48,64},{64,80},{80,96},{96,112},{112,128},... | collective-permute-start | bytes 294920 | tf_op jit(solution)/shard_map/ppermute | solution.py:453
  14.4 4.0 %shard_map.48 = (f32[3,336,128]{2,1,0:T(8,128)S(1)}, f32[3,336,128]{2,1,0:T(8,128)S(1)}, f32[3,336,128]{2,1,0:T(8,128)S(1)}, f32[3,336,128]{2,1,0:T(8,128)S(1)},...) custom-call(s32[4]{0:T(128)S(1)} %add_convert_fusion.edges, ...), custom_call_target="tpu_custom_call" | custom-call | flops 8388608 | bytes 4194304 | tf_op jit(solution)/shard_map/pallas_call | solution.py:457
  18.4 0.0 collective-permute-done.2.above
  18.4 1.2 %collective-permute-done.3.below = f32[4,3,16,128]{3,2,1,0:T(8,128)S(1)} collective-permute-done((f32[4,3,16,128]{3,2,1,0:T(8,128)S(1)}, f32[4,3,16,128]{3,2,1,0:T(8,128)S(1)}, u32[]{:S(2)}, u32[]{:S(2)}) %collective-permute-start.3) | collective-permute-done | bytes 98336 | tf_op jit(solution)/shard_map/ppermute | solution.py:453
  19.7 5.9 %shard_map.49 = (f32[3,336,128]{2,1,0:T(8,128)S(1)}, f32[3,336,128]{2,1,0:T(8,128)S(1)}, f32[3,336,128]{2,1,0:T(8,128)S(1)}, f32[3,336,128]{2,1,0:T(8,128)S(1)},...) custom-call(s32[4]{0:T(128)S(1)} %add_convert_fusion.edges, ...), custom_call_target="tpu_custom_call", output_to_operand_aliasing={{0}: (3, {}), {1}: (4, {}), {2}: (5, {}), {3}: (6, {}), {4}... | custom-call | flops 8388608 | bytes 4194304 | tf_op jit(solution)/shard_map/pallas_call | solution.py:457
  25.5 0.0 collective-permute-start.4
  25.6 5.1 %collective-permute-start.5 = (f32[64,128]{1,0:T(8,128)S(1)}, f32[64,128]{1,0:T(8,128)S(1)}, u32[]{:S(2)}, u32[]{:S(2)}) collective-permute-start(f32[64,128]{1,0:T(8,128)S(1)} %get-tuple-element.68), channel_id=1, source_target_pairs={{1,0},{2,1},{3,2},{4,3},{5,4},{6,5},{7,6},{8,7},{9,8},{10,9},{11,1... | collective-permute-start | bytes 98312 | tf_op jit(solution)/shard_map/ppermute | solution.py:453
  30.7 1.2 %collective-permute-done.4.left = f32[64,128]{1,0:T(8,128)S(1)} collective-permute-done((f32[64,128]{1,0:T(8,128)S(1)}, f32[64,128]{1,0:T(8,128)S(1)}, u32[]{:S(2)}, u32[]{:S(2)}) %collective-permute-start.4) | collective-permute-done | bytes 32800 | tf_op jit(solution)/shard_map/ppermute | solution.py:453
  31.9 0.0 collective-permute-done.5.right
  31.9 0.6 shard_map.50
  32.6 2.7 %collective-permute-start.6 = (f32[3,24,128]{2,1,0:T(8,128)S(1)}, f32[3,24,128]{2,1,0:T(8,128)S(1)}, u32[]{:S(2)}, u32[]{:S(2)}) collective-permute-start(f32[3,24,128]{2,1,0:T(8,128)S(1)} %get-tuple-element.70), channel_id=1, source_target_pairs={{0,16},{16,32},{32,48},{48,64},{64,80},{80,96},{96,112},{112,128},... | collective-permute-start | bytes 110600 | tf_op jit(solution)/shard_map/ppermute | solution.py:453
  35.3 0.0 collective-permute-start.7
  35.3 1.1 %collective-permute-done.6.above = f32[3,24,128]{2,1,0:T(8,128)S(1)} collective-permute-done((f32[3,24,128]{2,1,0:T(8,128)S(1)}, f32[3,24,128]{2,1,0:T(8,128)S(1)}, u32[]{:S(2)}, u32[]{:S(2)}) %collective-permute-start.6) | collective-permute-done | bytes 36896 | tf_op jit(solution)/shard_map/ppermute | solution.py:453
  36.3 3.5 %collective-permute-done.7.below = f32[3,24,128]{2,1,0:T(8,128)S(1)} collective-permute-done((f32[3,24,128]{2,1,0:T(8,128)S(1)}, f32[3,24,128]{2,1,0:T(8,128)S(1)}, u32[]{:S(2)}, u32[]{:S(2)}) %collective-permute-start.7) | collective-permute-done | bytes 36896 | tf_op jit(solution)/shard_map/ppermute | solution.py:453
  39.9 2.2 %shard_map.51 = (f32[1,128,128]{2,1,0:T(8,128)S(1)}, f32[1,128,128]{2,1,0:T(8,128)S(1)}, f32[1,128,128]{2,1,0:T(8,128)S(1)}, f32[1,128,128]{2,1,0:T(8,128)S(1)},...) custom-call(s32[4]{0:T(128)S(1)} %add_convert_fusion.edges, ...), custom_call_target="tpu_custom_call" | custom-call | flops 8388608 | bytes 4194304 | tf_op jit(solution)/shard_map/pallas_call | solution.py:457
  42.1 5.2 %collective-permute-start.9 = (f32[3,32,128]{2,1,0:T(8,128)S(1)}, f32[3,32,128]{2,1,0:T(8,128)S(1)}, u32[]{:S(2)}, u32[]{:S(2)}) collective-permute-start(f32[3,32,128]{2,1,0:T(8,128)S(1)} %get-tuple-element.72.message), channel_id=1, source_target_pairs={{1,0},{2,1},{3,2},{4,3},{5,4},{6,5},{7,6},{8,7},{9,8},{10,9},{11,1... | collective-permute-start | bytes 147464 | tf_op jit(solution)/shard_map/ppermute | solution.py:453
  47.3 0.0 collective-permute-start.8
  47.3 1.2 %collective-permute-done.9.right = f32[3,32,128]{2,1,0:T(8,128)S(1)} collective-permute-done((f32[3,32,128]{2,1,0:T(8,128)S(1)}, f32[3,32,128]{2,1,0:T(8,128)S(1)}, u32[]{:S(2)}, u32[]{:S(2)}) %collective-permute-start.9) | collective-permute-done | bytes 49184 | tf_op jit(solution)/shard_map/ppermute | solution.py:453
  48.5 5.1 %collective-permute-done.8.left = f32[3,32,128]{2,1,0:T(8,128)S(1)} collective-permute-done((f32[3,32,128]{2,1,0:T(8,128)S(1)}, f32[3,32,128]{2,1,0:T(8,128)S(1)}, u32[]{:S(2)}, u32[]{:S(2)}) %collective-permute-start.8) | collective-permute-done | bytes 49184 | tf_op jit(solution)/shard_map/ppermute | solution.py:453
  53.6 0.6 shard_map.52.wide
  54.2 0.0 collective-permute-start.11
  54.2 2.9 %collective-permute-start.10 = (f32[3,32,128]{2,1,0:T(8,128)S(1)}, f32[3,32,128]{2,1,0:T(8,128)S(1)}, u32[]{:S(2)}, u32[]{:S(2)}) collective-permute-start(f32[3,32,128]{2,1,0:T(8,128)S(1)} %shard_map.52.wide), channel_id=1, source_target_pairs={{0,16},{16,32},{32,48},{48,64},{64,80},{80,96},{96,112},{112,128},... | collective-permute-start | bytes 147464 | tf_op jit(solution)/shard_map/ppermute | solution.py:453
  57.2 1.8 %collective-permute-done.11.lower = f32[3,32,128]{2,1,0:T(8,128)S(1)} collective-permute-done((f32[3,32,128]{2,1,0:T(8,128)S(1)}, f32[3,32,128]{2,1,0:T(8,128)S(1)}, u32[]{:S(2)}, u32[]{:S(2)}) %collective-permute-start.11) | collective-permute-done | bytes 49184 | tf_op jit(solution)/shard_map/ppermute | solution.py:453
  58.9 0.0 collective-permute-done.10.upper
  58.9 7.8 %shard_map.53 = f32[256,256]{1,0:T(8,128)} custom-call(s32[4]{0:T(128)S(1)} %add_convert_fusion.edges, f32[3,32,128]{2,1,0:T(8,128)S(1)} %shard_map.52.wide, f32[3,32,128]{2,1,0:T(8,128)S(1)} %collective-permute-done.10.upper, f32[3,32,128]{2,1,0:T(8,128)S(1)} %collective-permute-done.11.lower, f32[3,336,128]{2,1,0:T(8,128)S(1)} %get-tuple-element.73.refs_0_, ...), custom_call_target="tpu_custom_call" | custom-call | flops 41943040 | bytes 12582912 | tf_op jit(solution)/shard_map/pallas_call | solution.py:511
  (1 shorter events, 0.0 us)
Async XLA Ops:
  2.7 6.7 %collective-permute-start = (f32[128,128]{1,0:T(8,128)S(1)}, f32[128,128]{1,0:T(8,128)S(1)}, u32[]{:S(2)}, u32[]{:S(2)}) collective-permute-start(f32[128,128]{1,0:T(8,128)S(1)} %get-tuple-element.52), channel_id=1, source_target_pairs={{0,1},{1,2},{2,3},{3,4},{4,5},{5,6},{6,7},{7,8},{8,9},{9,10},{10,1... | collective-permute-start | bytes 196616 | tf_op jit(solution)/shard_map/ppermute | solution.py:453
  4.1 5.3 %collective-permute-start.1 = (f32[128,128]{1,0:T(8,128)S(1)}, f32[128,128]{1,0:T(8,128)S(1)}, u32[]{:S(2)}, u32[]{:S(2)}) collective-permute-start(f32[128,128]{1,0:T(8,128)S(1)} %get-tuple-element.53), channel_id=1, source_target_pairs={{1,0},{2,1},{3,2},{4,3},{5,4},{6,5},{7,6},{8,7},{9,8},{10,9},{11,1... | collective-permute-start | bytes 196616 | tf_op jit(solution)/shard_map/ppermute | solution.py:453
  10.0 8.4 %collective-permute-start.2 = (f32[4,3,16,128]{3,2,1,0:T(8,128)S(1)}, f32[4,3,16,128]{3,2,1,0:T(8,128)S(1)}, u32[]{:S(2)}, u32[]{:S(2)}) collective-permute-start(f32[4,3,16,128]{3,2,1,0:T(8,128)S(1)} %get-tuple-element.54), channel_id=1, source_target_pairs={{0,16},{16,32},{32,48},{48,64},{64,80},{80,96},{96,112},{112,128},... | collective-permute-start | bytes 294920 | tf_op jit(solution)/shard_map/ppermute | solution.py:453
  14.4 5.3 %collective-permute-start.3 = (f32[4,3,16,128]{3,2,1,0:T(8,128)S(1)}, f32[4,3,16,128]{3,2,1,0:T(8,128)S(1)}, u32[]{:S(2)}, u32[]{:S(2)}) collective-permute-start(f32[4,3,16,128]{3,2,1,0:T(8,128)S(1)} %get-tuple-element.55), channel_id=1, source_target_pairs={{16,0},{32,16},{48,32},{64,48},{80,64},{96,80},{112,96},{128,112},... | collective-permute-start | bytes 294920 | tf_op jit(solution)/shard_map/ppermute | solution.py:453
  25.5 6.4 %collective-permute-start.4 = (f32[64,128]{1,0:T(8,128)S(1)}, f32[64,128]{1,0:T(8,128)S(1)}, u32[]{:S(2)}, u32[]{:S(2)}) collective-permute-start(f32[64,128]{1,0:T(8,128)S(1)} %get-tuple-element.67), channel_id=1, source_target_pairs={{0,1},{1,2},{2,3},{3,4},{4,5},{5,6},{6,7},{7,8},{8,9},{9,10},{10,1... | collective-permute-start | bytes 98312 | tf_op jit(solution)/shard_map/ppermute | solution.py:453
  25.6 6.4 %collective-permute-start.5 = (f32[64,128]{1,0:T(8,128)S(1)}, f32[64,128]{1,0:T(8,128)S(1)}, u32[]{:S(2)}, u32[]{:S(2)}) collective-permute-start(f32[64,128]{1,0:T(8,128)S(1)} %get-tuple-element.68), channel_id=1, source_target_pairs={{1,0},{2,1},{3,2},{4,3},{5,4},{6,5},{7,6},{8,7},{9,8},{10,9},{11,1... | collective-permute-start | bytes 98312 | tf_op jit(solution)/shard_map/ppermute | solution.py:453
  32.6 3.7 %collective-permute-start.6 = (f32[3,24,128]{2,1,0:T(8,128)S(1)}, f32[3,24,128]{2,1,0:T(8,128)S(1)}, u32[]{:S(2)}, u32[]{:S(2)}) collective-permute-start(f32[3,24,128]{2,1,0:T(8,128)S(1)} %get-tuple-element.70), channel_id=1, source_target_pairs={{0,16},{16,32},{32,48},{48,64},{64,80},{80,96},{96,112},{112,128},... | collective-permute-start | bytes 110600 | tf_op jit(solution)/shard_map/ppermute | solution.py:453
  35.3 4.6 %collective-permute-start.7 = (f32[3,24,128]{2,1,0:T(8,128)S(1)}, f32[3,24,128]{2,1,0:T(8,128)S(1)}, u32[]{:S(2)}, u32[]{:S(2)}) collective-permute-start(f32[3,24,128]{2,1,0:T(8,128)S(1)} %get-tuple-element.71), channel_id=1, source_target_pairs={{16,0},{32,16},{48,32},{64,48},{80,64},{96,80},{112,96},{128,112},... | collective-permute-start | bytes 110600 | tf_op jit(solution)/shard_map/ppermute | solution.py:453
  42.1 6.4 %collective-permute-start.9 = (f32[3,32,128]{2,1,0:T(8,128)S(1)}, f32[3,32,128]{2,1,0:T(8,128)S(1)}, u32[]{:S(2)}, u32[]{:S(2)}) collective-permute-start(f32[3,32,128]{2,1,0:T(8,128)S(1)} %get-tuple-element.72.message), channel_id=1, source_target_pairs={{1,0},{2,1},{3,2},{4,3},{5,4},{6,5},{7,6},{8,7},{9,8},{10,9},{11,1... | collective-permute-start | bytes 147464 | tf_op jit(solution)/shard_map/ppermute | solution.py:453
  47.3 6.3 %collective-permute-start.8 = (f32[3,32,128]{2,1,0:T(8,128)S(1)}, f32[3,32,128]{2,1,0:T(8,128)S(1)}, u32[]{:S(2)}, u32[]{:S(2)}) collective-permute-start(f32[3,32,128]{2,1,0:T(8,128)S(1)} %get-tuple-element.72.message), channel_id=1, source_target_pairs={{0,1},{1,2},{2,3},{3,4},{4,5},{5,6},{6,7},{7,8},{8,9},{9,10},{10,1... | collective-permute-start | bytes 147464 | tf_op jit(solution)/shard_map/ppermute | solution.py:453
  54.2 4.7 %collective-permute-start.11 = (f32[3,32,128]{2,1,0:T(8,128)S(1)}, f32[3,32,128]{2,1,0:T(8,128)S(1)}, u32[]{:S(2)}, u32[]{:S(2)}) collective-permute-start(f32[3,32,128]{2,1,0:T(8,128)S(1)} %shard_map.52.wide), channel_id=1, source_target_pairs={{16,0},{32,16},{48,32},{64,48},{80,64},{96,80},{112,96},{128,112},... | collective-permute-start | bytes 147464 | tf_op jit(solution)/shard_map/ppermute | solution.py:453
  54.2 4.7 %collective-permute-start.10 = (f32[3,32,128]{2,1,0:T(8,128)S(1)}, f32[3,32,128]{2,1,0:T(8,128)S(1)}, u32[]{:S(2)}, u32[]{:S(2)}) collective-permute-start(f32[3,32,128]{2,1,0:T(8,128)S(1)} %shard_map.52.wide), channel_id=1, source_target_pairs={{0,16},{16,32},{32,48},{48,64},{64,80},{80,96},{96,112},{112,128},... | collective-permute-start | bytes 147464 | tf_op jit(solution)/shard_map/ppermute | solution.py:453

commit v5 on v4

--- a/solution.py
+++ b/solution.py
@@ -128,7 +128,8 @@
 
 
 def coarsen_pass(triples, step, first, last):
-    height = 2 if (last - first) % 16 == 0 else 1
+    trips = (last - first) // 8
+    height = max(n for n in (1, 2, 4, 6, 8) if trips % n == 0)
 
     def body(row):
         for j in range(height):
@@ -141,14 +142,18 @@
 
 
 def correct_pass(source, base, target, first, last, shift):
-    def body(row):
-        for t in range(source.shape[0]):
-            x = source[t, pl.ds(row, 8), :]
-            for half in range(2):
-                at = pl.ds(2 * row - shift + half, 8, stride=2)
-                target[t, at, :] = base[t, at, :] + x
-
-    over_rows(first, last, 1, body)
+    trips = (last - first) // 8
+    height = max(n for n in range(1, 8) if trips % n == 0)
+
+    def body(row):
+        for j in range(height):
+            for t in range(source.shape[0]):
+                x = source[t, rows_at(row, j), :]
+                for half in range(2):
+                    at = pl.ds(2 * row + 16 * j - shift + half, 8, stride=2)
+                    target[t, at, :] = base[t, at, :] + x
+
+    over_rows(first, last, height, body)
 
 
 def clear_rows(refs, at):
@@ -209,7 +214,7 @@
         yield i, 2, jnp.where(lane < HALO * edges[1], high, low)
 
 
-def edge_kernel(edges, own, before, after, top, bottom):
+def edge_kernel(edges, own, before, after, _, top, bottom):
     for j in range(HALO // 8):
         for target, row, half in ((top, 8 * j, 0), (bottom, SIZE - HALO + 8 * j, 1)):
             for i, t, x in widened(edges, own, before, after, row, half):
@@ -253,6 +258,21 @@
     return levels
 
 
+def shrink_kernel(edges, own, k1, s1, k2, s2):
+    def halve(source, target, step, from_row, to_row, count, factor):
+        def body(row):
+            for j in range(4):
+                for t in range(2):
+                    x = pair_sum(source, t, 2 * row + 16 * j + from_row, step)
+                    target[t, rows_at(row + to_row, j), :] = factor * x
+
+        over_rows(0, count, 4, body)
+
+    for i, first, second, factor in ((0, k1, k2, 0.5), (1, s1, s2, 1.0)):
+        halve(own.at[i], first, 1, 0, PAD + 16, 128, factor)
+        halve(first, second, 2, PAD + 16, 0, 64, factor)
+
+
 ALL = KEPT + "ksud"
 
 
@@ -262,18 +282,19 @@
     for half in range(2):
 
         def fill(row):
-            for i, t, x in widened(edges, own, before, after, row, half):
-                frame[i][t, pl.ds(PAD + 32 + row, 8), :] = x
-
-        over_rows(128 * half, 128 * half + 128, 1, fill)
+            for j in range(4):
+                for i, t, x in widened(edges, own, before, after, row + 8 * j, half):
+                    frame[i][t, rows_at(PAD + 32 + row, j), :] = x
+
+        over_rows(128 * half, 128 * half + 128, 4, fill)
     face_pass(zero, PAD + 40, PAD + 280, 5, zero["v"])
 
 
 def fine_kernel(edges, above, below, *refs):
-    started, rest, kept1, own2, low2, high2, refs = refs[10:20], refs[0:10], refs[20:26], *refs[26:29], refs[29:]
-    zero = dict(zip(ALL, started), step=STEP[0])
-    one = dict(zip(ALL, (*kept1, *refs[:4])), step=STEP[1])
-    two = refs[4]
+    k2, s2, refs = refs[12], refs[13], refs[14:]
+    zero = dict(zip(ALL, refs[0:10]), step=STEP[0])
+    own2, low2, high2, u1, d1, b2 = refs[18:24]
+    one = dict(zip(ALL, (*refs[10:18], u1, d1)), step=STEP[1])
     clear_rows([zero[n] for n in "ksbvuweon"], (PAD + 8, PAD + 304))
     clear_rows([one[n] for n in "ksbvuweon"], (PAD, PAD + 152))
     frame = [zero[n] for n in "ksbv"]
@@ -289,17 +310,22 @@
 
     face_pass(zero, PAD + 16, PAD + 40, 3, zero["v"])
     face_pass(zero, PAD + 280, PAD + 304, 3, zero["v"])
-    sweep_pass(zero, zero["u"], zero["v"], PAD + 16, PAD + 304, 4)
-    residual_pass(zero, zero["v"], zero["u"], PAD + 16, PAD + 304, 4)
-    coarsen_into(zero, (one["k"], one["s"], one["b"]), 8, 152)
+    sweep_pass(zero, zero["u"], zero["v"], PAD + 16, PAD + 304, 12)
+    residual_pass(zero, zero["v"], zero["u"], PAD + 16, PAD + 304, 12)
+    pairs = [(zero[n], one[n], factor) for n, factor in (("k", 0.5), ("s", 1.0))]
+    third = [(source.at[pl.ds(2, 1)], target.at[pl.ds(2, 1)], factor) for source, target, factor in pairs]
+    coarsen_pass([(zero["u"], one["b"], 1.0), *third], 1, 8, 152)
+    first = [(source.at[pl.ds(0, 2)], target.at[pl.ds(0, 2)], factor) for source, target, factor in pairs]
+    coarsen_pass(first, 1, 8, 16)
+    coarsen_pass(first, 1, 144, 152)
     smooth_down(one, 8, 152, 6)
-    coarsen_into(one, (two.at[0], two.at[1], two.at[2]), 8, 72)
+    coarsen_pass([(one["u"].at[pl.ds(0, 2)], b2, 1.0)], 2, 8, 72)
 
     total = None
     for t in range(2):
         inside = lambda c: (c >= RIM) & (c < RIM + 64)
         chooser = pick(lambda r, c: (r + LANES * t == 4 * (c - RIM)) & inside(c))
-        rows = jnp.concatenate([two[i, t, pl.ds(PAD + 8, 64), :] for i in range(3)], axis=0)
+        rows = jnp.concatenate([k2[t], s2[t], b2[t, pl.ds(PAD + 8, 64), :]], axis=0)
         part = choose(rows, chooser)
         total = part if total is None else total + part
     for i in range(3):
@@ -415,18 +441,18 @@
         turn = lambda c: jnp.where(c < 64, 0, 96) if t == 2 else 0
         coarse_fine[t, :, :] = choose(fine, pick(lambda r, c: r == (c + LANES * t) // 4 + RIM - turn(c)))
     c = rise(1, coarse_fine, 0, 80, -8, 16, 160, 6)
-    rise(0, c, 16, 160, 8, 32, 304, 2, False)
+    rise(0, c, 16, 160, 8, 24, 312, 12, False)
 
     level = levels[0]
 
     def body(row):
-        cells = around(level["u"], row, 2, 1)
-        for j in range(2):
+        cells = around(level["u"], row, 8, 1)
+        for j in range(8):
             for t in range(2):
                 value = (1.0 - OMEGA) * cells[t, j][0] + weighted(level, t, rows_at(row, j), cells[t, j])
                 out[pl.ds(row + 8 * j - PAD - 32, 8), LANES * t : LANES * (t + 1)] = value
 
-    over_rows(PAD + 32, PAD + 32 + SIZE, 2, body)
+    over_rows(PAD + 32, PAD + 32 + SIZE, 8, body)
 
 
 def shape_of(*shape):
@@ -481,18 +507,19 @@
         compiler_params=pltpu.CompilerParams(vmem_limit_bytes=2 * MIB),
     )(*[pltpu.with_memory_space_constraint(block, pltpu.HBM) for block in blocks])
     before, after = exchange(high, low, "gy")
-    top, bottom = call(edge_kernel, [(4, 3, HALO, LANES)] * 2, (edges, own, before, after))
+    shrunk = call(shrink_kernel, [array_of(1)] * 2 + [(2, 64, LANES)] * 2, (edges, own))
+    top, bottom = call(edge_kernel, [(4, 3, HALO, LANES)] * 2, (edges, own, before, after, shrunk[3]))
     above, below = exchange(bottom, top, "gx")
 
     started = call(start_kernel, [array_of(0)] * 10, (edges, own, before, after))
     *kept, own2, low2, high2 = call(
         fine_kernel,
-        [array_of(0)] * 10 + [array_of(1)] * 6 + [(3, 64, LANES), (64, LANES), (64, LANES)],
-        (edges, above, below, *started),
-        [vmem(*array_of(1))] * 4 + [vmem(3, 3, 80 + 2 * PAD, LANES)],
-        aliases={3 + n: n for n in range(10)},
+        [array_of(0)] * 10 + [array_of(1)] * 8 + [(3, 64, LANES), (64, LANES), (64, LANES)],
+        (edges, above, below, *started, *shrunk),
+        [vmem(*array_of(1))] * 2 + [vmem(2, 80 + 2 * PAD, LANES)],
+        aliases={3 + n: n for n in range(10)} | {13: 16, 14: 17},
     )
-    kept = kept[:6] + kept[10:]
+    kept = kept[:6] + kept[10:16]
     left, right = exchange(high2, low2, "gy")
     wide2, top2, bottom2 = call(
         join_kernel, [(3, 64, LANES), (3, RIM, LANES), (3, RIM, LANES)], (edges, own2, left, right)

time: 66.8 us -> 61.1 us (0.915)
  Pallas kernels: 24.4 us -> 20.4 us
  starting transfers between devices: 25.5 us -> 23.8 us
    pallas_call x1, Pallas kernels: 7.75 us -> 5.49 us  [per_device(): pl.pallas_call(up_kernel, out_shape=shape_of(SIZE, SIZE), in_specs=[SCALA...]
    pallas_call x6 -> x7, Pallas kernels: 14 us -> 12.2 us  [call(): pl.pallas_call(kernel, out_shape=tuple((shape_of(*shape) for shape in out...]
    ppermute x6, starting transfers between devices: 11.4 us -> 9.69 us  [exchange(): lax.ppermute(up_block, axis, up)]
    ppermute x6, waiting for transfers between devices: 7.71 us -> 9.33 us  [exchange(): lax.ppermute(down_block, axis, down)]
    ppermute x6, waiting for transfers between devices: 8.85 us -> 7.36 us  [exchange(): lax.ppermute(up_block, axis, up)]
  transfers between devices with their start and end apart: 12 -> 12, of which waited for: 8 -> 7; matrix products, arithmetic and copies ran while one was open for 0% -> 0% of each run, Pallas kernels for 6% -> 7%
where the time goes in v5:
time: 61.1 us; the launch traced here: 61 us
  starting transfers between devices  23.8 us (39%)
  Pallas kernels  20.4 us (33%)
  waiting for transfers between devices  16.7 us (27%)
    ppermute x6, starting transfers between devices, exchange(): lax.ppermute(down_block, axis, down)  14.1 us
    pallas_call x7, Pallas kernels, call(): pl.pallas_call(kernel, out_shape=tuple((shape_of(*shape) for shape in out...  12.2 us
    ppermute x6, starting transfers between devices, exchange(): lax.ppermute(up_block, axis, up)  9.69 us
    ppermute x6, waiting for transfers between devices, exchange(): lax.ppermute(down_block, axis, down)  9.33 us
    ppermute x6, waiting for transfers between devices, exchange(): lax.ppermute(up_block, axis, up)  7.36 us
    pallas_call x1, Pallas kernels, per_device(): pl.pallas_call(up_kernel, out_shape=shape_of(SIZE, SIZE), in_specs=[SCALA...  5.49 us
    pallas_call x1, Pallas kernels, per_device(): pl.pallas_call(pack_kernel, out_shape=(shape_of(4, 2, SIZE, LANES), shape...  2.69 us
  transfers between devices with their start and end apart: 12, of which 7 were waited for; matrix products, arithmetic and copies ran while one was open for 0% of the time, Pallas kernels for 7%

profile of v5, /device:TPU:97, one launch (start us, length us, event | category | flops | bytes accessed | tf_op | source)
XLA Modules:
  0.0 61.0 jit_solution(9192678082907846029)
XLA Ops:
  0.0 2.7 %shard_map.46 = (f32[4,2,256,128]{3,2,1,0:T(8,128)S(1)}, f32[128,128]{1,0:T(8,128)S(1)}, f32[128,128]{1,0:T(8,128)S(1)}) custom-call(f32[256,256]{1,0:T(8,128)} %k.1, f32[256,256]{1,0:T(8,128)} %s.1, f32[256,256]{1,0:T(8,128)} %b.1, f32[256,256]{1,0:T(8,128)} %v.1), custom_call_target="tpu_custom_call" | custom-call | flops 2097152 | bytes 2097152 | tf_op jit(solution)/shard_map/pallas_call | solution.py:500
  2.7 1.4 %collective-permute-start = (f32[128,128]{1,0:T(8,128)S(1)}, f32[128,128]{1,0:T(8,128)S(1)}, u32[]{:S(2)}, u32[]{:S(2)}) collective-permute-start(f32[128,128]{1,0:T(8,128)S(1)} %get-tuple-element.56), channel_id=1, source_target_pairs={{0,1},{1,2},{2,3},{3,4},{4,5},{5,6},{6,7},{7,8},{8,9},{9,10},{10,1... | collective-permute-start | bytes 196616 | tf_op jit(solution)/shard_map/ppermute | solution.py:479
  4.1 3.7 %collective-permute-start.1 = (f32[128,128]{1,0:T(8,128)S(1)}, f32[128,128]{1,0:T(8,128)S(1)}, u32[]{:S(2)}, u32[]{:S(2)}) collective-permute-start(f32[128,128]{1,0:T(8,128)S(1)} %get-tuple-element.57), channel_id=1, source_target_pairs={{1,0},{2,1},{3,2},{4,3},{5,4},{6,5},{7,6},{8,7},{9,8},{10,9},{11,1... | collective-permute-start | bytes 196616 | tf_op jit(solution)/shard_map/ppermute | solution.py:479
  7.8 0.1 add_convert_fusion.edges
  7.9 1.6 %shard_map.47 = (f32[3,176,128]{2,1,0:T(8,128)S(1)}, f32[3,176,128]{2,1,0:T(8,128)S(1)}, f32[2,64,128]{2,1,0:T(8,128)S(1)}, f32[2,64,128]{2,1,0:T(8,128)S(1)}) custom-call(s32[4]{0:T(128)S(1)} %add_convert_fusion.edges, f32[4,2,256,128]{3,2,1,0:T(8,128)S(1)} %get-tuple-element.55.own), custom_call_target="tpu_custom_call" | custom-call | flops 8388608 | bytes 4194304 | tf_op jit(solution)/shard_map/pallas_call | solution.py:483
  9.5 0.0 collective-permute-done.before
  9.5 0.0 collective-permute-done.1.after
  9.5 0.6 %shard_map.48 = (f32[4,3,16,128]{3,2,1,0:T(8,128)S(1)}, f32[4,3,16,128]{3,2,1,0:T(8,128)S(1)}) custom-call(s32[4]{0:T(128)S(1)} %add_convert_fusion.edges, f32[4,2,256,128]{3,2,1,0:T(8,128)S(1)} %get-tuple-element.55.own, f32[128,128]{1,0:T(8,128)S(1)} %collective-permute-done.before, f32[128,128]{1,0:T(8,128)S(1)} %collective-permute-done.1.after, ...), custom_call_target="tpu_custom_call" | custom-call | flops 8388608 | bytes 4194304 | tf_op jit(solution)/shard_map/pallas_call | solution.py:483
  10.1 4.3 %collective-permute-start.2 = (f32[4,3,16,128]{3,2,1,0:T(8,128)S(1)}, f32[4,3,16,128]{3,2,1,0:T(8,128)S(1)}, u32[]{:S(2)}, u32[]{:S(2)}) collective-permute-start(f32[4,3,16,128]{3,2,1,0:T(8,128)S(1)} %get-tuple-element.59), channel_id=1, source_target_pairs={{0,16},{16,32},{32,48},{48,64},{64,80},{80,96},{96,112},{112,128},... | collective-permute-start | bytes 294920 | tf_op jit(solution)/shard_map/ppermute | solution.py:479
  14.4 0.0 collective-permute-start.3
  14.4 2.4 %shard_map.49 = (f32[3,336,128]{2,1,0:T(8,128)S(1)}, f32[3,336,128]{2,1,0:T(8,128)S(1)}, f32[3,336,128]{2,1,0:T(8,128)S(1)}, f32[3,336,128]{2,1,0:T(8,128)S(1)},...) custom-call(s32[4]{0:T(128)S(1)} %add_convert_fusion.edges, ...), custom_call_target="tpu_custom_call" | custom-call | flops 8388608 | bytes 4194304 | tf_op jit(solution)/shard_map/pallas_call | solution.py:483
  16.8 0.0 collective-permute-done.2.above
  16.8 2.9 %collective-permute-done.3.below = f32[4,3,16,128]{3,2,1,0:T(8,128)S(1)} collective-permute-done((f32[4,3,16,128]{3,2,1,0:T(8,128)S(1)}, f32[4,3,16,128]{3,2,1,0:T(8,128)S(1)}, u32[]{:S(2)}, u32[]{:S(2)}) %collective-permute-start.3) | collective-permute-done | bytes 98336 | tf_op jit(solution)/shard_map/ppermute | solution.py:479
  19.7 4.2 %shard_map.50 = (f32[3,336,128]{2,1,0:T(8,128)S(1)}, f32[3,336,128]{2,1,0:T(8,128)S(1)}, f32[3,336,128]{2,1,0:T(8,128)S(1)}, f32[3,336,128]{2,1,0:T(8,128)S(1)},...) custom-call(s32[4]{0:T(128)S(1)} %add_convert_fusion.edges, ...), custom_call_target="tpu_custom_call", output_to_operand_aliasing={{0}: (3, {}), {1}: (4, {}), {2}: (5, {}), {3}: (6, {}), {4}... | custom-call | flops 8388608 | bytes 4194304 | tf_op jit(solution)/shard_map/pallas_call | solution.py:483
  23.9 0.0 collective-permute-start.4
  23.9 5.1 %collective-permute-start.5 = (f32[64,128]{1,0:T(8,128)S(1)}, f32[64,128]{1,0:T(8,128)S(1)}, u32[]{:S(2)}, u32[]{:S(2)}) collective-permute-start(f32[64,128]{1,0:T(8,128)S(1)} %get-tuple-element.76), channel_id=1, source_target_pairs={{1,0},{2,1},{3,2},{4,3},{5,4},{6,5},{7,6},{8,7},{9,8},{10,9},{11,1... | collective-permute-start | bytes 98312 | tf_op jit(solution)/shard_map/ppermute | solution.py:479
  29.1 1.2 %collective-permute-done.4.left = f32[64,128]{1,0:T(8,128)S(1)} collective-permute-done((f32[64,128]{1,0:T(8,128)S(1)}, f32[64,128]{1,0:T(8,128)S(1)}, u32[]{:S(2)}, u32[]{:S(2)}) %collective-permute-start.4) | collective-permute-done | bytes 32800 | tf_op jit(solution)/shard_map/ppermute | solution.py:479
  30.3 0.0 collective-permute-done.5.right
  30.3 0.6 %shard_map.51 = (f32[3,64,128]{2,1,0:T(8,128)S(1)}, f32[3,24,128]{2,1,0:T(8,128)S(1)}, f32[3,24,128]{2,1,0:T(8,128)S(1)}) custom-call(s32[4]{0:T(128)S(1)} %add_convert_fusion.edges, f32[3,64,128]{2,1,0:T(8,128)S(1)} %get-tuple-element.74.own2, f32[64,128]{1,0:T(8,128)S(1)} %collective-permute-done.4.left, f32[64,128]{1,0:T(8,128)S(1)} %collective-permute-done.5.right), custom_call_target="tpu_custom_call" | custom-call | flops 8388608 | bytes 4194304 | tf_op jit(solution)/shard_map/pallas_call | solution.py:483
  30.9 1.0 %collective-permute-start.6 = (f32[3,24,128]{2,1,0:T(8,128)S(1)}, f32[3,24,128]{2,1,0:T(8,128)S(1)}, u32[]{:S(2)}, u32[]{:S(2)}) collective-permute-start(f32[3,24,128]{2,1,0:T(8,128)S(1)} %get-tuple-element.78), channel_id=1, source_target_pairs={{0,16},{16,32},{32,48},{48,64},{64,80},{80,96},{96,112},{112,128},... | collective-permute-start | bytes 110600 | tf_op jit(solution)/shard_map/ppermute | solution.py:479
  32.0 0.0 collective-permute-start.7
  32.0 1.1 %collective-permute-done.6.above = f32[3,24,128]{2,1,0:T(8,128)S(1)} collective-permute-done((f32[3,24,128]{2,1,0:T(8,128)S(1)}, f32[3,24,128]{2,1,0:T(8,128)S(1)}, u32[]{:S(2)}, u32[]{:S(2)}) %collective-permute-start.6) | collective-permute-done | bytes 36896 | tf_op jit(solution)/shard_map/ppermute | solution.py:479
  33.0 3.5 %collective-permute-done.7.below = f32[3,24,128]{2,1,0:T(8,128)S(1)} collective-permute-done((f32[3,24,128]{2,1,0:T(8,128)S(1)}, f32[3,24,128]{2,1,0:T(8,128)S(1)}, u32[]{:S(2)}, u32[]{:S(2)}) %collective-permute-start.7) | collective-permute-done | bytes 36896 | tf_op jit(solution)/shard_map/ppermute | solution.py:479
  36.6 2.1 %shard_map.52 = (f32[1,128,128]{2,1,0:T(8,128)S(1)}, f32[1,128,128]{2,1,0:T(8,128)S(1)}, f32[1,128,128]{2,1,0:T(8,128)S(1)}, f32[1,128,128]{2,1,0:T(8,128)S(1)},...) custom-call(s32[4]{0:T(128)S(1)} %add_convert_fusion.edges, ...), custom_call_target="tpu_custom_call" | custom-call | flops 8388608 | bytes 4194304 | tf_op jit(solution)/shard_map/pallas_call | solution.py:483
  38.7 5.2 %collective-permute-start.9 = (f32[3,32,128]{2,1,0:T(8,128)S(1)}, f32[3,32,128]{2,1,0:T(8,128)S(1)}, u32[]{:S(2)}, u32[]{:S(2)}) collective-permute-start(f32[3,32,128]{2,1,0:T(8,128)S(1)} %get-tuple-element.80.message), channel_id=1, source_target_pairs={{1,0},{2,1},{3,2},{4,3},{5,4},{6,5},{7,6},{8,7},{9,8},{10,9},{11,1... | collective-permute-start | bytes 147464 | tf_op jit(solution)/shard_map/ppermute | solution.py:479
  43.9 1.2 %collective-permute-done.9.right = f32[3,32,128]{2,1,0:T(8,128)S(1)} collective-permute-done((f32[3,32,128]{2,1,0:T(8,128)S(1)}, f32[3,32,128]{2,1,0:T(8,128)S(1)}, u32[]{:S(2)}, u32[]{:S(2)}) %collective-permute-start.9) | collective-permute-done | bytes 49184 | tf_op jit(solution)/shard_map/ppermute | solution.py:479
  45.1 5.1 %collective-permute-done.8.left = f32[3,32,128]{2,1,0:T(8,128)S(1)} collective-permute-done((f32[3,32,128]{2,1,0:T(8,128)S(1)}, f32[3,32,128]{2,1,0:T(8,128)S(1)}, u32[]{:S(2)}, u32[]{:S(2)}) %collective-permute-start.8) | collective-permute-done | bytes 49184 | tf_op jit(solution)/shard_map/ppermute | solution.py:479
  50.2 0.6 %shard_map.53.wide = f32[3,32,128]{2,1,0:T(8,128)S(1)} custom-call(s32[4]{0:T(128)S(1)} %add_convert_fusion.edges, f32[3,32,128]{2,1,0:T(8,128)S(1)} %get-tuple-element.80.message, f32[3,32,128]{2,1,0:T(8,128)S(1)} %collective-permute-done.8.left, f32[3,32,128]{2,1,0:T(8,128)S(1)} %collective-permute-done.9.right), custom_call_target="tpu_custom_call" | custom-call | flops 8388608 | bytes 4194304 | tf_op jit(solution)/shard_map/pallas_call | solution.py:483
  50.8 0.0 collective-permute-start.11
  50.8 2.9 %collective-permute-start.10 = (f32[3,32,128]{2,1,0:T(8,128)S(1)}, f32[3,32,128]{2,1,0:T(8,128)S(1)}, u32[]{:S(2)}, u32[]{:S(2)}) collective-permute-start(f32[3,32,128]{2,1,0:T(8,128)S(1)} %shard_map.53.wide), channel_id=1, source_target_pairs={{0,16},{16,32},{32,48},{48,64},{64,80},{80,96},{96,112},{112,128},... | collective-permute-start | bytes 147464 | tf_op jit(solution)/shard_map/ppermute | solution.py:479
  53.8 1.8 %collective-permute-done.11.lower = f32[3,32,128]{2,1,0:T(8,128)S(1)} collective-permute-done((f32[3,32,128]{2,1,0:T(8,128)S(1)}, f32[3,32,128]{2,1,0:T(8,128)S(1)}, u32[]{:S(2)}, u32[]{:S(2)}) %collective-permute-start.11) | collective-permute-done | bytes 49184 | tf_op jit(solution)/shard_map/ppermute | solution.py:479
  55.6 5.5 %shard_map.54 = f32[256,256]{1,0:T(8,128)} custom-call(s32[4]{0:T(128)S(1)} %add_convert_fusion.edges, f32[3,32,128]{2,1,0:T(8,128)S(1)} %shard_map.53.wide, f32[3,32,128]{2,1,0:T(8,128)S(1)} %collective-permute-done.10.upper, f32[3,32,128]{2,1,0:T(8,128)S(1)} %collective-permute-done.11.lower, f32[3,336,128]{2,1,0:T(8,128)S(1)} %get-tuple-element.81.refs_0_, ...), custom_call_target="tpu_custom_call" | custom-call | flops 41943040 | bytes 12582912 | tf_op jit(solution)/shard_map/pallas_call | solution.py:538
  (2 shorter events, 0.0 us)
Async XLA Ops:
  2.7 6.8 %collective-permute-start = (f32[128,128]{1,0:T(8,128)S(1)}, f32[128,128]{1,0:T(8,128)S(1)}, u32[]{:S(2)}, u32[]{:S(2)}) collective-permute-start(f32[128,128]{1,0:T(8,128)S(1)} %get-tuple-element.56), channel_id=1, source_target_pairs={{0,1},{1,2},{2,3},{3,4},{4,5},{5,6},{6,7},{7,8},{8,9},{9,10},{10,1... | collective-permute-start | bytes 196616 | tf_op jit(solution)/shard_map/ppermute | solution.py:479
  4.1 5.4 %collective-permute-start.1 = (f32[128,128]{1,0:T(8,128)S(1)}, f32[128,128]{1,0:T(8,128)S(1)}, u32[]{:S(2)}, u32[]{:S(2)}) collective-permute-start(f32[128,128]{1,0:T(8,128)S(1)} %get-tuple-element.57), channel_id=1, source_target_pairs={{1,0},{2,1},{3,2},{4,3},{5,4},{6,5},{7,6},{8,7},{9,8},{10,9},{11,1... | collective-permute-start | bytes 196616 | tf_op jit(solution)/shard_map/ppermute | solution.py:479
  10.1 6.7 %collective-permute-start.2 = (f32[4,3,16,128]{3,2,1,0:T(8,128)S(1)}, f32[4,3,16,128]{3,2,1,0:T(8,128)S(1)}, u32[]{:S(2)}, u32[]{:S(2)}) collective-permute-start(f32[4,3,16,128]{3,2,1,0:T(8,128)S(1)} %get-tuple-element.59), channel_id=1, source_target_pairs={{0,16},{16,32},{32,48},{48,64},{64,80},{80,96},{96,112},{112,128},... | collective-permute-start | bytes 294920 | tf_op jit(solution)/shard_map/ppermute | solution.py:479
  14.4 5.3 %collective-permute-start.3 = (f32[4,3,16,128]{3,2,1,0:T(8,128)S(1)}, f32[4,3,16,128]{3,2,1,0:T(8,128)S(1)}, u32[]{:S(2)}, u32[]{:S(2)}) collective-permute-start(f32[4,3,16,128]{3,2,1,0:T(8,128)S(1)} %get-tuple-element.60), channel_id=1, source_target_pairs={{16,0},{32,16},{48,32},{64,48},{80,64},{96,80},{112,96},{128,112},... | collective-permute-start | bytes 294920 | tf_op jit(solution)/shard_map/ppermute | solution.py:479
  23.9 6.4 %collective-permute-start.4 = (f32[64,128]{1,0:T(8,128)S(1)}, f32[64,128]{1,0:T(8,128)S(1)}, u32[]{:S(2)}, u32[]{:S(2)}) collective-permute-start(f32[64,128]{1,0:T(8,128)S(1)} %get-tuple-element.75), channel_id=1, source_target_pairs={{0,1},{1,2},{2,3},{3,4},{4,5},{5,6},{6,7},{7,8},{8,9},{9,10},{10,1... | collective-permute-start | bytes 98312 | tf_op jit(solution)/shard_map/ppermute | solution.py:479
  23.9 6.4 %collective-permute-start.5 = (f32[64,128]{1,0:T(8,128)S(1)}, f32[64,128]{1,0:T(8,128)S(1)}, u32[]{:S(2)}, u32[]{:S(2)}) collective-permute-start(f32[64,128]{1,0:T(8,128)S(1)} %get-tuple-element.76), channel_id=1, source_target_pairs={{1,0},{2,1},{3,2},{4,3},{5,4},{6,5},{7,6},{8,7},{9,8},{10,9},{11,1... | collective-permute-start | bytes 98312 | tf_op jit(solution)/shard_map/ppermute | solution.py:479
  30.9 2.1 %collective-permute-start.6 = (f32[3,24,128]{2,1,0:T(8,128)S(1)}, f32[3,24,128]{2,1,0:T(8,128)S(1)}, u32[]{:S(2)}, u32[]{:S(2)}) collective-permute-start(f32[3,24,128]{2,1,0:T(8,128)S(1)} %get-tuple-element.78), channel_id=1, source_target_pairs={{0,16},{16,32},{32,48},{48,64},{64,80},{80,96},{96,112},{112,128},... | collective-permute-start | bytes 110600 | tf_op jit(solution)/shard_map/ppermute | solution.py:479
  32.0 4.6 %collective-permute-start.7 = (f32[3,24,128]{2,1,0:T(8,128)S(1)}, f32[3,24,128]{2,1,0:T(8,128)S(1)}, u32[]{:S(2)}, u32[]{:S(2)}) collective-permute-start(f32[3,24,128]{2,1,0:T(8,128)S(1)} %get-tuple-element.79), channel_id=1, source_target_pairs={{16,0},{32,16},{48,32},{64,48},{80,64},{96,80},{112,96},{128,112},... | collective-permute-start | bytes 110600 | tf_op jit(solution)/shard_map/ppermute | solution.py:479
  38.7 6.4 %collective-permute-start.9 = (f32[3,32,128]{2,1,0:T(8,128)S(1)}, f32[3,32,128]{2,1,0:T(8,128)S(1)}, u32[]{:S(2)}, u32[]{:S(2)}) collective-permute-start(f32[3,32,128]{2,1,0:T(8,128)S(1)} %get-tuple-element.80.message), channel_id=1, source_target_pairs={{1,0},{2,1},{3,2},{4,3},{5,4},{6,5},{7,6},{8,7},{9,8},{10,9},{11,1... | collective-permute-start | bytes 147464 | tf_op jit(solution)/shard_map/ppermute | solution.py:479
  43.9 6.3 %collective-permute-start.8 = (f32[3,32,128]{2,1,0:T(8,128)S(1)}, f32[3,32,128]{2,1,0:T(8,128)S(1)}, u32[]{:S(2)}, u32[]{:S(2)}) collective-permute-start(f32[3,32,128]{2,1,0:T(8,128)S(1)} %get-tuple-element.80.message), channel_id=1, source_target_pairs={{0,1},{1,2},{2,3},{3,4},{4,5},{5,6},{6,7},{7,8},{8,9},{9,10},{10,1... | collective-permute-start | bytes 147464 | tf_op jit(solution)/shard_map/ppermute | solution.py:479
  50.8 4.7 %collective-permute-start.11 = (f32[3,32,128]{2,1,0:T(8,128)S(1)}, f32[3,32,128]{2,1,0:T(8,128)S(1)}, u32[]{:S(2)}, u32[]{:S(2)}) collective-permute-start(f32[3,32,128]{2,1,0:T(8,128)S(1)} %shard_map.53.wide), channel_id=1, source_target_pairs={{16,0},{32,16},{48,32},{64,48},{80,64},{96,80},{112,96},{128,112},... | collective-permute-start | bytes 147464 | tf_op jit(solution)/shard_map/ppermute | solution.py:479
  50.8 4.7 %collective-permute-start.10 = (f32[3,32,128]{2,1,0:T(8,128)S(1)}, f32[3,32,128]{2,1,0:T(8,128)S(1)}, u32[]{:S(2)}, u32[]{:S(2)}) collective-permute-start(f32[3,32,128]{2,1,0:T(8,128)S(1)} %shard_map.53.wide), channel_id=1, source_target_pairs={{0,16},{16,32},{32,48},{48,64},{64,80},{80,96},{96,112},{112,128},... | collective-permute-start | bytes 147464 | tf_op jit(solution)/shard_map/ppermute | solution.py:479

commit v6 on v5

--- a/solution.py
+++ b/solution.py
@@ -129,7 +129,7 @@
 
 def coarsen_pass(triples, step, first, last):
     trips = (last - first) // 8
-    height = max(n for n in (1, 2, 4, 6, 8) if trips % n == 0)
+    height = max(n for n in range(1, 9) if trips % n == 0)
 
     def body(row):
         for j in range(height):
@@ -333,13 +333,14 @@
 
     def send(row):
         lane = iota(1)
-        at = pl.ds(row, 8)
-        x = [own2[i, at, :] for i in range(3)]
-        for target, start in ((low2, RIM), (high2, 64)):
-            y = [roll(x[i], RIM * i - start, 1) for i in range(3)]
-            target[at, :] = jnp.where(lane < RIM, y[0], jnp.where(lane < 2 * RIM, y[1], y[2]))
-
-    over_rows(0, 64, 1, send)
+        for j in range(4):
+            at = rows_at(row, j)
+            x = [own2[i, at, :] for i in range(3)]
+            for target, start in ((low2, RIM), (high2, 64)):
+                y = [roll(x[i], RIM * i - start, 1) for i in range(3)]
+                target[at, :] = jnp.where(lane < RIM, y[0], jnp.where(lane < 2 * RIM, y[1], y[2]))
+
+    over_rows(0, 64, 4, send)
 
 
 def join_kernel(edges, own2, left, right, wide, top, bottom):
@@ -374,7 +375,7 @@
             two[name][0, pl.ds(PAD + 8 * j, 8), :] = up
             two[name][0, pl.ds(PAD + RIM + 64 + 8 * j, 8), :] = down
         two[name][0, pl.ds(PAD + RIM, 64), :] = wide[i]
-    smooth_down(two, 0, 112, 7)
+    smooth_down(two, 0, 112, 14)
     coarsen_into(two, (three["k"], three["s"], three["b"]), 0, 56)
     smooth_down(three, 0, 56, 7)
     coarsen_into(three, (four.at[0], four.at[1], four.at[2]), 0, 32)
@@ -412,7 +413,7 @@
         four[name][0, pl.ds(PAD + 44, 18), :] = jnp.where(column < LANES * edges[3], lower[i], 0.0)[10:28]
     clear_rows([four[n] for n in "kvu"], (0, PAD + 64))
     clear_rows([five[n] for n in "kvu"], (0, PAD + 32))
-    smooth_down(four, 0, 64, 4)
+    smooth_down(four, 0, 64, 8)
     coarsen_into(four, (five["k"], five["s"], five["b"]), 0, 32)
     face_pass(five, PAD, PAD + 32, 4)
     v, u = five["v"], five["u"]
@@ -420,8 +421,8 @@
         sweep_pass(five, u, v, PAD, PAD + 32, 4)
         v, u = u, v
     correct_pass(u, four["v"], four["v"], PAD, PAD + 32, PAD)
-    sweep_pass(four, four["v"], four["u"], PAD, PAD + 64, 4)
-    sweep_pass(four, four["u"], four["v"], PAD, PAD + 64, 4)
+    sweep_pass(four, four["v"], four["u"], PAD, PAD + 64, 8)
+    sweep_pass(four, four["u"], four["v"], PAD, PAD + 64, 8)
     from4[0, :, :] = choose(four["v"][0, pl.ds(PAD + 16, 32), :], pick(lambda r, c: r == c // 4 + 18))
 
     def rise(depth, coarse, first, last, shift, start, stop, height, twice=True):
@@ -435,7 +436,7 @@
         return c
 
     c = rise(3, from4, 0, 32, -4, 8, 64, 7)
-    c = rise(2, c, 8, 64, 8, 24, 104, 5)
+    c = rise(2, c, 8, 64, 8, 24, 104, 10)
     fine = c[0, pl.ds(24, 80), :]
     for t in range(3):
         turn = lambda c: jnp.where(c < 64, 0, 96) if t == 2 else 0

time: 61.1 us -> 59.2 us (0.969)
  Pallas kernels: 20.4 us -> 18.4 us
    pallas_call x7, Pallas kernels: 12.2 us -> 11 us  [call(): pl.pallas_call(kernel, out_shape=tuple((shape_of(*shape) for shape in out...]
    pallas_call x1, Pallas kernels: 5.49 us -> 4.76 us  [per_device(): pl.pallas_call(up_kernel, out_shape=shape_of(SIZE, SIZE), in_specs=[SCALA...]
where the time goes in v6:
time: 59.2 us; the launch traced here: 59.1 us
  starting transfers between devices  23.8 us (40%)
  Pallas kernels  18.4 us (31%)
  waiting for transfers between devices  16.7 us (28%)
    ppermute x6, starting transfers between devices, exchange(): lax.ppermute(down_block, axis, down)  14.1 us
    pallas_call x7, Pallas kernels, call(): pl.pallas_call(kernel, out_shape=tuple((shape_of(*shape) for shape in out...  11 us
    ppermute x6, starting transfers between devices, exchange(): lax.ppermute(up_block, axis, up)  9.73 us
    ppermute x6, waiting for transfers between devices, exchange(): lax.ppermute(down_block, axis, down)  9.33 us
    ppermute x6, waiting for transfers between devices, exchange(): lax.ppermute(up_block, axis, up)  7.36 us
    pallas_call x1, Pallas kernels, per_device(): pl.pallas_call(up_kernel, out_shape=shape_of(SIZE, SIZE), in_specs=[SCALA...  4.76 us
    pallas_call x1, Pallas kernels, per_device(): pl.pallas_call(pack_kernel, out_shape=(shape_of(4, 2, SIZE, LANES), shape...  2.69 us
  transfers between devices with their start and end apart: 12, of which 7 were waited for; matrix products, arithmetic and copies ran while one was open for 0% of the time, Pallas kernels for 7%

profile of v6, /device:TPU:97, one launch (start us, length us, event | category | flops | bytes accessed | tf_op | source)
XLA Modules:
  0.0 59.1 jit_solution(5590397965363824307)
XLA Ops:
  0.0 2.7 %shard_map.46 = (f32[4,2,256,128]{3,2,1,0:T(8,128)S(1)}, f32[128,128]{1,0:T(8,128)S(1)}, f32[128,128]{1,0:T(8,128)S(1)}) custom-call(f32[256,256]{1,0:T(8,128)} %k.1, f32[256,256]{1,0:T(8,128)} %s.1, f32[256,256]{1,0:T(8,128)} %b.1, f32[256,256]{1,0:T(8,128)} %v.1), custom_call_target="tpu_custom_call" | custom-call | flops 2097152 | bytes 2097152 | tf_op jit(solution)/shard_map/pallas_call | solution.py:501
  2.7 1.4 %collective-permute-start = (f32[128,128]{1,0:T(8,128)S(1)}, f32[128,128]{1,0:T(8,128)S(1)}, u32[]{:S(2)}, u32[]{:S(2)}) collective-permute-start(f32[128,128]{1,0:T(8,128)S(1)} %get-tuple-element.56), channel_id=1, source_target_pairs={{0,1},{1,2},{2,3},{3,4},{4,5},{5,6},{6,7},{7,8},{8,9},{9,10},{10,1... | collective-permute-start | bytes 196616 | tf_op jit(solution)/shard_map/ppermute | solution.py:480
  4.1 3.7 %collective-permute-start.1 = (f32[128,128]{1,0:T(8,128)S(1)}, f32[128,128]{1,0:T(8,128)S(1)}, u32[]{:S(2)}, u32[]{:S(2)}) collective-permute-start(f32[128,128]{1,0:T(8,128)S(1)} %get-tuple-element.57), channel_id=1, source_target_pairs={{1,0},{2,1},{3,2},{4,3},{5,4},{6,5},{7,6},{8,7},{9,8},{10,9},{11,1... | collective-permute-start | bytes 196616 | tf_op jit(solution)/shard_map/ppermute | solution.py:480
  7.8 0.1 add_convert_fusion.edges
  7.9 1.6 %shard_map.47 = (f32[3,176,128]{2,1,0:T(8,128)S(1)}, f32[3,176,128]{2,1,0:T(8,128)S(1)}, f32[2,64,128]{2,1,0:T(8,128)S(1)}, f32[2,64,128]{2,1,0:T(8,128)S(1)}) custom-call(s32[4]{0:T(128)S(1)} %add_convert_fusion.edges, f32[4,2,256,128]{3,2,1,0:T(8,128)S(1)} %get-tuple-element.55.own), custom_call_target="tpu_custom_call" | custom-call | flops 8388608 | bytes 4194304 | tf_op jit(solution)/shard_map/pallas_call | solution.py:484
  9.5 0.0 collective-permute-done.before
  9.5 0.0 collective-permute-done.1.after
  9.5 0.6 %shard_map.48 = (f32[4,3,16,128]{3,2,1,0:T(8,128)S(1)}, f32[4,3,16,128]{3,2,1,0:T(8,128)S(1)}) custom-call(s32[4]{0:T(128)S(1)} %add_convert_fusion.edges, f32[4,2,256,128]{3,2,1,0:T(8,128)S(1)} %get-tuple-element.55.own, f32[128,128]{1,0:T(8,128)S(1)} %collective-permute-done.before, f32[128,128]{1,0:T(8,128)S(1)} %collective-permute-done.1.after, ...), custom_call_target="tpu_custom_call" | custom-call | flops 8388608 | bytes 4194304 | tf_op jit(solution)/shard_map/pallas_call | solution.py:484
  10.1 4.3 %collective-permute-start.2 = (f32[4,3,16,128]{3,2,1,0:T(8,128)S(1)}, f32[4,3,16,128]{3,2,1,0:T(8,128)S(1)}, u32[]{:S(2)}, u32[]{:S(2)}) collective-permute-start(f32[4,3,16,128]{3,2,1,0:T(8,128)S(1)} %get-tuple-element.59), channel_id=1, source_target_pairs={{0,16},{16,32},{32,48},{48,64},{64,80},{80,96},{96,112},{112,128},... | collective-permute-start | bytes 294920 | tf_op jit(solution)/shard_map/ppermute | solution.py:480
  14.4 0.0 collective-permute-start.3
  14.4 2.4 %shard_map.49 = (f32[3,336,128]{2,1,0:T(8,128)S(1)}, f32[3,336,128]{2,1,0:T(8,128)S(1)}, f32[3,336,128]{2,1,0:T(8,128)S(1)}, f32[3,336,128]{2,1,0:T(8,128)S(1)},...) custom-call(s32[4]{0:T(128)S(1)} %add_convert_fusion.edges, ...), custom_call_target="tpu_custom_call" | custom-call | flops 8388608 | bytes 4194304 | tf_op jit(solution)/shard_map/pallas_call | solution.py:484
  16.8 0.0 collective-permute-done.2.above
  16.8 2.9 %collective-permute-done.3.below = f32[4,3,16,128]{3,2,1,0:T(8,128)S(1)} collective-permute-done((f32[4,3,16,128]{3,2,1,0:T(8,128)S(1)}, f32[4,3,16,128]{3,2,1,0:T(8,128)S(1)}, u32[]{:S(2)}, u32[]{:S(2)}) %collective-permute-start.3) | collective-permute-done | bytes 98336 | tf_op jit(solution)/shard_map/ppermute | solution.py:480
  19.7 3.8 %shard_map.50 = (f32[3,336,128]{2,1,0:T(8,128)S(1)}, f32[3,336,128]{2,1,0:T(8,128)S(1)}, f32[3,336,128]{2,1,0:T(8,128)S(1)}, f32[3,336,128]{2,1,0:T(8,128)S(1)},...) custom-call(s32[4]{0:T(128)S(1)} %add_convert_fusion.edges, ...), custom_call_target="tpu_custom_call", output_to_operand_aliasing={{0}: (3, {}), {1}: (4, {}), {2}: (5, {}), {3}: (6, {}), {4}... | custom-call | flops 8388608 | bytes 4194304 | tf_op jit(solution)/shard_map/pallas_call | solution.py:484
  23.5 0.1 collective-permute-start.4
  23.6 5.1 %collective-permute-start.5 = (f32[64,128]{1,0:T(8,128)S(1)}, f32[64,128]{1,0:T(8,128)S(1)}, u32[]{:S(2)}, u32[]{:S(2)}) collective-permute-start(f32[64,128]{1,0:T(8,128)S(1)} %get-tuple-element.76), channel_id=1, source_target_pairs={{1,0},{2,1},{3,2},{4,3},{5,4},{6,5},{7,6},{8,7},{9,8},{10,9},{11,1... | collective-permute-start | bytes 98312 | tf_op jit(solution)/shard_map/ppermute | solution.py:480
  28.7 1.2 %collective-permute-done.4.left = f32[64,128]{1,0:T(8,128)S(1)} collective-permute-done((f32[64,128]{1,0:T(8,128)S(1)}, f32[64,128]{1,0:T(8,128)S(1)}, u32[]{:S(2)}, u32[]{:S(2)}) %collective-permute-start.4) | collective-permute-done | bytes 32800 | tf_op jit(solution)/shard_map/ppermute | solution.py:480
  29.9 0.6 %shard_map.51 = (f32[3,64,128]{2,1,0:T(8,128)S(1)}, f32[3,24,128]{2,1,0:T(8,128)S(1)}, f32[3,24,128]{2,1,0:T(8,128)S(1)}) custom-call(s32[4]{0:T(128)S(1)} %add_convert_fusion.edges, f32[3,64,128]{2,1,0:T(8,128)S(1)} %get-tuple-element.74.own2, f32[64,128]{1,0:T(8,128)S(1)} %collective-permute-done.4.left, f32[64,128]{1,0:T(8,128)S(1)} %collective-permute-done.5.right), custom_call_target="tpu_custom_call" | custom-call | flops 8388608 | bytes 4194304 | tf_op jit(solution)/shard_map/pallas_call | solution.py:484
  30.6 1.0 %collective-permute-start.6 = (f32[3,24,128]{2,1,0:T(8,128)S(1)}, f32[3,24,128]{2,1,0:T(8,128)S(1)}, u32[]{:S(2)}, u32[]{:S(2)}) collective-permute-start(f32[3,24,128]{2,1,0:T(8,128)S(1)} %get-tuple-element.78), channel_id=1, source_target_pairs={{0,16},{16,32},{32,48},{48,64},{64,80},{80,96},{96,112},{112,128},... | collective-permute-start | bytes 110600 | tf_op jit(solution)/shard_map/ppermute | solution.py:480
  31.6 0.0 collective-permute-start.7
  31.6 1.1 %collective-permute-done.6.above = f32[3,24,128]{2,1,0:T(8,128)S(1)} collective-permute-done((f32[3,24,128]{2,1,0:T(8,128)S(1)}, f32[3,24,128]{2,1,0:T(8,128)S(1)}, u32[]{:S(2)}, u32[]{:S(2)}) %collective-permute-start.6) | collective-permute-done | bytes 36896 | tf_op jit(solution)/shard_map/ppermute | solution.py:480
  32.7 3.5 %collective-permute-done.7.below = f32[3,24,128]{2,1,0:T(8,128)S(1)} collective-permute-done((f32[3,24,128]{2,1,0:T(8,128)S(1)}, f32[3,24,128]{2,1,0:T(8,128)S(1)}, u32[]{:S(2)}, u32[]{:S(2)}) %collective-permute-start.7) | collective-permute-done | bytes 36896 | tf_op jit(solution)/shard_map/ppermute | solution.py:480
  36.2 1.3 %shard_map.52 = (f32[1,128,128]{2,1,0:T(8,128)S(1)}, f32[1,128,128]{2,1,0:T(8,128)S(1)}, f32[1,128,128]{2,1,0:T(8,128)S(1)}, f32[1,128,128]{2,1,0:T(8,128)S(1)},...) custom-call(s32[4]{0:T(128)S(1)} %add_convert_fusion.edges, ...), custom_call_target="tpu_custom_call" | custom-call | flops 8388608 | bytes 4194304 | tf_op jit(solution)/shard_map/pallas_call | solution.py:484
  37.5 5.2 %collective-permute-start.9 = (f32[3,32,128]{2,1,0:T(8,128)S(1)}, f32[3,32,128]{2,1,0:T(8,128)S(1)}, u32[]{:S(2)}, u32[]{:S(2)}) collective-permute-start(f32[3,32,128]{2,1,0:T(8,128)S(1)} %get-tuple-element.80.message), channel_id=1, source_target_pairs={{1,0},{2,1},{3,2},{4,3},{5,4},{6,5},{7,6},{8,7},{9,8},{10,9},{11,1... | collective-permute-start | bytes 147464 | tf_op jit(solution)/shard_map/ppermute | solution.py:480
  42.7 1.2 %collective-permute-done.9.right = f32[3,32,128]{2,1,0:T(8,128)S(1)} collective-permute-done((f32[3,32,128]{2,1,0:T(8,128)S(1)}, f32[3,32,128]{2,1,0:T(8,128)S(1)}, u32[]{:S(2)}, u32[]{:S(2)}) %collective-permute-start.9) | collective-permute-done | bytes 49184 | tf_op jit(solution)/shard_map/ppermute | solution.py:480
  43.9 5.1 %collective-permute-done.8.left = f32[3,32,128]{2,1,0:T(8,128)S(1)} collective-permute-done((f32[3,32,128]{2,1,0:T(8,128)S(1)}, f32[3,32,128]{2,1,0:T(8,128)S(1)}, u32[]{:S(2)}, u32[]{:S(2)}) %collective-permute-start.8) | collective-permute-done | bytes 49184 | tf_op jit(solution)/shard_map/ppermute | solution.py:480
  49.0 0.6 %shard_map.53.wide = f32[3,32,128]{2,1,0:T(8,128)S(1)} custom-call(s32[4]{0:T(128)S(1)} %add_convert_fusion.edges, f32[3,32,128]{2,1,0:T(8,128)S(1)} %get-tuple-element.80.message, f32[3,32,128]{2,1,0:T(8,128)S(1)} %collective-permute-done.8.left, f32[3,32,128]{2,1,0:T(8,128)S(1)} %collective-permute-done.9.right), custom_call_target="tpu_custom_call" | custom-call | flops 8388608 | bytes 4194304 | tf_op jit(solution)/shard_map/pallas_call | solution.py:484
  49.6 0.0 collective-permute-start.11
  49.7 2.9 %collective-permute-start.10 = (f32[3,32,128]{2,1,0:T(8,128)S(1)}, f32[3,32,128]{2,1,0:T(8,128)S(1)}, u32[]{:S(2)}, u32[]{:S(2)}) collective-permute-start(f32[3,32,128]{2,1,0:T(8,128)S(1)} %shard_map.53.wide), channel_id=1, source_target_pairs={{0,16},{16,32},{32,48},{48,64},{64,80},{80,96},{96,112},{112,128},... | collective-permute-start | bytes 147464 | tf_op jit(solution)/shard_map/ppermute | solution.py:480
  52.6 1.8 %collective-permute-done.11.lower = f32[3,32,128]{2,1,0:T(8,128)S(1)} collective-permute-done((f32[3,32,128]{2,1,0:T(8,128)S(1)}, f32[3,32,128]{2,1,0:T(8,128)S(1)}, u32[]{:S(2)}, u32[]{:S(2)}) %collective-permute-start.11) | collective-permute-done | bytes 49184 | tf_op jit(solution)/shard_map/ppermute | solution.py:480
  54.4 0.0 collective-permute-done.10.upper
  54.4 4.8 %shard_map.54 = f32[256,256]{1,0:T(8,128)} custom-call(s32[4]{0:T(128)S(1)} %add_convert_fusion.edges, f32[3,32,128]{2,1,0:T(8,128)S(1)} %shard_map.53.wide, f32[3,32,128]{2,1,0:T(8,128)S(1)} %collective-permute-done.10.upper, f32[3,32,128]{2,1,0:T(8,128)S(1)} %collective-permute-done.11.lower, f32[3,336,128]{2,1,0:T(8,128)S(1)} %get-tuple-element.81.refs_0_, ...), custom_call_target="tpu_custom_call" | custom-call | flops 41943040 | bytes 12582912 | tf_op jit(solution)/shard_map/pallas_call | solution.py:539
  (2 shorter events, 0.0 us)
Async XLA Ops:
  2.7 6.8 %collective-permute-start = (f32[128,128]{1,0:T(8,128)S(1)}, f32[128,128]{1,0:T(8,128)S(1)}, u32[]{:S(2)}, u32[]{:S(2)}) collective-permute-start(f32[128,128]{1,0:T(8,128)S(1)} %get-tuple-element.56), channel_id=1, source_target_pairs={{0,1},{1,2},{2,3},{3,4},{4,5},{5,6},{6,7},{7,8},{8,9},{9,10},{10,1... | collective-permute-start | bytes 196616 | tf_op jit(solution)/shard_map/ppermute | solution.py:480
  4.1 5.4 %collective-permute-start.1 = (f32[128,128]{1,0:T(8,128)S(1)}, f32[128,128]{1,0:T(8,128)S(1)}, u32[]{:S(2)}, u32[]{:S(2)}) collective-permute-start(f32[128,128]{1,0:T(8,128)S(1)} %get-tuple-element.57), channel_id=1, source_target_pairs={{1,0},{2,1},{3,2},{4,3},{5,4},{6,5},{7,6},{8,7},{9,8},{10,9},{11,1... | collective-permute-start | bytes 196616 | tf_op jit(solution)/shard_map/ppermute | solution.py:480
  10.1 6.7 %collective-permute-start.2 = (f32[4,3,16,128]{3,2,1,0:T(8,128)S(1)}, f32[4,3,16,128]{3,2,1,0:T(8,128)S(1)}, u32[]{:S(2)}, u32[]{:S(2)}) collective-permute-start(f32[4,3,16,128]{3,2,1,0:T(8,128)S(1)} %get-tuple-element.59), channel_id=1, source_target_pairs={{0,16},{16,32},{32,48},{48,64},{64,80},{80,96},{96,112},{112,128},... | collective-permute-start | bytes 294920 | tf_op jit(solution)/shard_map/ppermute | solution.py:480
  14.4 5.3 %collective-permute-start.3 = (f32[4,3,16,128]{3,2,1,0:T(8,128)S(1)}, f32[4,3,16,128]{3,2,1,0:T(8,128)S(1)}, u32[]{:S(2)}, u32[]{:S(2)}) collective-permute-start(f32[4,3,16,128]{3,2,1,0:T(8,128)S(1)} %get-tuple-element.60), channel_id=1, source_target_pairs={{16,0},{32,16},{48,32},{64,48},{80,64},{96,80},{112,96},{128,112},... | collective-permute-start | bytes 294920 | tf_op jit(solution)/shard_map/ppermute | solution.py:480
  23.5 6.4 %collective-permute-start.4 = (f32[64,128]{1,0:T(8,128)S(1)}, f32[64,128]{1,0:T(8,128)S(1)}, u32[]{:S(2)}, u32[]{:S(2)}) collective-permute-start(f32[64,128]{1,0:T(8,128)S(1)} %get-tuple-element.75), channel_id=1, source_target_pairs={{0,1},{1,2},{2,3},{3,4},{4,5},{5,6},{6,7},{7,8},{8,9},{9,10},{10,1... | collective-permute-start | bytes 98312 | tf_op jit(solution)/shard_map/ppermute | solution.py:480
  23.6 6.4 %collective-permute-start.5 = (f32[64,128]{1,0:T(8,128)S(1)}, f32[64,128]{1,0:T(8,128)S(1)}, u32[]{:S(2)}, u32[]{:S(2)}) collective-permute-start(f32[64,128]{1,0:T(8,128)S(1)} %get-tuple-element.76), channel_id=1, source_target_pairs={{1,0},{2,1},{3,2},{4,3},{5,4},{6,5},{7,6},{8,7},{9,8},{10,9},{11,1... | collective-permute-start | bytes 98312 | tf_op jit(solution)/shard_map/ppermute | solution.py:480
  30.6 2.1 %collective-permute-start.6 = (f32[3,24,128]{2,1,0:T(8,128)S(1)}, f32[3,24,128]{2,1,0:T(8,128)S(1)}, u32[]{:S(2)}, u32[]{:S(2)}) collective-permute-start(f32[3,24,128]{2,1,0:T(8,128)S(1)} %get-tuple-element.78), channel_id=1, source_target_pairs={{0,16},{16,32},{32,48},{48,64},{64,80},{80,96},{96,112},{112,128},... | collective-permute-start | bytes 110600 | tf_op jit(solution)/shard_map/ppermute | solution.py:480
  31.6 4.6 %collective-permute-start.7 = (f32[3,24,128]{2,1,0:T(8,128)S(1)}, f32[3,24,128]{2,1,0:T(8,128)S(1)}, u32[]{:S(2)}, u32[]{:S(2)}) collective-permute-start(f32[3,24,128]{2,1,0:T(8,128)S(1)} %get-tuple-element.79), channel_id=1, source_target_pairs={{16,0},{32,16},{48,32},{64,48},{80,64},{96,80},{112,96},{128,112},... | collective-permute-start | bytes 110600 | tf_op jit(solution)/shard_map/ppermute | solution.py:480
  37.5 6.4 %collective-permute-start.9 = (f32[3,32,128]{2,1,0:T(8,128)S(1)}, f32[3,32,128]{2,1,0:T(8,128)S(1)}, u32[]{:S(2)}, u32[]{:S(2)}) collective-permute-start(f32[3,32,128]{2,1,0:T(8,128)S(1)} %get-tuple-element.80.message), channel_id=1, source_target_pairs={{1,0},{2,1},{3,2},{4,3},{5,4},{6,5},{7,6},{8,7},{9,8},{10,9},{11,1... | collective-permute-start | bytes 147464 | tf_op jit(solution)/shard_map/ppermute | solution.py:480
  42.7 6.3 %collective-permute-start.8 = (f32[3,32,128]{2,1,0:T(8,128)S(1)}, f32[3,32,128]{2,1,0:T(8,128)S(1)}, u32[]{:S(2)}, u32[]{:S(2)}) collective-permute-start(f32[3,32,128]{2,1,0:T(8,128)S(1)} %get-tuple-element.80.message), channel_id=1, source_target_pairs={{0,1},{1,2},{2,3},{3,4},{4,5},{5,6},{6,7},{7,8},{8,9},{9,10},{10,1... | collective-permute-start | bytes 147464 | tf_op jit(solution)/shard_map/ppermute | solution.py:480
  49.6 4.7 %collective-permute-start.11 = (f32[3,32,128]{2,1,0:T(8,128)S(1)}, f32[3,32,128]{2,1,0:T(8,128)S(1)}, u32[]{:S(2)}, u32[]{:S(2)}) collective-permute-start(f32[3,32,128]{2,1,0:T(8,128)S(1)} %shard_map.53.wide), channel_id=1, source_target_pairs={{16,0},{32,16},{48,32},{64,48},{80,64},{96,80},{112,96},{128,112},... | collective-permute-start | bytes 147464 | tf_op jit(solution)/shard_map/ppermute | solution.py:480
  49.7 4.7 %collective-permute-start.10 = (f32[3,32,128]{2,1,0:T(8,128)S(1)}, f32[3,32,128]{2,1,0:T(8,128)S(1)}, u32[]{:S(2)}, u32[]{:S(2)}) collective-permute-start(f32[3,32,128]{2,1,0:T(8,128)S(1)} %shard_map.53.wide), channel_id=1, source_target_pairs={{0,16},{16,32},{32,48},{48,64},{64,80},{80,96},{96,112},{112,128},... | collective-permute-start | bytes 147464 | tf_op jit(solution)/shard_map/ppermute | solution.py:480

commit v7 on v6

--- a/solution.py
+++ b/solution.py
@@ -318,7 +318,7 @@
     first = [(source.at[pl.ds(0, 2)], target.at[pl.ds(0, 2)], factor) for source, target, factor in pairs]
     coarsen_pass(first, 1, 8, 16)
     coarsen_pass(first, 1, 144, 152)
-    smooth_down(one, 8, 152, 6)
+    smooth_down(one, 8, 152, 18)
     coarsen_pass([(one["u"].at[pl.ds(0, 2)], b2, 1.0)], 2, 8, 72)
 
     total = None
@@ -441,7 +441,7 @@
     for t in range(3):
         turn = lambda c: jnp.where(c < 64, 0, 96) if t == 2 else 0
         coarse_fine[t, :, :] = choose(fine, pick(lambda r, c: r == (c + LANES * t) // 4 + RIM - turn(c)))
-    c = rise(1, coarse_fine, 0, 80, -8, 16, 160, 6)
+    c = rise(1, coarse_fine, 0, 80, -8, 16, 160, 18)
     rise(0, c, 16, 160, 8, 24, 312, 12, False)
 
     level = levels[0]

time: 59.2 us -> 58.3 us (0.985)
  Pallas kernels: 18.4 us -> 17.5 us
    pallas_call x7, Pallas kernels: 11 us -> 10.3 us  [call(): pl.pallas_call(kernel, out_shape=tuple((shape_of(*shape) for shape in out...]
where the time goes in v7:
time: 58.3 us; the launch traced here: 58.2 us
  starting transfers between devices  23.8 us (41%)
  Pallas kernels  17.5 us (30%)
  waiting for transfers between devices  16.7 us (29%)
    ppermute x6, starting transfers between devices, exchange(): lax.ppermute(down_block, axis, down)  14.1 us
    pallas_call x7, Pallas kernels, call(): pl.pallas_call(kernel, out_shape=tuple((shape_of(*shape) for shape in out...  10.3 us
    ppermute x6, starting transfers between devices, exchange(): lax.ppermute(up_block, axis, up)  9.73 us
    ppermute x6, waiting for transfers between devices, exchange(): lax.ppermute(down_block, axis, down)  9.33 us
    ppermute x6, waiting for transfers between devices, exchange(): lax.ppermute(up_block, axis, up)  7.36 us
    pallas_call x1, Pallas kernels, per_device(): pl.pallas_call(up_kernel, out_shape=shape_of(SIZE, SIZE), in_specs=[SCALA...  4.44 us
    pallas_call x1, Pallas kernels, per_device(): pl.pallas_call(pack_kernel, out_shape=(shape_of(4, 2, SIZE, LANES), shape...  2.69 us
  transfers between devices with their start and end apart: 12, of which 7 were waited for; matrix products, arithmetic and copies ran while one was open for 0% of the time, Pallas kernels for 7%

profile of v7, /device:TPU:97, one launch (start us, length us, event | category | flops | bytes accessed | tf_op | source)
XLA Modules:
  0.0 58.2 jit_solution(3107656889834304836)
XLA Ops:
  0.0 2.7 %shard_map.46 = (f32[4,2,256,128]{3,2,1,0:T(8,128)S(1)}, f32[128,128]{1,0:T(8,128)S(1)}, f32[128,128]{1,0:T(8,128)S(1)}) custom-call(f32[256,256]{1,0:T(8,128)} %k.1, f32[256,256]{1,0:T(8,128)} %s.1, f32[256,256]{1,0:T(8,128)} %b.1, f32[256,256]{1,0:T(8,128)} %v.1), custom_call_target="tpu_custom_call" | custom-call | flops 2097152 | bytes 2097152 | tf_op jit(solution)/shard_map/pallas_call | solution.py:501
  2.7 1.4 %collective-permute-start = (f32[128,128]{1,0:T(8,128)S(1)}, f32[128,128]{1,0:T(8,128)S(1)}, u32[]{:S(2)}, u32[]{:S(2)}) collective-permute-start(f32[128,128]{1,0:T(8,128)S(1)} %get-tuple-element.56), channel_id=1, source_target_pairs={{0,1},{1,2},{2,3},{3,4},{4,5},{5,6},{6,7},{7,8},{8,9},{9,10},{10,1... | collective-permute-start | bytes 196616 | tf_op jit(solution)/shard_map/ppermute | solution.py:480
  4.1 3.7 %collective-permute-start.1 = (f32[128,128]{1,0:T(8,128)S(1)}, f32[128,128]{1,0:T(8,128)S(1)}, u32[]{:S(2)}, u32[]{:S(2)}) collective-permute-start(f32[128,128]{1,0:T(8,128)S(1)} %get-tuple-element.57), channel_id=1, source_target_pairs={{1,0},{2,1},{3,2},{4,3},{5,4},{6,5},{7,6},{8,7},{9,8},{10,9},{11,1... | collective-permute-start | bytes 196616 | tf_op jit(solution)/shard_map/ppermute | solution.py:480
  7.8 0.1 add_convert_fusion.edges
  7.9 1.6 %shard_map.47 = (f32[3,176,128]{2,1,0:T(8,128)S(1)}, f32[3,176,128]{2,1,0:T(8,128)S(1)}, f32[2,64,128]{2,1,0:T(8,128)S(1)}, f32[2,64,128]{2,1,0:T(8,128)S(1)}) custom-call(s32[4]{0:T(128)S(1)} %add_convert_fusion.edges, f32[4,2,256,128]{3,2,1,0:T(8,128)S(1)} %get-tuple-element.55.own), custom_call_target="tpu_custom_call" | custom-call | flops 8388608 | bytes 4194304 | tf_op jit(solution)/shard_map/pallas_call | solution.py:484
  9.5 0.0 collective-permute-done.before
  9.5 0.0 collective-permute-done.1.after
  9.5 0.6 %shard_map.48 = (f32[4,3,16,128]{3,2,1,0:T(8,128)S(1)}, f32[4,3,16,128]{3,2,1,0:T(8,128)S(1)}) custom-call(s32[4]{0:T(128)S(1)} %add_convert_fusion.edges, f32[4,2,256,128]{3,2,1,0:T(8,128)S(1)} %get-tuple-element.55.own, f32[128,128]{1,0:T(8,128)S(1)} %collective-permute-done.before, f32[128,128]{1,0:T(8,128)S(1)} %collective-permute-done.1.after, ...), custom_call_target="tpu_custom_call" | custom-call | flops 8388608 | bytes 4194304 | tf_op jit(solution)/shard_map/pallas_call | solution.py:484
  10.1 4.3 %collective-permute-start.2 = (f32[4,3,16,128]{3,2,1,0:T(8,128)S(1)}, f32[4,3,16,128]{3,2,1,0:T(8,128)S(1)}, u32[]{:S(2)}, u32[]{:S(2)}) collective-permute-start(f32[4,3,16,128]{3,2,1,0:T(8,128)S(1)} %get-tuple-element.59), channel_id=1, source_target_pairs={{0,16},{16,32},{32,48},{48,64},{64,80},{80,96},{96,112},{112,128},... | collective-permute-start | bytes 294920 | tf_op jit(solution)/shard_map/ppermute | solution.py:480
  14.4 0.0 collective-permute-start.3
  14.4 2.4 %shard_map.49 = (f32[3,336,128]{2,1,0:T(8,128)S(1)}, f32[3,336,128]{2,1,0:T(8,128)S(1)}, f32[3,336,128]{2,1,0:T(8,128)S(1)}, f32[3,336,128]{2,1,0:T(8,128)S(1)},...) custom-call(s32[4]{0:T(128)S(1)} %add_convert_fusion.edges, ...), custom_call_target="tpu_custom_call" | custom-call | flops 8388608 | bytes 4194304 | tf_op jit(solution)/shard_map/pallas_call | solution.py:484
  16.8 0.0 collective-permute-done.2.above
  16.8 2.9 %collective-permute-done.3.below = f32[4,3,16,128]{3,2,1,0:T(8,128)S(1)} collective-permute-done((f32[4,3,16,128]{3,2,1,0:T(8,128)S(1)}, f32[4,3,16,128]{3,2,1,0:T(8,128)S(1)}, u32[]{:S(2)}, u32[]{:S(2)}) %collective-permute-start.3) | collective-permute-done | bytes 98336 | tf_op jit(solution)/shard_map/ppermute | solution.py:480
  19.7 3.2 %shard_map.50 = (f32[3,336,128]{2,1,0:T(8,128)S(1)}, f32[3,336,128]{2,1,0:T(8,128)S(1)}, f32[3,336,128]{2,1,0:T(8,128)S(1)}, f32[3,336,128]{2,1,0:T(8,128)S(1)},...) custom-call(s32[4]{0:T(128)S(1)} %add_convert_fusion.edges, ...), custom_call_target="tpu_custom_call", output_to_operand_aliasing={{0}: (3, {}), {1}: (4, {}), {2}: (5, {}), {3}: (6, {}), {4}... | custom-call | flops 8388608 | bytes 4194304 | tf_op jit(solution)/shard_map/pallas_call | solution.py:484
  22.9 0.1 collective-permute-start.4
  23.0 5.1 %collective-permute-start.5 = (f32[64,128]{1,0:T(8,128)S(1)}, f32[64,128]{1,0:T(8,128)S(1)}, u32[]{:S(2)}, u32[]{:S(2)}) collective-permute-start(f32[64,128]{1,0:T(8,128)S(1)} %get-tuple-element.76), channel_id=1, source_target_pairs={{1,0},{2,1},{3,2},{4,3},{5,4},{6,5},{7,6},{8,7},{9,8},{10,9},{11,1... | collective-permute-start | bytes 98312 | tf_op jit(solution)/shard_map/ppermute | solution.py:480
  28.1 1.2 %collective-permute-done.4.left = f32[64,128]{1,0:T(8,128)S(1)} collective-permute-done((f32[64,128]{1,0:T(8,128)S(1)}, f32[64,128]{1,0:T(8,128)S(1)}, u32[]{:S(2)}, u32[]{:S(2)}) %collective-permute-start.4) | collective-permute-done | bytes 32800 | tf_op jit(solution)/shard_map/ppermute | solution.py:480
  29.3 0.0 collective-permute-done.5.right
  29.3 0.6 %shard_map.51 = (f32[3,64,128]{2,1,0:T(8,128)S(1)}, f32[3,24,128]{2,1,0:T(8,128)S(1)}, f32[3,24,128]{2,1,0:T(8,128)S(1)}) custom-call(s32[4]{0:T(128)S(1)} %add_convert_fusion.edges, f32[3,64,128]{2,1,0:T(8,128)S(1)} %get-tuple-element.74.own2, f32[64,128]{1,0:T(8,128)S(1)} %collective-permute-done.4.left, f32[64,128]{1,0:T(8,128)S(1)} %collective-permute-done.5.right), custom_call_target="tpu_custom_call" | custom-call | flops 8388608 | bytes 4194304 | tf_op jit(solution)/shard_map/pallas_call | solution.py:484
  30.0 1.0 %collective-permute-start.6 = (f32[3,24,128]{2,1,0:T(8,128)S(1)}, f32[3,24,128]{2,1,0:T(8,128)S(1)}, u32[]{:S(2)}, u32[]{:S(2)}) collective-permute-start(f32[3,24,128]{2,1,0:T(8,128)S(1)} %get-tuple-element.78), channel_id=1, source_target_pairs={{0,16},{16,32},{32,48},{48,64},{64,80},{80,96},{96,112},{112,128},... | collective-permute-start | bytes 110600 | tf_op jit(solution)/shard_map/ppermute | solution.py:480
  31.0 0.0 collective-permute-start.7
  31.0 1.1 %collective-permute-done.6.above = f32[3,24,128]{2,1,0:T(8,128)S(1)} collective-permute-done((f32[3,24,128]{2,1,0:T(8,128)S(1)}, f32[3,24,128]{2,1,0:T(8,128)S(1)}, u32[]{:S(2)}, u32[]{:S(2)}) %collective-permute-start.6) | collective-permute-done | bytes 36896 | tf_op jit(solution)/shard_map/ppermute | solution.py:480
  32.1 3.5 %collective-permute-done.7.below = f32[3,24,128]{2,1,0:T(8,128)S(1)} collective-permute-done((f32[3,24,128]{2,1,0:T(8,128)S(1)}, f32[3,24,128]{2,1,0:T(8,128)S(1)}, u32[]{:S(2)}, u32[]{:S(2)}) %collective-permute-start.7) | collective-permute-done | bytes 36896 | tf_op jit(solution)/shard_map/ppermute | solution.py:480
  35.6 1.3 %shard_map.52 = (f32[1,128,128]{2,1,0:T(8,128)S(1)}, f32[1,128,128]{2,1,0:T(8,128)S(1)}, f32[1,128,128]{2,1,0:T(8,128)S(1)}, f32[1,128,128]{2,1,0:T(8,128)S(1)},...) custom-call(s32[4]{0:T(128)S(1)} %add_convert_fusion.edges, ...), custom_call_target="tpu_custom_call" | custom-call | flops 8388608 | bytes 4194304 | tf_op jit(solution)/shard_map/pallas_call | solution.py:484
  36.9 5.2 %collective-permute-start.9 = (f32[3,32,128]{2,1,0:T(8,128)S(1)}, f32[3,32,128]{2,1,0:T(8,128)S(1)}, u32[]{:S(2)}, u32[]{:S(2)}) collective-permute-start(f32[3,32,128]{2,1,0:T(8,128)S(1)} %get-tuple-element.80.message), channel_id=1, source_target_pairs={{1,0},{2,1},{3,2},{4,3},{5,4},{6,5},{7,6},{8,7},{9,8},{10,9},{11,1... | collective-permute-start | bytes 147464 | tf_op jit(solution)/shard_map/ppermute | solution.py:480
  42.1 1.2 %collective-permute-done.9.right = f32[3,32,128]{2,1,0:T(8,128)S(1)} collective-permute-done((f32[3,32,128]{2,1,0:T(8,128)S(1)}, f32[3,32,128]{2,1,0:T(8,128)S(1)}, u32[]{:S(2)}, u32[]{:S(2)}) %collective-permute-start.9) | collective-permute-done | bytes 49184 | tf_op jit(solution)/shard_map/ppermute | solution.py:480
  43.3 5.1 %collective-permute-done.8.left = f32[3,32,128]{2,1,0:T(8,128)S(1)} collective-permute-done((f32[3,32,128]{2,1,0:T(8,128)S(1)}, f32[3,32,128]{2,1,0:T(8,128)S(1)}, u32[]{:S(2)}, u32[]{:S(2)}) %collective-permute-start.8) | collective-permute-done | bytes 49184 | tf_op jit(solution)/shard_map/ppermute | solution.py:480
  48.4 0.6 %shard_map.53.wide = f32[3,32,128]{2,1,0:T(8,128)S(1)} custom-call(s32[4]{0:T(128)S(1)} %add_convert_fusion.edges, f32[3,32,128]{2,1,0:T(8,128)S(1)} %get-tuple-element.80.message, f32[3,32,128]{2,1,0:T(8,128)S(1)} %collective-permute-done.8.left, f32[3,32,128]{2,1,0:T(8,128)S(1)} %collective-permute-done.9.right), custom_call_target="tpu_custom_call" | custom-call | flops 8388608 | bytes 4194304 | tf_op jit(solution)/shard_map/pallas_call | solution.py:484
  49.0 0.0 collective-permute-start.11
  49.0 2.9 %collective-permute-start.10 = (f32[3,32,128]{2,1,0:T(8,128)S(1)}, f32[3,32,128]{2,1,0:T(8,128)S(1)}, u32[]{:S(2)}, u32[]{:S(2)}) collective-permute-start(f32[3,32,128]{2,1,0:T(8,128)S(1)} %shard_map.53.wide), channel_id=1, source_target_pairs={{0,16},{16,32},{32,48},{48,64},{64,80},{80,96},{96,112},{112,128},... | collective-permute-start | bytes 147464 | tf_op jit(solution)/shard_map/ppermute | solution.py:480
  52.0 1.8 %collective-permute-done.11.lower = f32[3,32,128]{2,1,0:T(8,128)S(1)} collective-permute-done((f32[3,32,128]{2,1,0:T(8,128)S(1)}, f32[3,32,128]{2,1,0:T(8,128)S(1)}, u32[]{:S(2)}, u32[]{:S(2)}) %collective-permute-start.11) | collective-permute-done | bytes 49184 | tf_op jit(solution)/shard_map/ppermute | solution.py:480
  53.8 4.4 %shard_map.54 = f32[256,256]{1,0:T(8,128)} custom-call(s32[4]{0:T(128)S(1)} %add_convert_fusion.edges, f32[3,32,128]{2,1,0:T(8,128)S(1)} %shard_map.53.wide, f32[3,32,128]{2,1,0:T(8,128)S(1)} %collective-permute-done.10.upper, f32[3,32,128]{2,1,0:T(8,128)S(1)} %collective-permute-done.11.lower, f32[3,336,128]{2,1,0:T(8,128)S(1)} %get-tuple-element.81.refs_0_, ...), custom_call_target="tpu_custom_call" | custom-call | flops 41943040 | bytes 12582912 | tf_op jit(solution)/shard_map/pallas_call | solution.py:539
  (2 shorter events, 0.0 us)
Async XLA Ops:
  2.7 6.8 %collective-permute-start = (f32[128,128]{1,0:T(8,128)S(1)}, f32[128,128]{1,0:T(8,128)S(1)}, u32[]{:S(2)}, u32[]{:S(2)}) collective-permute-start(f32[128,128]{1,0:T(8,128)S(1)} %get-tuple-element.56), channel_id=1, source_target_pairs={{0,1},{1,2},{2,3},{3,4},{4,5},{5,6},{6,7},{7,8},{8,9},{9,10},{10,1... | collective-permute-start | bytes 196616 | tf_op jit(solution)/shard_map/ppermute | solution.py:480
  4.1 5.4 %collective-permute-start.1 = (f32[128,128]{1,0:T(8,128)S(1)}, f32[128,128]{1,0:T(8,128)S(1)}, u32[]{:S(2)}, u32[]{:S(2)}) collective-permute-start(f32[128,128]{1,0:T(8,128)S(1)} %get-tuple-element.57), channel_id=1, source_target_pairs={{1,0},{2,1},{3,2},{4,3},{5,4},{6,5},{7,6},{8,7},{9,8},{10,9},{11,1... | collective-permute-start | bytes 196616 | tf_op jit(solution)/shard_map/ppermute | solution.py:480
  10.1 6.7 %collective-permute-start.2 = (f32[4,3,16,128]{3,2,1,0:T(8,128)S(1)}, f32[4,3,16,128]{3,2,1,0:T(8,128)S(1)}, u32[]{:S(2)}, u32[]{:S(2)}) collective-permute-start(f32[4,3,16,128]{3,2,1,0:T(8,128)S(1)} %get-tuple-element.59), channel_id=1, source_target_pairs={{0,16},{16,32},{32,48},{48,64},{64,80},{80,96},{96,112},{112,128},... | collective-permute-start | bytes 294920 | tf_op jit(solution)/shard_map/ppermute | solution.py:480
  14.4 5.3 %collective-permute-start.3 = (f32[4,3,16,128]{3,2,1,0:T(8,128)S(1)}, f32[4,3,16,128]{3,2,1,0:T(8,128)S(1)}, u32[]{:S(2)}, u32[]{:S(2)}) collective-permute-start(f32[4,3,16,128]{3,2,1,0:T(8,128)S(1)} %get-tuple-element.60), channel_id=1, source_target_pairs={{16,0},{32,16},{48,32},{64,48},{80,64},{96,80},{112,96},{128,112},... | collective-permute-start | bytes 294920 | tf_op jit(solution)/shard_map/ppermute | solution.py:480
  22.9 6.4 %collective-permute-start.4 = (f32[64,128]{1,0:T(8,128)S(1)}, f32[64,128]{1,0:T(8,128)S(1)}, u32[]{:S(2)}, u32[]{:S(2)}) collective-permute-start(f32[64,128]{1,0:T(8,128)S(1)} %get-tuple-element.75), channel_id=1, source_target_pairs={{0,1},{1,2},{2,3},{3,4},{4,5},{5,6},{6,7},{7,8},{8,9},{9,10},{10,1... | collective-permute-start | bytes 98312 | tf_op jit(solution)/shard_map/ppermute | solution.py:480
  23.0 6.4 %collective-permute-start.5 = (f32[64,128]{1,0:T(8,128)S(1)}, f32[64,128]{1,0:T(8,128)S(1)}, u32[]{:S(2)}, u32[]{:S(2)}) collective-permute-start(f32[64,128]{1,0:T(8,128)S(1)} %get-tuple-element.76), channel_id=1, source_target_pairs={{1,0},{2,1},{3,2},{4,3},{5,4},{6,5},{7,6},{8,7},{9,8},{10,9},{11,1... | collective-permute-start | bytes 98312 | tf_op jit(solution)/shard_map/ppermute | solution.py:480
  30.0 2.1 %collective-permute-start.6 = (f32[3,24,128]{2,1,0:T(8,128)S(1)}, f32[3,24,128]{2,1,0:T(8,128)S(1)}, u32[]{:S(2)}, u32[]{:S(2)}) collective-permute-start(f32[3,24,128]{2,1,0:T(8,128)S(1)} %get-tuple-element.78), channel_id=1, source_target_pairs={{0,16},{16,32},{32,48},{48,64},{64,80},{80,96},{96,112},{112,128},... | collective-permute-start | bytes 110600 | tf_op jit(solution)/shard_map/ppermute | solution.py:480
  31.0 4.6 %collective-permute-start.7 = (f32[3,24,128]{2,1,0:T(8,128)S(1)}, f32[3,24,128]{2,1,0:T(8,128)S(1)}, u32[]{:S(2)}, u32[]{:S(2)}) collective-permute-start(f32[3,24,128]{2,1,0:T(8,128)S(1)} %get-tuple-element.79), channel_id=1, source_target_pairs={{16,0},{32,16},{48,32},{64,48},{80,64},{96,80},{112,96},{128,112},... | collective-permute-start | bytes 110600 | tf_op jit(solution)/shard_map/ppermute | solution.py:480
  36.9 6.4 %collective-permute-start.9 = (f32[3,32,128]{2,1,0:T(8,128)S(1)}, f32[3,32,128]{2,1,0:T(8,128)S(1)}, u32[]{:S(2)}, u32[]{:S(2)}) collective-permute-start(f32[3,32,128]{2,1,0:T(8,128)S(1)} %get-tuple-element.80.message), channel_id=1, source_target_pairs={{1,0},{2,1},{3,2},{4,3},{5,4},{6,5},{7,6},{8,7},{9,8},{10,9},{11,1... | collective-permute-start | bytes 147464 | tf_op jit(solution)/shard_map/ppermute | solution.py:480
  42.1 6.3 %collective-permute-start.8 = (f32[3,32,128]{2,1,0:T(8,128)S(1)}, f32[3,32,128]{2,1,0:T(8,128)S(1)}, u32[]{:S(2)}, u32[]{:S(2)}) collective-permute-start(f32[3,32,128]{2,1,0:T(8,128)S(1)} %get-tuple-element.80.message), channel_id=1, source_target_pairs={{0,1},{1,2},{2,3},{3,4},{4,5},{5,6},{6,7},{7,8},{8,9},{9,10},{10,1... | collective-permute-start | bytes 147464 | tf_op jit(solution)/shard_map/ppermute | solution.py:480
  49.0 4.7 %collective-permute-start.11 = (f32[3,32,128]{2,1,0:T(8,128)S(1)}, f32[3,32,128]{2,1,0:T(8,128)S(1)}, u32[]{:S(2)}, u32[]{:S(2)}) collective-permute-start(f32[3,32,128]{2,1,0:T(8,128)S(1)} %shard_map.53.wide), channel_id=1, source_target_pairs={{16,0},{32,16},{48,32},{64,48},{80,64},{96,80},{112,96},{128,112},... | collective-permute-start | bytes 147464 | tf_op jit(solution)/shard_map/ppermute | solution.py:480
  49.0 4.7 %collective-permute-start.10 = (f32[3,32,128]{2,1,0:T(8,128)S(1)}, f32[3,32,128]{2,1,0:T(8,128)S(1)}, u32[]{:S(2)}, u32[]{:S(2)}) collective-permute-start(f32[3,32,128]{2,1,0:T(8,128)S(1)} %shard_map.53.wide), channel_id=1, source_target_pairs={{0,16},{16,32},{32,48},{48,64},{64,80},{80,96},{96,112},{112,128},... | collective-permute-start | bytes 147464 | tf_op jit(solution)/shard_map/ppermute | solution.py:480
